TPU v7x, 32 devices: a whole 2x2x4 slice. The times are simulated.
32 devices in a mesh: fsdp: 2 (over y), ctx: 4 (over z), tp: 4 (over x, core).
Axes of the slice: x: 2, y: 2, z: 4, core: 2. Of those that a mesh axis runs over, the one named last changes fastest.
Arguments:
- tokens: bfloat16 [4096, 2048], P(('fsdp', 'ctx')), may hold values from -6 to 6
- token_segment: int32 [4096], P('fsdp'), may hold values from 0 to 12, as said below
- segment_parent: int32 [2, 13], P('fsdp'), may hold values from 0 to 4, as said below
- ln1_gain: bfloat16 [2048], replicated, may hold values from 0.5 to 1.5
- ln1_bias: bfloat16 [2048], replicated, may hold values from -1.1953125 to 1.1953125
- q_weight: bfloat16 [2048, 2048], P(('fsdp', 'ctx'), 'tp'), may hold values from -0.125 to 0.125
- q_bias: bfloat16 [2048], P('tp'), may hold values from -1.1953125 to 1.1953125
- kv_weight: bfloat16 [2048, 256], P(('fsdp', 'ctx')), may hold values from -0.125 to 0.125
- value_bias: bfloat16 [128], replicated, may hold values from -1.1953125 to 1.1953125
- o_weight: bfloat16 [2048, 2048], P('tp', ('fsdp', 'ctx')), may hold values from -1.5 to 1.5
- o_bias: bfloat16 [2048], replicated, may hold values from -1.1953125 to 1.1953125
- ln2_gain: bfloat16 [2048], replicated, may hold values from 0.5 to 1.5
- ln2_bias: bfloat16 [2048], replicated, may hold values from -1.1953125 to 1.1953125
- up_weight: bfloat16 [2048, 8192], P(('fsdp', 'ctx'), 'tp'), may hold values from -0.125 to 0.125
- up_bias: bfloat16 [8192], P('tp'), may hold values from -1.1953125 to 1.1953125
- down_weight: bfloat16 [8192, 2048], P('tp', ('fsdp', 'ctx')), may hold values from -0.0625 to 0.0625
- down_bias: bfloat16 [2048], replicated, may hold values from -1.1953125 to 1.1953125
- out_grad: bfloat16 [4096, 2048], P(('fsdp', 'ctx')), may hold values from -6 to 6
Outputs:
- layer_out: bfloat16 [4096, 2048], P(('fsdp', 'ctx', 'tp'))
- input_grad: bfloat16 [4096, 2048], P(('fsdp', 'ctx', 'tp'))
- ln1_gain_grad: float32 [2048], replicated
- ln1_bias_grad: float32 [2048], replicated
- q_weight_grad: float32 [2048, 2048], P(('fsdp', 'ctx'), 'tp')
- q_bias_grad: float32 [2048], P('tp')
- kv_weight_grad: float32 [2048, 256], P(('fsdp', 'ctx', 'tp'))
- value_bias_grad: float32 [128], replicated
- o_weight_grad: float32 [2048, 2048], P('tp', ('fsdp', 'ctx'))
- o_bias_grad: float32 [2048], replicated
- ln2_gain_grad: float32 [2048], replicated
- ln2_bias_grad: float32 [2048], replicated
- up_weight_grad: float32 [2048, 8192], P(('fsdp', 'ctx'), 'tp')
- up_bias_grad: float32 [8192], P('tp')
- down_weight_grad: float32 [8192, 2048], P('tp', ('fsdp', 'ctx'))
- down_bias_grad: float32 [2048], replicated
Inputs may be any that keep to these rules, and one draw needn't show every extreme that they name: `segment_parent`: row t gives the parent of each of the 13 segments of tree t: segment 0 is the trunk and its own parent, segments 1 to 4 are branches with parent 0, every later segment is a leaf whose parent is a branch, and each branch has 2 leaves. `token_segment`: within each tree the segment ids never fall, the first 768 tokens are segment 0, and every segment has at least one token.
All inputs are finite; a program needn't handle non-finite values.
Results may differ from a plain program's by a relative error of at most 0.02.
Values may be sent and summed in bfloat16 or wider, within the bound.
No kernel may reach another device: no remote copies, remote signals or barrier semaphores. Data moves between devices by JAX's collectives and lax.ppermute only.
A program may use at most 192 MiB of HBM per device.

v0:
```python
import math

import jax
import jax.numpy as jnp
from jax import lax
from jax.sharding import PartitionSpec as P

eps = 1e-05
masked_score = -1000000000.0


def layer_norm(values, gain, shift):
    center = jnp.mean(values, axis=-1, keepdims=True)
    centred = values - center
    spread = jnp.mean(centred * centred, axis=-1, keepdims=True)
    return centred * lax.rsqrt(spread + eps) * gain + shift


def gelu_tanh(values):
    return jax.nn.gelu(values, approximate=True)


def parent_lookup(seg_ids, parents):
    labels = jnp.arange(parents.shape[0], dtype=jnp.int32)
    picked = jnp.where(seg_ids[:, None] == labels[None, :], parents[None, :], 0)
    return jnp.sum(picked, axis=1)


def scores_of(query_block, keys_all, key_segments, key_places, info_block, score_scale):
    own_seg, seg_one, seg_two, query_place = info_block
    raw_scores = (
        jnp.einsum("qhd,kd->hqk", query_block, keys_all, preferred_element_type=jnp.float32)
        * score_scale
    )
    same_path = (
        (key_segments[None, :] == own_seg[:, None])
        | (key_segments[None, :] == seg_one[:, None])
        | (key_segments[None, :] == seg_two[:, None])
    )
    allowed = same_path & (key_places[None, :] <= query_place[:, None])
    return jnp.where(allowed[None, :, :], raw_scores, masked_score)


def body(
    tokens,
    token_segment,
    segment_parent,
    ln1_gain,
    ln1_bias,
    q_weight,
    q_bias,
    kv_weight,
    value_bias,
    o_weight,
    o_bias,
    ln2_gain,
    ln2_bias,
    up_weight,
    up_bias,
    down_weight,
    down_bias,
    out_grad,
):
    row_count = tokens.shape[0]
    head_size = value_bias.shape[0]
    local_width = q_weight.shape[1]
    local_units = up_weight.shape[1]
    local_heads = local_width // head_size
    tree_length = token_segment.shape[0]
    block_rows = min(256, row_count)
    block_count = row_count // block_rows
    score_scale = 1.0 / math.sqrt(head_size)
    first_row = lax.axis_index("ctx") * row_count
    tp_count = lax.axis_size("tp")
    tp_index = lax.axis_index("tp")
    share_rows = row_count // tp_count
    share_start = tp_index * share_rows
    full_query_w, full_out_w, full_up_w, full_down_w, full_kv_w = (
        lax.all_gather(q_weight, ("fsdp", "ctx"), axis=0, tiled=True),
        lax.all_gather(o_weight, ("fsdp", "ctx"), axis=1, tiled=True),
        lax.all_gather(up_weight, ("fsdp", "ctx"), axis=0, tiled=True),
        lax.all_gather(down_weight, ("fsdp", "ctx"), axis=1, tiled=True),
        lax.all_gather(kv_weight, ("fsdp", "ctx"), axis=0, tiled=True),
    )
    parents = segment_parent[0]
    key_places = jnp.arange(tree_length, dtype=jnp.int32)
    own_seg = lax.dynamic_slice_in_dim(token_segment, first_row, row_count)
    one_up = parent_lookup(own_seg, parents)
    two_up = parent_lookup(one_up, parents)
    query_place = first_row + jnp.arange(row_count, dtype=jnp.int32)
    query_info = tuple(
        (
            column.reshape(block_count, block_rows)
            for column in (own_seg, one_up, two_up, query_place)
        )
    )
    gain_one = ln1_gain.astype(jnp.float32)
    shift_one = ln1_bias.astype(jnp.float32)
    gain_two = ln2_gain.astype(jnp.float32)
    shift_two = ln2_bias.astype(jnp.float32)
    o_shift = o_bias.astype(jnp.float32)
    x_float = tokens.astype(jnp.float32)
    x_share = lax.dynamic_slice_in_dim(x_float, share_start, share_rows)
    act_one = layer_norm(x_float, gain_one, shift_one).astype(jnp.bfloat16)
    queries = (
        jnp.dot(act_one, full_query_w, preferred_element_type=jnp.float32)
        + q_bias.astype(jnp.float32)
    ).astype(jnp.bfloat16)
    kv_shift = jnp.concatenate(
        [jnp.zeros((head_size,), jnp.float32), value_bias.astype(jnp.float32)]
    )
    kv_local = (jnp.dot(act_one, full_kv_w, preferred_element_type=jnp.float32) + kv_shift).astype(
        jnp.bfloat16
    )
    kv_rows = lax.all_gather(kv_local, "ctx", axis=0, tiled=True)
    query_blocks = queries.reshape(block_count, block_rows, local_heads, head_size)

    def attend(carry_in, inputs):
        query_block = inputs[0]
        info_block = inputs[1:]
        keys_all = kv_rows[:, :head_size]
        values_all = kv_rows[:, head_size:]
        scores = scores_of(
            query_block, keys_all, token_segment, key_places, info_block, score_scale
        )
        row_max = jnp.max(scores, axis=2, keepdims=True)
        exp_scores = jnp.exp(scores - row_max)
        row_total = jnp.sum(exp_scores, axis=2, keepdims=True)
        probs_low = (exp_scores / row_total).astype(jnp.bfloat16)
        mixed_rows = jnp.einsum(
            "hqk,kd->qhd", probs_low, values_all, preferred_element_type=jnp.float32
        )
        return (
            carry_in,
            (mixed_rows.reshape(block_rows, local_width), (row_max + jnp.log(row_total))[:, :, 0]),
        )

    _, (mixed_blocks, log_totals) = lax.scan(
        attend, jnp.zeros((), jnp.float32), (query_blocks,) + query_info
    )
    attended = mixed_blocks.reshape(row_count, local_width).astype(jnp.bfloat16)
    attn_part = jnp.dot(attended, full_out_w, preferred_element_type=jnp.float32)
    attn_total = lax.psum(attn_part.astype(jnp.bfloat16), "tp").astype(jnp.float32)
    residual = x_float + (attn_total + o_shift)
    normed_two, ln2_pull = jax.vjp(layer_norm, residual, gain_two, shift_two)
    act_two = normed_two.astype(jnp.bfloat16)
    residual_share = lax.dynamic_slice_in_dim(residual, share_start, share_rows)
    pre_act = jnp.dot(act_two, full_up_w, preferred_element_type=jnp.float32) + up_bias.astype(
        jnp.float32
    )
    gelu_out, gelu_pull = jax.vjp(gelu_tanh, pre_act)
    hidden = gelu_out.astype(jnp.bfloat16)
    ffn_part = jnp.dot(hidden, full_down_w, preferred_element_type=jnp.float32)
    ffn_share = lax.psum_scatter(
        ffn_part.astype(jnp.bfloat16), "tp", scatter_dimension=0, tiled=True
    ).astype(jnp.float32)
    layer_out = (residual_share + (ffn_share + down_bias.astype(jnp.float32))).astype(jnp.bfloat16)
    grad_out = out_grad.astype(jnp.float32)
    grad_out_share = lax.dynamic_slice_in_dim(grad_out, share_start, share_rows)
    down_bias_grad = jnp.sum(grad_out_share, axis=0)
    down_grad = jnp.dot(hidden.T, out_grad, preferred_element_type=jnp.float32)
    grad_hidden = jnp.dot(out_grad, full_down_w.T, preferred_element_type=jnp.float32)
    grad_pre = gelu_pull(grad_hidden)[0].astype(jnp.bfloat16)
    up_bias_grad = jnp.sum(grad_pre.astype(jnp.float32), axis=0)
    up_grad = jnp.dot(act_two.T, grad_pre, preferred_element_type=jnp.float32)
    grad_two_part = jnp.dot(grad_pre, full_up_w.T, preferred_element_type=jnp.float32)
    grad_two = lax.psum(grad_two_part.astype(jnp.bfloat16), "tp").astype(jnp.float32)
    grad_norm, gain_two_total, shift_two_total = ln2_pull(grad_two)
    ln2_gain_grad = gain_two_total / tp_count
    ln2_bias_grad = shift_two_total / tp_count
    grad_res = grad_out + grad_norm
    grad_attn = grad_res.astype(jnp.bfloat16)
    grad_res_share = lax.dynamic_slice_in_dim(grad_res, share_start, share_rows)
    grad_attn_share = lax.dynamic_slice_in_dim(grad_attn, share_start, share_rows)
    o_bias_grad = jnp.sum(grad_attn_share.astype(jnp.float32), axis=0)
    out_w_grad = jnp.dot(attended.T, grad_attn, preferred_element_type=jnp.float32)
    grad_attended = jnp.dot(grad_attn, full_out_w.T, preferred_element_type=jnp.float32).astype(
        jnp.bfloat16
    )
    grad_blocks = grad_attended.reshape(block_count, block_rows, local_heads, head_size)

    def attend_back(carry_in, inputs):
        key_grad, value_grad = carry_in
        query_block, grad_block, log_block = (inputs[0], inputs[1], inputs[2])
        info_block = inputs[3:]
        keys_all = kv_rows[:, :head_size]
        values_all = kv_rows[:, head_size:]
        scores = scores_of(
            query_block, keys_all, token_segment, key_places, info_block, score_scale
        )
        attn_probs = jnp.exp(scores - log_block[:, :, None])
        probs_low = attn_probs.astype(jnp.bfloat16)
        grad_probs = jnp.einsum(
            "qhd,kd->hqk", grad_block, values_all, preferred_element_type=jnp.float32
        )
        row_delta = jnp.sum(attn_probs * grad_probs, axis=2, keepdims=True)
        grad_scores = (attn_probs * (grad_probs - row_delta)).astype(jnp.bfloat16)
        grad_query = (
            jnp.einsum("hqk,kd->qhd", grad_scores, keys_all, preferred_element_type=jnp.float32)
            * score_scale
        )
        key_grad = (
            key_grad
            + jnp.einsum(
                "hqk,qhd->kd", grad_scores, query_block, preferred_element_type=jnp.float32
            )
            * score_scale
        )
        value_grad = value_grad + jnp.einsum(
            "hqk,qhd->kd", probs_low, grad_block, preferred_element_type=jnp.float32
        )
        return ((key_grad, value_grad), grad_query.reshape(block_rows, local_width))

    zero_rows = jnp.zeros((tree_length, head_size), jnp.float32)
    (key_grad, value_grad), grad_query_blocks = lax.scan(
        attend_back, (zero_rows, zero_rows), (query_blocks, grad_blocks, log_totals) + query_info
    )
    grad_query = grad_query_blocks.reshape(row_count, local_width).astype(jnp.bfloat16)
    q_bias_grad = jnp.sum(grad_query.astype(jnp.float32), axis=0)
    query_w_grad = jnp.dot(act_one.T, grad_query, preferred_element_type=jnp.float32)
    kv_grad_part = lax.psum_scatter(
        jnp.concatenate([key_grad, value_grad], axis=1).astype(jnp.bfloat16),
        "ctx",
        scatter_dimension=0,
        tiled=True,
    )
    grad_act_part = jnp.dot(grad_query, full_query_w.T, preferred_element_type=jnp.float32)
    grad_act_share, kv_grad_share = (
        lax.psum_scatter(
            grad_act_part.astype(jnp.bfloat16), "tp", scatter_dimension=0, tiled=True
        ).astype(jnp.float32),
        lax.psum_scatter(kv_grad_part, "tp", scatter_dimension=0, tiled=True).astype(jnp.float32),
    )
    kv_low_share = kv_grad_share.astype(jnp.bfloat16)
    value_bias_grad = jnp.sum(kv_low_share[:, head_size:].astype(jnp.float32), axis=0)
    act_share = lax.dynamic_slice_in_dim(act_one, share_start, share_rows)
    kv_w_grad = jnp.dot(act_share.T, kv_low_share, preferred_element_type=jnp.float32)
    kv_w_shard = lax.psum_scatter(kv_w_grad, ("fsdp", "ctx", "tp"), scatter_dimension=0, tiled=True)
    grad_act_one = grad_act_share + jnp.dot(
        kv_low_share, full_kv_w.T, preferred_element_type=jnp.float32
    )
    _, ln1_pull = jax.vjp(layer_norm, x_share, gain_one, shift_one)
    grad_x_norm, ln1_gain_grad, ln1_bias_grad = ln1_pull(grad_act_one)
    input_grad = (grad_res_share + grad_x_norm).astype(jnp.bfloat16)
    query_shard, out_shard, up_shard, down_shard = (
        lax.psum_scatter(
            query_w_grad.astype(jnp.bfloat16), ("fsdp", "ctx"), scatter_dimension=0, tiled=True
        ).astype(jnp.float32),
        lax.psum_scatter(
            out_w_grad.astype(jnp.bfloat16), ("fsdp", "ctx"), scatter_dimension=1, tiled=True
        ).astype(jnp.float32),
        lax.psum_scatter(
            up_grad.astype(jnp.bfloat16), ("fsdp", "ctx"), scatter_dimension=0, tiled=True
        ).astype(jnp.float32),
        lax.psum_scatter(
            down_grad.astype(jnp.bfloat16), ("fsdp", "ctx"), scatter_dimension=1, tiled=True
        ).astype(jnp.float32),
    )
    q_bias_slots = lax.dynamic_update_slice_in_dim(
        jnp.zeros((local_width * tp_count,), jnp.float32), q_bias_grad, tp_index * local_width, 0
    )
    up_bias_slots = lax.dynamic_update_slice_in_dim(
        jnp.zeros((local_units * tp_count,), jnp.float32), up_bias_grad, tp_index * local_units, 0
    )
    small_sums = lax.psum(
        (
            ln1_gain_grad,
            ln1_bias_grad,
            q_bias_slots,
            value_bias_grad,
            o_bias_grad,
            ln2_gain_grad,
            ln2_bias_grad,
            up_bias_slots,
            down_bias_grad,
        ),
        ("fsdp", "ctx", "tp"),
    )
    q_bias_out = lax.dynamic_slice_in_dim(small_sums[2], tp_index * local_width, local_width)
    up_bias_out = lax.dynamic_slice_in_dim(small_sums[7], tp_index * local_units, local_units)
    return (
        layer_out,
        input_grad,
        small_sums[0],
        small_sums[1],
        query_shard,
        q_bias_out,
        kv_w_shard,
        small_sums[3],
        out_shard,
        small_sums[4],
        small_sums[5],
        small_sums[6],
        up_shard,
        up_bias_out,
        down_shard,
        small_sums[8],
    )


def solution(mesh):
    in_specs = (
        P(("fsdp", "ctx"), None),
        P("fsdp"),
        P("fsdp", None),
        P(),
        P(),
        P(("fsdp", "ctx"), "tp"),
        P("tp"),
        P(("fsdp", "ctx"), None),
        P(),
        P("tp", ("fsdp", "ctx")),
        P(),
        P(),
        P(),
        P(("fsdp", "ctx"), "tp"),
        P("tp"),
        P("tp", ("fsdp", "ctx")),
        P(),
        P(("fsdp", "ctx"), None),
    )
    out_specs = (
        P(("fsdp", "ctx", "tp"), None),
        P(("fsdp", "ctx", "tp"), None),
        P(),
        P(),
        P(("fsdp", "ctx"), "tp"),
        P("tp"),
        P(("fsdp", "ctx", "tp"), None),
        P(),
        P("tp", ("fsdp", "ctx")),
        P(),
        P(),
        P(),
        P(("fsdp", "ctx"), "tp"),
        P("tp"),
        P("tp", ("fsdp", "ctx")),
        P(),
    )
    return jax.shard_map(body, mesh=mesh, in_specs=in_specs, out_specs=out_specs, check_vma=False)
```

profile of v0, /device:TPU:0, one launch (start us, length us, event | category | flops | bytes accessed | tf_op | source)
XLA Modules:
  0.0 1463.9 jit_solution(8876229310707440190)
XLA Ops:
  17.2 35.8 %all-gather.9.cloned.1.call-done = bf16[2048,256]{1,0:T(8,128)(2,1)} async-done(((bf16[256,256]{1,0:T(8,128)(2,1)}), bf16[2048,256]{1,0:T(8,128)(2,1)}) %all-gather.9.cloned.1.call-update) | async-done | bytes 1048592 | tf_op jit(solution)/shard_map/all_gather | solution.py:83
  57.3 46.0 %all-gather.7.cloned.1.call-done = bf16[2048,512]{1,0:T(8,128)(2,1)} async-done(((bf16[256,512]{1,0:T(8,128)(2,1)}), bf16[2048,512]{1,0:T(8,128)(2,1)}) %all-gather.7.cloned.1.call-update) | async-done | bytes 2097168 | tf_op jit(solution)/shard_map/all_gather | solution.py:79
  107.0 24.9 %all-gather.11.cloned.1.call-done = bf16[2048,256]{1,0:T(8,128)(2,1)} async-done(((bf16[512,256]{1,0:T(8,128)(2,1)}), bf16[2048,256]{1,0:T(8,128)(2,1)}) %all-gather.11.cloned.1.call-update) | async-done | bytes 1048592 | tf_op jit(solution)/shard_map/all_gather | solution.py:115
  132.7 23.2 %while.28 = (s32[]{:T(128)}, bf16[2,256,512]{2,1,0:T(8,128)(2,1)}, f32[2,4,256]{2,1,0:T(4,128)S(1)}, s32[2048]{0:T(1024)S(1)}, s32[2,256]{1,0:T(2,128)S(1)}, /*i...) while((s32[]{:T(128)}, bf16[2,256,512]{2,1,0:T(8,128)(2,1)}, ...), condition=%wide.region_7.8_spmd.clone, body=%wide.region_4.7_spmd.clone.sunk | while | flops 1102576640 | bytes 36229284 | solution.py:138
  156.0 28.4 %all-gather.13.cloned.1.call-done = bf16[512,2048]{1,0:T(8,128)(2,1)} async-done(((bf16[512,256]{1,0:T(8,128)(2,1)}), bf16[512,2048]{1,0:T(8,128)(2,1)}) %all-gather.13.cloned.1.call-update) | async-done | bytes 2097168 | tf_op jit(solution)/shard_map/all_gather | solution.py:80
  190.5 48.0 %all-reduce.6.cloned.1.call-done = bf16[512,2048]{1,0:T(8,128)(2,1)} async-done(((bf16[512,2048]{1,0:T(8,128)(2,1)}), bf16[512,2048]{1,0:T(8,128)(2,1)}) %all-reduce.6.cloned.1.call-update) | async-done | bytes 2097168 | tf_op jit(solution)/shard_map/psum | solution.py:143
  243.4 122.4 %all-gather.15.cloned.1.call-done = bf16[2048,2048]{1,0:T(8,128)(2,1)} async-done(((bf16[256,2048]{1,0:T(8,128)(2,1)}), bf16[2048,2048]{1,0:T(8,128)(2,1)}) %all-gather.15.cloned.1.call-update) | async-done | bytes 8388624 | tf_op jit(solution)/shard_map/all_gather | solution.py:81
  365.7 11.2 fusion.68
  376.9 114.6 %all-gather.17.cloned.1.call-done = bf16[2048,2048]{1,0:T(8,128)(2,1)} async-done(((bf16[2048,256]{1,0:T(8,128)(2,1)}), bf16[2048,2048]{1,0:T(8,128)(2,1)}) %all-gather.17.cloned.1.call-update) | async-done | bytes 8388624 | tf_op jit(solution)/shard_map/all_gather | solution.py:82
  491.5 11.9 convert_reduce_fusion.1
  504.7 5.7 convolution_convert_fusion.5
  510.5 49.6 %all-reduce.8.cloned.1.call-done = bf16[512,2048]{1,0:T(8,128)(2,1)} async-done(((bf16[512,2048]{1,0:T(8,128)(2,1)}), bf16[512,2048]{1,0:T(8,128)(2,1)}) %all-reduce.8.cloned.1.call-update) | async-done | bytes 2097168 | tf_op jit(solution)/shard_map/psum | solution.py:167
  574.8 39.8 %while.29 = (s32[]{:T(128)}, f32[2048,128]{1,0:T(8,128)S(1)}, f32[2048,128]{1,0:T(8,128)}, bf16[2,256,512]{2,1,0:T(8,128)(2,1)}, s32[2048]{0:T(1024)S(1)}, /*ind...) while((s32[]{:T(128)}, f32[2048,128]{1,0:T(8,128)S(1)}, ...), condition=%wide.region_17.18_spmd.clone, body=%wide.region_15.17_spmd.clone.sunk | while | flops 2721053696 | bytes 82100464 | solution.py:215
  617.1 27.3 %reduce-scatter.14.cloned.1.call-done = bf16[512,256]{1,0:T(8,128)(2,1)} async-done(((bf16[2048,256]{1,0:T(8,128)(2,1)}), bf16[512,256]{1,0:T(8,128)(2,1)}) %reduce-scatter.14.cloned.1.call-update) | async-done | bytes 262160 | tf_op jit(solution)/shard_map/reduce_scatter | solution.py:221
  649.1 11.2 convolution_convert_fusion.6
  682.1 17.4 %reduce-scatter.12.cloned.1.call-done = bf16[128,2048]{1,0:T(8,128)(2,1)} async-done(((bf16[512,2048]{1,0:T(8,128)(2,1)}), bf16[128,2048]{1,0:T(8,128)(2,1)}) %reduce-scatter.12.cloned.1.call-update) | async-done | bytes 524304 | tf_op jit(solution)/shard_map/reduce_scatter | solution.py:229
  702.9 10.8 convolution_convert_fusion
  714.5 10.9 convolution_convert_fusion.1
  736.5 69.6 %reduce-scatter.22.cloned.1.call-done = bf16[512,256]{1,0:T(8,128)(2,1)} async-done(((bf16[512,2048]{1,0:T(8,128)(2,1)}), bf16[512,256]{1,0:T(8,128)(2,1)}) %reduce-scatter.22.cloned.1.call-update) | async-done | bytes 262160 | tf_op jit(solution)/shard_map/reduce_scatter | solution.py:249
  807.9 68.4 %reduce-scatter.18.cloned.1.call-done = bf16[256,512]{1,0:T(8,128)(2,1)} async-done(((bf16[2048,512]{1,0:T(8,128)(2,1)}), bf16[256,512]{1,0:T(8,128)(2,1)}) %reduce-scatter.18.cloned.1.call-update) | async-done | bytes 262160 | tf_op jit(solution)/shard_map/reduce_scatter | solution.py:246
  882.0 126.0 %all-reduce.10.cloned.1.call-done = (f32[2048]{0:T(1024)}, f32[2048]{0:T(1024)}, f32[2048]{0:T(1024)}, f32[128]{0:T(128)}, f32[2048]{0:T(1024)}, /*index=5*/f32[...) async-done(((f32[2048]{0:T(1024)}, f32[2048]{0:T(1024)}, f32[2048]{0:T(1024)}, f32[128]{0:T(128)}, f32[2048]{0:T(1024)}, /*index=5*/f32[2048]{0:T(1024)}, ...) | async-done | bytes 90640 | tf_op jit(solution)/shard_map/psum | solution.py:265
  1010.7 151.7 %reduce-scatter.26.cloned.1.call-done = bf16[2048,256]{1,0:T(8,128)(2,1)} async-done(((bf16[2048,2048]{1,0:T(8,128)(2,1)}), bf16[2048,256]{1,0:T(8,128)(2,1)}) %reduce-scatter.26.cloned.1.call-update) | async-done | bytes 1048592 | tf_op jit(solution)/shard_map/reduce_scatter | solution.py:255
  1165.1 148.8 %reduce-scatter.24.cloned.1.call-done = bf16[256,2048]{1,0:T(8,128)(2,1)} async-done(((bf16[2048,2048]{1,0:T(8,128)(2,1)}), bf16[256,2048]{1,0:T(8,128)(2,1)}) %reduce-scatter.24.cloned.1.call-update) | async-done | bytes 1048592 | tf_op jit(solution)/shard_map/reduce_scatter | solution.py:252
  1316.6 135.9 %reduce-scatter.20.cloned.1.call-done = f32[64,256]{1,0:T(8,128)} async-done(((f32[2048,256]{1,0:T(8,128)}), f32[64,256]{1,0:T(8,128)}) %reduce-scatter.20.cloned.1.call-update) | async-done | bytes 65552 | tf_op jit(solution)/shard_map/reduce_scatter | solution.py:238
  (273 shorter events, 163.4 us)
Async XLA Ops:
  7.2 45.9 %all-gather.9.cloned.1.call-start = ((), (), s32[]{:S(2)}) async-start(), calls=%async_computation.10 | async-start | bytes 1179648 | tf_op jit(solution)/shard_map/all_gather | solution.py:83
  7.9 95.4 %all-gather.7.cloned.1.call-start = ((), (), s32[]{:S(2)}) async-start(), calls=%async_computation.9 | async-start | bytes 2359296 | tf_op jit(solution)/shard_map/all_gather | solution.py:79
  8.7 123.2 %all-gather.11.cloned.1.call-start = ((), (), s32[]{:S(2)}) async-start(), calls=%async_computation.11 | async-start | bytes 1310720 | tf_op jit(solution)/shard_map/all_gather | solution.py:115
  56.3 128.0 %all-gather.13.cloned.1.call-start = ((), (), s32[]{:S(2)}) async-start(), calls=%async_computation.12 | async-start | bytes 2359296 | tf_op jit(solution)/shard_map/all_gather | solution.py:80
  56.9 181.5 %all-reduce.6.cloned.1.call-start = ((), (), s32[]{:S(2)}) async-start(), calls=%async_computation.13 | async-start | bytes 4194304 | tf_op jit(solution)/shard_map/psum | solution.py:143
  188.8 177.0 %all-gather.15.cloned.1.call-start = ((), (), s32[]{:S(2)}) async-start(), calls=%async_computation.14 | async-start | bytes 9437184 | tf_op jit(solution)/shard_map/all_gather | solution.py:81
  189.3 302.2 %all-gather.17.cloned.1.call-start = ((), (), s32[]{:S(2)}) async-start(), calls=%async_computation.15 | async-start | bytes 9437184 | tf_op jit(solution)/shard_map/all_gather | solution.py:82
  190.1 370.1 %all-reduce.8.cloned.1.call-start = ((), (), s32[]{:S(2)}) async-start(), calls=%async_computation.17 | async-start | bytes 4194304 | tf_op jit(solution)/shard_map/psum | solution.py:167
  510.5 134.0 %reduce-scatter.14.cloned.1.call-start = ((), (), s32[]{:S(2)}) async-start(), calls=%async_computation.19 | async-start | bytes 1310720 | tf_op jit(solution)/shard_map/reduce_scatter | solution.py:221
  617.1 63.8 %reduce-scatter.16.cloned.1.call-start = ((), (), s32[]{:S(2)}) async-start(), calls=%async_computation.20 | async-start | bytes 327680 | tf_op jit(solution)/shard_map/reduce_scatter | solution.py:232
  644.5 55.1 %reduce-scatter.12.cloned.1.call-start = ((), (), s32[]{:S(2)}) async-start(), calls=%async_computation.18 | async-start | bytes 2621440 | tf_op jit(solution)/shard_map/reduce_scatter | solution.py:229
  649.0 85.2 %reduce-scatter.10.cloned.1.call-start = ((), (), s32[]{:S(2)}) async-start(), calls=%async_computation.16 | async-start | bytes 2621440 | tf_op jit(solution)/shard_map/reduce_scatter | solution.py:154
  660.3 145.8 %reduce-scatter.22.cloned.1.call-start = ((), (), s32[]{:S(2)}) async-start(), calls=%async_computation.23 | async-start | bytes 2359296 | tf_op jit(solution)/shard_map/reduce_scatter | solution.py:249
  663.0 213.3 %reduce-scatter.18.cloned.1.call-start = ((), (), s32[]{:S(2)}) async-start(), calls=%async_computation.21 | async-start | bytes 2359296 | tf_op jit(solution)/shard_map/reduce_scatter | solution.py:246
  667.5 340.5 %all-reduce.10.cloned.1.call-start = ((), (), s32[]{:S(2)}) async-start(), calls=%async_computation.26 | async-start | bytes 181248 | tf_op jit(solution)/shard_map/psum | solution.py:265
  702.6 459.7 %reduce-scatter.26.cloned.1.call-start = ((), (), s32[]{:S(2)}) async-start(), calls=%async_computation.25 | async-start | bytes 9437184 | tf_op jit(solution)/shard_map/reduce_scatter | solution.py:255
  713.8 600.1 %reduce-scatter.24.cloned.1.call-start = ((), (), s32[]{:S(2)}) async-start(), calls=%async_computation.24 | async-start | bytes 9437184 | tf_op jit(solution)/shard_map/reduce_scatter | solution.py:252
  725.4 727.1 %reduce-scatter.20.cloned.1.call-start = ((), (), s32[]{:S(2)}) async-start(), calls=%async_computation.22 | async-start | bytes 2162688 | tf_op jit(solution)/shard_map/reduce_scatter | solution.py:238
  1008.0 445.2 %copy-start.37 = (f32[2048]{0:T(1024)S(1)}, f32[2048]{0:T(1024)}, u32[]{:S(2)}) copy-start(f32[2048]{0:T(1024)} %get-tuple-element.618) | copy-start | bytes 24580
  1008.0 445.8 %copy-start.48 = (f32[128]{0:T(128)S(1)}, f32[128]{0:T(128)}, u32[]{:S(2)}) copy-start(f32[128]{0:T(128)} %get-tuple-element.622) | copy-start | bytes 1540
  1008.0 446.3 %copy-start.36 = (f32[2048]{0:T(1024)S(1)}, f32[2048]{0:T(1024)}, u32[]{:S(2)}) copy-start(f32[2048]{0:T(1024)} %get-tuple-element.624) | copy-start | bytes 24580
  1008.0 446.9 %copy-start.35 = (f32[2048]{0:T(1024)S(1)}, f32[2048]{0:T(1024)}, u32[]{:S(2)}) copy-start(f32[2048]{0:T(1024)} %get-tuple-element.625) | copy-start | bytes 24580
  1008.0 447.5 %copy-start.34 = (f32[2048]{0:T(1024)S(1)}, f32[2048]{0:T(1024)}, u32[]{:S(2)}) copy-start(f32[2048]{0:T(1024)} %get-tuple-element.626) | copy-start | bytes 24580
  1008.0 448.1 %copy-start.33 = (f32[2048]{0:T(1024)S(1)}, f32[2048]{0:T(1024)}, u32[]{:S(2)}) copy-start(f32[2048]{0:T(1024)} %get-tuple-element.630) | copy-start | bytes 24580
  (47 other events, 2286.8 us)
Sparse Core Ops, SparseCore 0:
  10.2 42.8 all-gather.8
  55.2 48.0 all-gather.6
  105.4 26.4 all-gather.10
  133.7 50.5 all-gather.12
  188.9 49.5 all-reduce.5
  240.7 125.0 all-gather.14
  367.9 123.5 all-gather.16
  510.6 49.5 all-reduce.7
  617.2 27.2 reduce-scatter.13
  646.9 18.6 reduce-scatter.15
  668.1 31.4 reduce-scatter.11
  702.7 31.4 reduce-scatter.9
  737.7 68.3 reduce-scatter.21
  809.5 66.7 reduce-scatter.17
  883.7 124.1 all-reduce.9
  1011.9 150.4 reduce-scatter.25
  1165.8 147.9 reduce-scatter.23
  1316.6 135.8 reduce-scatter.19
where the time goes:
time: 1470 us; the launch traced here: 1460 us
  waiting for transfers between devices  1220 us (83%)
  matrix products  122 us (8%)
  other arithmetic  65.9 us (4%)
  local copies, waits for them, and re-layouts  26.8 us (2%)
  between operations  15.3 us (1%)
    reduce_scatter x1, waiting for transfers between devices, body(): lax.psum_scatter(down_grad.astype(jnp.bfloat16), ('fsdp', 'ctx'), scatter...  152 us
    reduce_scatter x1, waiting for transfers between devices, body(): lax.psum_scatter(up_grad.astype(jnp.bfloat16), ('fsdp', 'ctx'), scatter_d...  149 us
    reduce_scatter x1, waiting for transfers between devices, body(): lax.psum_scatter(kv_w_grad, ('fsdp', 'ctx', 'tp'), scatter_dimension=0, t...  136 us
    psum x1, waiting for transfers between devices, body(): lax.psum((ln1_gain_grad, ln1_bias_grad, q_bias_slots, value_bias_grad, o_...  126 us
    all_gather x1, waiting for transfers between devices, body(): lax.all_gather(up_weight, ('fsdp', 'ctx'), axis=0, tiled=True)  122 us
    all_gather x1, waiting for transfers between devices, body(): lax.all_gather(down_weight, ('fsdp', 'ctx'), axis=1, tiled=True)  115 us
    reduce_scatter x1, waiting for transfers between devices, body(): lax.psum_scatter(out_w_grad.astype(jnp.bfloat16), ('fsdp', 'ctx'), scatte...  69.6 us
    reduce_scatter x1, waiting for transfers between devices, body(): lax.psum_scatter(query_w_grad.astype(jnp.bfloat16), ('fsdp', 'ctx'), scat...  68.4 us
  transfers between devices with their start and end apart: 18, of which 17 were waited for; matrix products, arithmetic and copies ran while one was open for 9% of the time, Pallas kernels for 0%

commit v1 on v0

v1 whole, which is shorter than its diff:
```python
import math

import jax
import jax.numpy as jnp
import numpy as np
from jax import lax
from jax.sharding import PartitionSpec as P

eps = 1e-05
masked_score = -1000000000.0
f32 = jnp.float32
bf16 = jnp.bfloat16
ring_axes = ("fsdp", "ctx")


def ring_order(rows, cols):
    if rows == 1:
        return list(range(cols))
    if cols == 1:
        return list(range(rows))
    if rows % 2 == 0:
        walk = [(0, c) for c in range(cols)]
        for step, c in enumerate(range(cols - 1, -1, -1)):
            span = range(1, rows) if step % 2 == 0 else range(rows - 1, 0, -1)
            walk += [(r, c) for r in span]
        if cols % 2 == 0 or rows == 2:
            return [r * cols + c for r, c in walk]
    return list(range(rows * cols))


class Ring:
    def __init__(self, rows, cols, place):
        self.size = rows * cols
        order = ring_order(rows, cols)
        where = [0] * self.size
        for spot, owner in enumerate(order):
            where[owner] = spot
        n = self.size
        self.right = [(order[i], order[(i + 1) % n]) for i in range(n)]
        self.left = [(b, a) for a, b in self.right]
        spot = jnp.asarray(np.array(where, np.int32))[place]
        self.slots = jnp.asarray(np.array(order, np.int32))[
            lax.rem(spot - jnp.arange(n, dtype=jnp.int32) + n, n)
        ]
        self.homes = lax.rem(spot - jnp.asarray(np.array(where, np.int32)) + n, n)

    def hops(self, flip):
        far = self.size // 2
        near = self.size - 1 - far
        return (near, far) if flip else (far, near)

    def gather(self, shard, flip):
        hops_right, hops_left = self.hops(flip)
        slots = [shard] * self.size
        moving = shard
        for k in range(1, hops_right + 1):
            moving = lax.ppermute(moving, ring_axes, self.right)
            slots[k] = moving
        moving = shard
        for k in range(1, hops_left + 1):
            moving = lax.ppermute(moving, ring_axes, self.left)
            slots[self.size - k] = moving
        return slots

    def scatter(self, part, flip):
        hops_right, hops_left = self.hops(flip)
        n = self.size
        total = part(0)
        for hops, sign, pairs in ((hops_right, -1, self.right), (hops_left, 1, self.left)):
            moving = None
            for k in range(hops, 0, -1):
                piece = part((sign * k) % n)
                if moving is not None:
                    piece = piece + moving.astype(f32)
                moving = lax.ppermute(piece.astype(bf16), ring_axes, pairs)
            if moving is not None:
                total = total + moving.astype(f32)
        return total

    def into(self, values):
        width = values.shape[-1] // self.size
        return jnp.concatenate(
            [
                lax.dynamic_slice_in_dim(values, self.slots[k] * width, width, values.ndim - 1)
                for k in range(self.size)
            ],
            axis=-1,
        )

    def back(self, values):
        width = values.shape[-1] // self.size
        return jnp.concatenate(
            [
                lax.dynamic_slice_in_dim(values, self.homes[k] * width, width, values.ndim - 1)
                for k in range(self.size)
            ],
            axis=-1,
        )


def swap(values, axis, bit):
    count = lax.axis_size(axis)
    return lax.ppermute(values, axis, [(i, i ^ bit) for i in range(count)])


def bits_of(axis):
    count = lax.axis_size(axis)
    bit = 1
    while bit < count:
        yield bit
        bit *= 2


def share_sum(rows):
    for bit in bits_of("tp"):
        count = lax.axis_size("tp") // bit
        pairs = rows.reshape((count // 2, 2) + (-1,) + rows.shape[1:])
        other = swap(pairs[:, 1].astype(bf16), "tp", bit)
        rows = pairs[:, 0].astype(f32) + other.astype(f32)
        rows = rows.reshape((-1,) + rows.shape[2:])
    return rows


def share_spread(rows):
    for bit in reversed(list(bits_of("tp"))):
        rows = rows.reshape((-1, 1) + (lax.axis_size("tp") and rows.shape[-2:]))
        rows = jnp.concatenate([rows, swap(rows, "tp", bit)], axis=1)
        rows = rows.reshape((-1,) + rows.shape[2:])
    return rows.reshape((-1,) + rows.shape[-1:])


def everyone_sum(values, axes):
    for axis in axes:
        for bit in bits_of(axis):
            values = values + swap(values, axis, bit)
    return values


def dot(left, right, dims):
    return lax.dot_general(left, right, (dims, ((), ())), preferred_element_type=f32)


NN = ((1,), (0,))
NT = ((1,), (1,))
TN = ((0,), (0,))


def normed(values):
    center = jnp.mean(values, axis=-1, keepdims=True)
    centred = values - center
    spread = jnp.mean(centred * centred, axis=-1, keepdims=True)
    inv = lax.rsqrt(spread + eps)
    return centred * inv, inv


def normed_back(grad, gain, norm, inv):
    pulled = grad * gain
    term = pulled - jnp.mean(pulled, axis=-1, keepdims=True)
    return inv * (term - norm * jnp.mean(pulled * norm, axis=-1, keepdims=True))


def parent_lookup(seg_ids, parents):
    labels = jnp.arange(parents.shape[0], dtype=jnp.int32)
    picked = jnp.where(seg_ids[:, None] == labels[None, :], parents[None, :], 0)
    return jnp.sum(picked, axis=1)


def gelu_parts(values):
    scale = math.sqrt(2.0 / math.pi)
    squared = values * values
    bend = jnp.tanh(scale * (values + 0.044715 * squared * values))
    out = 0.5 * values * (1.0 + bend)
    slope = 0.5 * (1.0 + bend) + 0.5 * values * (1.0 - bend * bend) * scale * (
        1.0 + 3 * 0.044715 * squared
    )
    return out, slope


def body(
    tokens,
    token_segment,
    segment_parent,
    ln1_gain,
    ln1_bias,
    q_weight,
    q_bias,
    kv_weight,
    value_bias,
    o_weight,
    o_bias,
    ln2_gain,
    ln2_bias,
    up_weight,
    up_bias,
    down_weight,
    down_bias,
    out_grad,
):
    row_count, width = tokens.shape
    head_size = value_bias.shape[0]
    local_width = q_weight.shape[1]
    local_heads = local_width // head_size
    tree_length = token_segment.shape[0]
    score_scale = 1.0 / math.sqrt(head_size)
    ctx_count = lax.axis_size("ctx")
    tp_count = lax.axis_size("tp")
    ctx_index = lax.axis_index("ctx")
    tp_index = lax.axis_index("tp")
    share_rows = row_count // tp_count
    ring = Ring(lax.axis_size("fsdp"), ctx_count, lax.axis_index("fsdp") * ctx_count + ctx_index)
    n = ring.size
    piece = width // n

    qkv_slots = ring.gather(jnp.concatenate([q_weight, kv_weight], axis=1), False)
    o_slots = ring.gather(o_weight, True)
    up_slots = ring.gather(up_weight, False)
    down_slots = ring.gather(down_weight, True)

    row_blocks = [tp_index ^ j for j in range(tp_count)]

    def rows_in(values):
        return jnp.concatenate(
            [
                lax.dynamic_slice_in_dim(values, b * share_rows, share_rows, 0)
                for b in row_blocks
            ],
            axis=0,
        )

    x_low = ring.into(rows_in(tokens))
    g_low = ring.into(rows_in(out_grad))
    vectors = ring.into(
        jnp.stack([ln1_gain, ln1_bias, o_bias, ln2_gain, ln2_bias, down_bias])
    ).astype(f32)
    gain_one, shift_one, o_shift, gain_two, shift_two, down_shift = (
        vectors[i : i + 1] for i in range(6)
    )
    own_place = rows_in(jnp.arange(row_count, dtype=jnp.int32))

    parents = segment_parent[0]
    query_place = ctx_index * row_count + own_place
    key_places = []
    for d in range(ctx_count):
        start = (ctx_index - d) * row_count
        key_places.append(jnp.where(start >= 0, start + own_place, tree_length))
    key_place = jnp.concatenate(key_places)
    segment_blocks = rows_in(token_segment.reshape(ctx_count, row_count).T)
    own_seg = lax.dynamic_slice_in_dim(segment_blocks, ctx_index, 1, 1)[:, 0]
    key_segment = jnp.concatenate(
        [
            lax.dynamic_slice_in_dim(
                segment_blocks, lax.rem(ctx_index - d + ctx_count, ctx_count), 1, 1
            )[:, 0]
            for d in range(ctx_count)
        ]
    )
    seg_one = parent_lookup(own_seg, parents)
    seg_two = parent_lookup(seg_one, parents)
    allowed = (
        (key_segment[None, :] == own_seg[:, None])
        | (key_segment[None, :] == seg_one[:, None])
        | (key_segment[None, :] == seg_two[:, None])
    ) & (key_place[None, :] <= query_place[:, None])

    norm_one, inv_one = normed(x_low.astype(f32))
    act_one = (norm_one * gain_one + shift_one).astype(bf16)
    qkv_full = jnp.concatenate(qkv_slots, axis=0)
    qkv_shift = jnp.concatenate(
        [q_bias.astype(f32), jnp.zeros((head_size,), f32), value_bias.astype(f32)]
    )
    qkv = (dot(act_one, qkv_full, NN) + qkv_shift).astype(bf16)
    queries = qkv[:, :local_width]
    kv_own = qkv[:, local_width:]
    kv_rows = jnp.concatenate(
        [kv_own]
        + [
            lax.ppermute(kv_own, "ctx", [(c, c + d) for c in range(ctx_count - d)])
            for d in range(1, ctx_count)
        ],
        axis=0,
    )
    keys_all = kv_rows[:, :head_size]
    values_all = kv_rows[:, head_size:]

    def scores_of(h):
        raw = dot(queries[:, h * head_size : (h + 1) * head_size], keys_all, NT) * score_scale
        return jnp.where(allowed, raw, masked_score)

    mixed, logs = [], []
    for h in range(local_heads):
        scores = scores_of(h)
        row_max = jnp.max(scores, axis=1, keepdims=True)
        exp_scores = jnp.exp(scores - row_max)
        row_total = jnp.sum(exp_scores, axis=1, keepdims=True)
        probs_low = (exp_scores / row_total).astype(bf16)
        mixed.append(dot(probs_low, values_all, NN).astype(bf16))
        logs.append(row_max + jnp.log(row_total))
    attended = jnp.concatenate(mixed, axis=1)

    o_full = jnp.concatenate(o_slots, axis=1)
    attn_share = share_sum(dot(attended, o_full, NN).astype(bf16))
    x_share = x_low[:share_rows].astype(f32)
    residual = x_share + (attn_share + o_shift)
    norm_two, inv_two = normed(residual)
    act_two = share_spread((norm_two * gain_two + shift_two).astype(bf16))

    up_full = jnp.concatenate(up_slots, axis=0)
    pre_act = dot(act_two, up_full, NN) + up_bias.astype(f32)
    gelu_out, gelu_slope = gelu_parts(pre_act)
    hidden = gelu_out.astype(bf16)
    down_w_grad = ring.scatter(
        lambda k: dot(hidden, g_low[:, k * piece : (k + 1) * piece], TN), False
    )
    down_full = jnp.concatenate(down_slots, axis=1)
    grad_hidden = dot(g_low, down_full, NT)
    grad_pre = (grad_hidden * gelu_slope).astype(bf16)
    up_w_grad = ring.scatter(
        lambda k: dot(act_two[:, k * piece : (k + 1) * piece], grad_pre, TN), True
    )
    grad_two = share_sum(dot(grad_pre, up_full, NT).astype(bf16))
    ffn_share = share_sum(dot(hidden, down_full, NN).astype(bf16))
    layer_out = ring.back((residual + (ffn_share + down_shift)).astype(bf16))

    up_bias_grad = jnp.sum(grad_pre.astype(f32), axis=0)
    g_share = g_low[:share_rows].astype(f32)
    grad_res = g_share + normed_back(grad_two, gain_two, norm_two, inv_two)
    grad_attn_share = grad_res.astype(bf16)
    grad_attn = share_spread(grad_attn_share)
    out_w_grad = ring.scatter(
        lambda k: dot(attended, grad_attn[:, k * piece : (k + 1) * piece], TN), False
    )
    grad_attended = dot(grad_attn, o_full, NT).astype(bf16)
    early = jnp.stack(
        [
            jnp.sum(g_share, axis=0),
            jnp.sum(grad_attn_share.astype(f32), axis=0),
            jnp.sum(grad_two * norm_two, axis=0),
            jnp.sum(grad_two, axis=0),
        ]
    )
    early = everyone_sum(ring.back(early), ("tp", "ctx", "fsdp"))
    up_bias_out = everyone_sum(up_bias_grad, ("ctx", "fsdp"))

    key_grad = jnp.zeros((tree_length, head_size), f32)
    value_grad = jnp.zeros((tree_length, head_size), f32)
    query_grads = []
    for h in range(local_heads):
        cols = slice(h * head_size, (h + 1) * head_size)
        attn_probs = jnp.exp(scores_of(h) - logs[h])
        probs_low = attn_probs.astype(bf16)
        grad_head = grad_attended[:, cols]
        grad_probs = dot(grad_head, values_all, NT)
        row_delta = jnp.sum(attn_probs * grad_probs, axis=1, keepdims=True)
        grad_scores = (attn_probs * (grad_probs - row_delta)).astype(bf16)
        query_grads.append((dot(grad_scores, keys_all, NN) * score_scale).astype(bf16))
        key_grad = key_grad + dot(grad_scores, queries[:, cols], TN) * score_scale
        value_grad = value_grad + dot(probs_low, grad_head, TN)
    grad_query = jnp.concatenate(query_grads, axis=1)
    q_bias_grad = jnp.sum(grad_query.astype(f32), axis=0)

    kv_part = jnp.concatenate([key_grad, value_grad], axis=1).astype(bf16)
    kv_part = kv_part.reshape(ctx_count, tp_count, share_rows, 2 * head_size)
    kv_part = jnp.swapaxes(kv_part, 0, 1).reshape(tp_count * ctx_count * share_rows, -1)
    kv_part = share_sum(kv_part).reshape(ctx_count, share_rows, 2 * head_size)
    kv_sum = kv_part[0]
    for d in range(1, ctx_count):
        kv_sum = kv_sum + lax.ppermute(
            kv_part[d].astype(bf16), "ctx", [(c, c - d) for c in range(d, ctx_count)]
        ).astype(f32)
    kv_low_share = kv_sum.astype(bf16)
    kv_low = share_spread(kv_low_share)

    sub = piece // tp_count
    kv_cols = act_one.reshape(row_count, n, tp_count, sub)
    kv_cols = lax.dynamic_slice_in_dim(kv_cols, tp_index, 1, 2).reshape(row_count, n * sub)

    def q_kv_part(k):
        q_piece = dot(act_one[:, k * piece : (k + 1) * piece], grad_query, TN)
        kv_piece = dot(kv_cols[:, k * sub : (k + 1) * sub], kv_low, TN)
        return jnp.concatenate([q_piece.reshape(-1), kv_piece.reshape(-1)]).reshape(
            -1, local_width
        )

    q_kv = ring.scatter(q_kv_part, True)
    q_w_grad = q_kv[:piece]
    kv_w_grad = q_kv[piece:].reshape(sub, 2 * head_size)

    q_full = qkv_full[:, :local_width]
    kv_full = qkv_full[:, local_width:]
    grad_act = share_sum(dot(grad_query, q_full, NT).astype(bf16)) + dot(
        kv_low_share, kv_full, NT
    )
    norm_share = norm_one[:share_rows]
    inv_share = inv_one[:share_rows]
    input_grad = ring.back(
        (grad_res + normed_back(grad_act, gain_one, norm_share, inv_share)).astype(bf16)
    )
    late = jnp.stack([jnp.sum(grad_act * norm_share, axis=0), jnp.sum(grad_act, axis=0)])
    late = ring.back(late).reshape(-1)
    value_bias_grad = jnp.sum(kv_low_share[:, head_size:].astype(f32), axis=0)
    late = everyone_sum(jnp.concatenate([late, value_bias_grad]), ("tp",))
    late = everyone_sum(jnp.concatenate([late, q_bias_grad]), ("ctx", "fsdp"))
    return (
        layer_out,
        input_grad,
        late[:width],
        late[width : 2 * width],
        q_w_grad,
        late[2 * width + head_size :],
        kv_w_grad,
        late[2 * width : 2 * width + head_size],
        out_w_grad,
        early[1],
        early[2],
        early[3],
        up_w_grad,
        up_bias_out,
        down_w_grad,
        early[0],
    )


def solution(mesh):
    whole = P()
    rows = P(("fsdp", "ctx"), None)
    split = P(("fsdp", "ctx"), "tp")
    turned = P("tp", ("fsdp", "ctx"))
    thin = P(("fsdp", "ctx", "tp"), None)
    in_specs = (
        rows, P("fsdp"), P("fsdp", None), whole, whole, split, P("tp"), rows, whole,
        turned, whole, whole, whole, split, P("tp"), turned, whole, rows,
    )
    out_specs = (
        thin, thin, whole, whole, split, P("tp"), thin, whole, turned, whole, whole, whole,
        split, P("tp"), turned, whole,
    )
    return jax.shard_map(body, mesh=mesh, in_specs=in_specs, out_specs=out_specs, check_vma=False)
```

time: 1470 us -> 714 us (0.49)
  waiting for transfers between devices: 1220 us -> 258 us
  starting transfers between devices: 1.45 us -> 128 us
  local copies, waits for them, and re-layouts: 26.8 us -> 118 us
    reduce_scatter x9 -> x0, waiting for transfers between devices: 624 us -> none  [the longest x1 152 us: body(): lax.psum_scatter(down_grad.astype(jnp.bfloat16), ('fsdp', 'ctx'), scatter...]
    all_gather x6 -> x0, waiting for transfers between devices: 372 us -> none  [the longest x1 122 us: body(): lax.all_gather(up_weight, ('fsdp', 'ctx'), axis=0, tiled=True)]
    ppermute x0 -> x91, waiting for transfers between devices: none -> 258 us  [the longest x29 96.6 us: swap(): return lax.ppermute(values, axis, [(i, i ^ bit) for i in range(count)])]
    psum x3 -> x0, waiting for transfers between devices: 224 us -> none  [the longest x1 126 us: body(): lax.psum((ln1_gain_grad, ln1_bias_grad, q_bias_slots, value_bias_grad, o_...]
    ppermute x0 -> x91, starting transfers between devices: none -> 128 us  [the longest x14 51.8 us: gather(): moving = lax.ppermute(moving, ring_axes, self.right)]
    unnamed x102 -> x314, local copies, waits for them, and re-layouts: 10.4 us -> 65.9 us
    reduce_sum x15 -> x13, other arithmetic: 28.1 us -> 8.2 us  [the longest x4 2.82 us: body(): row_total = jnp.sum(exp_scores, axis=1, keepdims=True)]
    dynamic_slice x13 -> x17, local copies, waits for them, and re-layouts: 4.91 us -> 21.7 us  [the longest x8 13.7 us: into(): lax.dynamic_slice_in_dim(values, self.slots[k] * width, width, values.ndi...]
  transfers between devices with their start and end apart: 18 -> 91, of which waited for: 17 -> 37; matrix products, arithmetic and copies ran while one was open for 9% -> 32% of each run, Pallas kernels for 0% -> 0%
where the time goes in v1:
time: 714 us; the launch traced here: 704 us
  waiting for transfers between devices  258 us (36%)
  starting transfers between devices  128 us (18%)
  local copies, waits for them, and re-layouts  118 us (17%)
  matrix products  118 us (17%)
  other arithmetic  56.7 us (8%)
  between operations  25.8 us (4%)
    dot_general x73, matrix products, dot(): lax.dot_general(left, right, (dims, ((), ())), preferred_element_type=f32)  118 us
    ppermute x29, waiting for transfers between devices, swap(): return lax.ppermute(values, axis, [(i, i ^ bit) for i in range(count)])  96.6 us
    ppermute x14, waiting for transfers between devices, gather(): moving = lax.ppermute(moving, ring_axes, self.left)  91 us
    unnamed x314, local copies, waits for them, and re-layouts  65.9 us
    ppermute x14, starting transfers between devices, gather(): moving = lax.ppermute(moving, ring_axes, self.right)  51.8 us
    ppermute x28, waiting for transfers between devices, scatter(): moving = lax.ppermute(piece.astype(bf16), ring_axes, pairs)  44.8 us
    ppermute x28, starting transfers between devices, scatter(): moving = lax.ppermute(piece.astype(bf16), ring_axes, pairs)  32.7 us
    ppermute x29, starting transfers between devices, swap(): return lax.ppermute(values, axis, [(i, i ^ bit) for i in range(count)])  26.6 us
  transfers between devices with their start and end apart: 91, of which 37 were waited for; matrix products, arithmetic and copies ran while one was open for 32% of the time, Pallas kernels for 0%

profile of v1, /device:TPU:0, one launch (start us, length us, event | category | flops | bytes accessed | tf_op | source)
XLA Modules:
  0.0 703.8 jit_solution(14402140095300521635)
XLA Ops:
  120.8 23.7 %collective-permute-done.6 = bf16[256,768]{1,0:T(8,128)(2,1)S(1)} collective-permute-done((bf16[256,768]{1,0:T(8,128)(2,1)S(1)}, bf16[256,768]{1,0:T(8,128)(2,1)S(1)}, u32[]{:S(2)}, u32[]{:S(2)}) %collective-permute-start.6) | collective-permute-done | bytes 393248 | tf_op jit(solution)/shard_map/ppermute | solution.py:61
  167.8 13.1 %collective-permute-start.22 = (bf16[256,2048]{1,0:T(8,128)(2,1)}, bf16[256,2048]{1,0:T(8,128)(2,1)S(1)}, u32[]{:S(2)}, u32[]{:S(2)}) collective-permute-start(bf16[256,2048]{1,0:T(8,128)(2,1)} %collective-permute-done.21), channel_id=1, source_target_pairs={{0,4},{4,8},{8,12},{12,28},{28,24},{24,20},{20,16},{16,0},{1,5},{5... | collective-permute-start | bytes 3145736 | tf_op jit(solution)/shard_map/ppermute | solution.py:57
  218.4 7.2 %collective-permute-start.23 = (bf16[256,2048]{1,0:T(8,128)(2,1)S(1)}, bf16[256,2048]{1,0:T(8,128)(2,1)S(1)}, u32[]{:S(2)}, u32[]{:S(2)}) collective-permute-start(bf16[256,2048]{1,0:T(8,128)(2,1)S(1)} %collective-permute-done.22), channel_id=1, source_target_pairs={{0,4},{4,8},{8,12},{12,28},{28,24},{24,20},{20,16},{16,0},{1,5},{5... | collective-permute-start | bytes 3145736 | tf_op jit(solution)/shard_map/ppermute | solution.py:57
  228.8 7.8 %collective-permute-done.26 = bf16[256,2048]{1,0:T(8,128)(2,1)S(1)} collective-permute-done((bf16[256,2048]{1,0:T(8,128)(2,1)S(1)}, bf16[256,2048]{1,0:T(8,128)(2,1)S(1)}, u32[]{:S(2)}, u32[]{:S(2)}) %collective-permute-start.26) | collective-permute-done | bytes 1048608 | tf_op jit(solution)/shard_map/ppermute | solution.py:61
  236.6 4.2 collective-permute-done.29
  240.8 7.2 %collective-permute-start.30 = (bf16[2048,256]{1,0:T(8,128)(2,1)S(1)}, bf16[2048,256]{1,0:T(8,128)(2,1)S(1)}, u32[]{:S(2)}, u32[]{:S(2)}) collective-permute-start(bf16[2048,256]{1,0:T(8,128)(2,1)S(1)} %collective-permute-done.29), channel_id=1, source_target_pairs={{0,4},{4,8},{8,12},{12,28},{28,24},{24,20},{20,16},{16,0},{1,5},{5... | collective-permute-start | bytes 3145736 | tf_op jit(solution)/shard_map/ppermute | solution.py:57
  248.0 11.1 %collective-permute-done.32 = bf16[2048,256]{1,0:T(8,128)(2,1)S(1)} collective-permute-done((bf16[2048,256]{1,0:T(8,128)(2,1)S(1)}, bf16[2048,256]{1,0:T(8,128)(2,1)S(1)}, u32[]{:S(2)}, u32[]{:S(2)}) %collective-permute-start.32) | collective-permute-done | bytes 1048608 | tf_op jit(solution)/shard_map/ppermute | solution.py:61
  259.2 4.1 collective-permute-done.23
  263.3 7.2 %collective-permute-start.24 = (bf16[256,2048]{1,0:T(8,128)(2,1)S(1)}, bf16[256,2048]{1,0:T(8,128)(2,1)S(1)}, u32[]{:S(2)}, u32[]{:S(2)}) collective-permute-start(bf16[256,2048]{1,0:T(8,128)(2,1)S(1)} %collective-permute-done.23), channel_id=1, source_target_pairs={{0,4},{4,8},{8,12},{12,28},{28,24},{24,20},{20,16},{16,0},{1,5},{5... | collective-permute-start | bytes 3145736 | tf_op jit(solution)/shard_map/ppermute | solution.py:57
  275.0 27.1 %collective-permute-done.33 = bf16[2048,256]{1,0:T(8,128)(2,1)S(1)} collective-permute-done((bf16[2048,256]{1,0:T(8,128)(2,1)S(1)}, bf16[2048,256]{1,0:T(8,128)(2,1)S(1)}, u32[]{:S(2)}, u32[]{:S(2)}) %collective-permute-start.33) | collective-permute-done | bytes 1048608 | tf_op jit(solution)/shard_map/ppermute | solution.py:61
  305.8 20.3 %collective-permute-done.34 = bf16[2048,256]{1,0:T(8,128)(2,1)S(1)} collective-permute-done((bf16[2048,256]{1,0:T(8,128)(2,1)S(1)}, bf16[2048,256]{1,0:T(8,128)(2,1)S(1)}, u32[]{:S(2)}, u32[]{:S(2)}) %collective-permute-start.34) | collective-permute-done | bytes 1048608 | tf_op jit(solution)/shard_map/ppermute | solution.py:61
  331.3 7.0 multiply_convert_fusion.5
  346.4 12.5 %convert_reduce_fusion.1 = (f32[2048]{0:T(1024)}, bf16[512,2048]{1,0:T(8,128)(2,1)S(1)}) fusion(f32[512,2048]{1,0:T(8,128)} %get-tuple-element.115, f32[2048]{0:T(1024)} %convert_element_type.476, bf16[512,2048]{1,0:T(8,128)(2,1)} %dynamic-slice_dynamic-update-slice_fusion, bf16[2048,2048]{1,0:T(8,128)(2,1)} %constant_dynamic-update-slice_fusion.43), kind=kOutput, calls=%fused_computation.9 | convolution fusion | flops 4316985344 | bytes 16793600 | tf_op jit(solution)/shard_map/dot_general | solution.py:140
  361.9 9.7 %convolution_convert_fusion.1 = bf16[512,2048]{1,0:T(8,128)(2,1)} fusion(bf16[512,2048]{1,0:T(8,128)(2,1)S(1)} %get-tuple-element.125, bf16[2048,2048]{1,0:T(8,128)(2,1)} %copy-done.47), kind=kOutput, calls=%fused_computation.47 | convolution fusion | flops 4296015872 | bytes 12582912 | tf_op jit(solution)/shard_map/dot_general | solution.py:140
  371.7 8.3 %convolution_convert_fusion.2 = bf16[512,2048]{1,0:T(8,128)(2,1)S(1)} fusion(bf16[512,2048]{1,0:T(8,128)(2,1)S(1)} %get-tuple-element.114, bf16[2048,2048]{1,0:T(8,128)(2,1)} %constant_dynamic-update-slice_fusion.43), kind=kOutput, calls=%fused_computation.48 | convolution fusion | flops 4296015872 | bytes 12582912 | tf_op jit(solution)/shard_map/dot_general | solution.py:140
  387.3 19.5 %collective-permute-done.81 = f32[2048]{0:T(1024)S(1)} collective-permute-done((f32[2048]{0:T(1024)S(1)}, f32[2048]{0:T(1024)S(1)}, u32[]{:S(2)}, u32[]{:S(2)}) %collective-permute-start.81) | collective-permute-done | bytes 8224 | tf_op jit(solution)/shard_map/ppermute | solution.py:103
  408.5 16.2 %collective-permute-done.82 = f32[2048]{0:T(1024)S(1)} collective-permute-done((f32[2048]{0:T(1024)S(1)}, f32[2048]{0:T(1024)S(1)}, u32[]{:S(2)}, u32[]{:S(2)}) %collective-permute-start.82) | collective-permute-done | bytes 8224 | tf_op jit(solution)/shard_map/ppermute | solution.py:103
  439.5 11.3 %collective-permute-done.38 = bf16[1,128,2048]{2,1,0:T(8,128)(2,1)S(1)} collective-permute-done((bf16[1,128,2048]{2,1,0:T(8,128)(2,1)S(1)}, bf16[1,128,2048]{2,1,0:T(8,128)(2,1)S(1)}, u32[]{:S(2)}, u32[]{:S(2)}) %collective-permute-start.38) | collective-permute-done | bytes 524320 | tf_op jit(solution)/shard_map/ppermute | solution.py:103
  452.9 10.1 %collective-permute-done.36 = bf16[1,128,2048]{2,1,0:T(8,128)(2,1)S(1)} collective-permute-done((bf16[1,128,2048]{2,1,0:T(8,128)(2,1)S(1)}, bf16[1,128,2048]{2,1,0:T(8,128)(2,1)S(1)}, u32[]{:S(2)}, u32[]{:S(2)}) %collective-permute-start.36) | collective-permute-done | bytes 524320 | tf_op jit(solution)/shard_map/ppermute | solution.py:103
  472.1 9.3 %collective-permute-done.71 = f32[4,2048]{1,0:T(4,128)S(1)} collective-permute-done((f32[4,2048]{1,0:T(4,128)S(1)}, f32[4,2048]{1,0:T(4,128)S(1)}, u32[]{:S(2)}, u32[]{:S(2)}) %collective-permute-start.71) | collective-permute-done | bytes 32800 | tf_op jit(solution)/shard_map/ppermute | solution.py:103
  493.6 7.3 %collective-permute-done.39 = bf16[1,1,128,2048]{3,2,1,0:T(8,128)(2,1)S(1)} collective-permute-done((bf16[1,1,128,2048]{3,2,1,0:T(8,128)(2,1)S(1)}, bf16[1,1,128,2048]{3,2,1,0:T(8,128)(2,1)S(1)}, u32[]{:S(2)}, u32[]{:S(2)}) %collective-permute-start.39) | collective-permute-done | bytes 524320 | tf_op jit(solution)/shard_map/ppermute | solution.py:103
  544.7 6.0 collective-permute-done.79
  569.7 4.6 collective-permute-done.63
  603.2 30.3 %collective-permute-done.87 = bf16[2048,256]{1,0:T(8,128)(2,1)S(1)} collective-permute-done((bf16[2048,256]{1,0:T(8,128)(2,1)S(1)}, bf16[2048,256]{1,0:T(8,128)(2,1)S(1)}, u32[]{:S(2)}, u32[]{:S(2)}) %collective-permute-start.87) | collective-permute-done | bytes 1048608 | tf_op jit(solution)/shard_map/ppermute | solution.py:75
  (739 shorter events, 393.0 us)
Async XLA Ops:
  4.4 77.4 %collective-permute-start = (bf16[256,768]{1,0:T(8,128)(2,1)}, bf16[256,768]{1,0:T(8,128)(2,1)}, u32[]{:S(2)}, u32[]{:S(2)}) collective-permute-start(bf16[256,768]{1,0:T(8,128)(2,1)} %get-tuple-element.67), channel_id=1, source_target_pairs={{0,4},{4,8},{8,12},{12,28},{28,24},{24,20},{20,16},{16,0},{1,5},{5... | collective-permute-start | bytes 1179656 | tf_op jit(solution)/shard_map/ppermute | solution.py:57
  7.4 94.1 %collective-permute-start.4 = (bf16[256,768]{1,0:T(8,128)(2,1)}, bf16[256,768]{1,0:T(8,128)(2,1)}, u32[]{:S(2)}, u32[]{:S(2)}) collective-permute-start(bf16[256,768]{1,0:T(8,128)(2,1)} %get-tuple-element.67), channel_id=1, source_target_pairs={{4,0},{8,4},{12,8},{28,12},{24,28},{20,24},{16,20},{0,16},{5,1},{9... | collective-permute-start | bytes 1179656 | tf_op jit(solution)/shard_map/ppermute | solution.py:61
  7.4 78.5 %collective-permute-start.10 = (bf16[512,256]{1,0:T(8,128)(2,1)}, bf16[512,256]{1,0:T(8,128)(2,1)}, u32[]{:S(2)}, u32[]{:S(2)}) collective-permute-start(bf16[512,256]{1,0:T(8,128)(2,1)} %param.30), channel_id=1, source_target_pairs={{0,4},{4,8},{8,12},{12,28},{28,24},{24,20},{20,16},{16,0},{1,5},{5... | collective-permute-start | bytes 786440 | tf_op jit(solution)/shard_map/ppermute | solution.py:57
  9.4 74.6 %collective-permute-start.13 = (bf16[512,256]{1,0:T(8,128)(2,1)}, bf16[512,256]{1,0:T(8,128)(2,1)}, u32[]{:S(2)}, u32[]{:S(2)}) collective-permute-start(bf16[512,256]{1,0:T(8,128)(2,1)} %param.30), channel_id=1, source_target_pairs={{4,0},{8,4},{12,8},{28,12},{24,28},{20,24},{16,20},{0,16},{5,1},{9... | collective-permute-start | bytes 786440 | tf_op jit(solution)/shard_map/ppermute | solution.py:61
  9.4 152.7 %collective-permute-start.21 = (bf16[256,2048]{1,0:T(8,128)(2,1)}, bf16[256,2048]{1,0:T(8,128)(2,1)}, u32[]{:S(2)}, u32[]{:S(2)}) collective-permute-start(bf16[256,2048]{1,0:T(8,128)(2,1)} %param.34), channel_id=1, source_target_pairs={{0,4},{4,8},{8,12},{12,28},{28,24},{24,20},{20,16},{16,0},{1,5},{5... | collective-permute-start | bytes 3145736 | tf_op jit(solution)/shard_map/ppermute | solution.py:57
  111.1 99.3 %collective-permute-start.25 = (bf16[256,2048]{1,0:T(8,128)(2,1)S(1)}, bf16[256,2048]{1,0:T(8,128)(2,1)S(1)}, u32[]{:S(2)}, u32[]{:S(2)}) collective-permute-start(bf16[256,2048]{1,0:T(8,128)(2,1)S(1)} %copy-done.30), channel_id=1, source_target_pairs={{4,0},{8,4},{12,8},{28,12},{24,28},{20,24},{16,20},{0,16},{5,1},{9... | collective-permute-start | bytes 3145736 | tf_op jit(solution)/shard_map/ppermute | solution.py:61
  162.1 48.4 %collective-permute-start.28 = (bf16[2048,256]{1,0:T(8,128)(2,1)S(1)}, bf16[2048,256]{1,0:T(8,128)(2,1)S(1)}, u32[]{:S(2)}, u32[]{:S(2)}) collective-permute-start(bf16[2048,256]{1,0:T(8,128)(2,1)S(1)} %copy-done.31), channel_id=1, source_target_pairs={{0,4},{4,8},{8,12},{12,28},{28,24},{24,20},{20,16},{16,0},{1,5},{5... | collective-permute-start | bytes 3145736 | tf_op jit(solution)/shard_map/ppermute | solution.py:57
  162.2 50.3 %collective-permute-start.31 = (bf16[2048,256]{1,0:T(8,128)(2,1)S(1)}, bf16[2048,256]{1,0:T(8,128)(2,1)S(1)}, u32[]{:S(2)}, u32[]{:S(2)}) collective-permute-start(bf16[2048,256]{1,0:T(8,128)(2,1)S(1)} %copy-done.31), channel_id=1, source_target_pairs={{4,0},{8,4},{12,8},{28,12},{24,28},{20,24},{16,20},{0,16},{5,1},{9... | collective-permute-start | bytes 3145736 | tf_op jit(solution)/shard_map/ppermute | solution.py:61
  167.8 50.7 %collective-permute-start.22 = (bf16[256,2048]{1,0:T(8,128)(2,1)}, bf16[256,2048]{1,0:T(8,128)(2,1)S(1)}, u32[]{:S(2)}, u32[]{:S(2)}) collective-permute-start(bf16[256,2048]{1,0:T(8,128)(2,1)} %collective-permute-done.21), channel_id=1, source_target_pairs={{0,4},{4,8},{8,12},{12,28},{28,24},{24,20},{20,16},{16,0},{1,5},{5... | collective-permute-start | bytes 3145736 | tf_op jit(solution)/shard_map/ppermute | solution.py:57
  212.5 46.5 %collective-permute-start.32 = (bf16[2048,256]{1,0:T(8,128)(2,1)S(1)}, bf16[2048,256]{1,0:T(8,128)(2,1)S(1)}, u32[]{:S(2)}, u32[]{:S(2)}) collective-permute-start(bf16[2048,256]{1,0:T(8,128)(2,1)S(1)} %collective-permute-done.31), channel_id=1, source_target_pairs={{4,0},{8,4},{12,8},{28,12},{24,28},{20,24},{16,20},{0,16},{5,1},{9... | collective-permute-start | bytes 3145736 | tf_op jit(solution)/shard_map/ppermute | solution.py:61
  236.6 68.9 %collective-permute-start.27 = (bf16[256,2048]{1,0:T(8,128)(2,1)S(1)}, bf16[256,2048]{1,0:T(8,128)(2,1)S(1)}, u32[]{:S(2)}, u32[]{:S(2)}) collective-permute-start(bf16[256,2048]{1,0:T(8,128)(2,1)S(1)} %collective-permute-done.26), channel_id=1, source_target_pairs={{4,0},{8,4},{12,8},{28,12},{24,28},{20,24},{16,20},{0,16},{5,1},{9... | collective-permute-start | bytes 3145736 | tf_op jit(solution)/shard_map/ppermute | solution.py:61
  240.8 61.7 %collective-permute-start.30 = (bf16[2048,256]{1,0:T(8,128)(2,1)S(1)}, bf16[2048,256]{1,0:T(8,128)(2,1)S(1)}, u32[]{:S(2)}, u32[]{:S(2)}) collective-permute-start(bf16[2048,256]{1,0:T(8,128)(2,1)S(1)} %collective-permute-done.29), channel_id=1, source_target_pairs={{0,4},{4,8},{8,12},{12,28},{28,24},{24,20},{20,16},{16,0},{1,5},{5... | collective-permute-start | bytes 3145736 | tf_op jit(solution)/shard_map/ppermute | solution.py:57
  380.0 49.0 %collective-permute-start.84 = (bf16[2048,256]{1,0:T(8,128)(2,1)S(1)}, bf16[2048,256]{1,0:T(8,128)(2,1)S(1)}, u32[]{:S(2)}, u32[]{:S(2)}) collective-permute-start(bf16[2048,256]{1,0:T(8,128)(2,1)S(1)} %copy-done.94), channel_id=1, source_target_pairs={{0,4},{4,8},{8,12},{12,28},{28,24},{24,20},{20,16},{16,0},{1,5},{5... | collective-permute-start | bytes 3145736 | tf_op jit(solution)/shard_map/ppermute | solution.py:75
  430.3 62.1 %collective-permute-start.85 = (bf16[2048,256]{1,0:T(8,128)(2,1)S(1)}, bf16[2048,256]{1,0:T(8,128)(2,1)S(1)}, u32[]{:S(2)}, u32[]{:S(2)}) collective-permute-start(bf16[2048,256]{1,0:T(8,128)(2,1)S(1)} %add_convert_fusion.5), channel_id=1, source_target_pairs={{0,4},{4,8},{8,12},{12,28},{28,24},{24,20},{20,16},{16,0},{1,5},{5... | collective-permute-start | bytes 3145736 | tf_op jit(solution)/shard_map/ppermute | solution.py:75
  432.3 68.9 %collective-permute-start.89 = (bf16[2048,256]{1,0:T(8,128)(2,1)S(1)}, bf16[2048,256]{1,0:T(8,128)(2,1)S(1)}, u32[]{:S(2)}, u32[]{:S(2)}) collective-permute-start(bf16[2048,256]{1,0:T(8,128)(2,1)S(1)} %add_convert_fusion.2), channel_id=1, source_target_pairs={{4,0},{8,4},{12,8},{28,12},{24,28},{20,24},{16,20},{0,16},{5,1},{9... | collective-permute-start | bytes 3145736 | tf_op jit(solution)/shard_map/ppermute | solution.py:75
  434.0 71.3 %collective-permute-start.75 = (bf16[256,2048]{1,0:T(8,128)(2,1)S(1)}, bf16[256,2048]{1,0:T(8,128)(2,1)S(1)}, u32[]{:S(2)}, u32[]{:S(2)}) collective-permute-start(bf16[256,2048]{1,0:T(8,128)(2,1)S(1)} %add_convert_fusion.10), channel_id=1, source_target_pairs={{0,4},{4,8},{8,12},{12,28},{28,24},{24,20},{20,16},{16,0},{1,5},{5... | collective-permute-start | bytes 3145736 | tf_op jit(solution)/shard_map/ppermute | solution.py:75
  436.7 65.9 %collective-permute-start.78 = (bf16[256,2048]{1,0:T(8,128)(2,1)S(1)}, bf16[256,2048]{1,0:T(8,128)(2,1)S(1)}, u32[]{:S(2)}, u32[]{:S(2)}) collective-permute-start(bf16[256,2048]{1,0:T(8,128)(2,1)S(1)} %add_convert_fusion.8), channel_id=1, source_target_pairs={{4,0},{8,4},{12,8},{28,12},{24,28},{20,24},{16,20},{0,16},{5,1},{9... | collective-permute-start | bytes 3145736 | tf_op jit(solution)/shard_map/ppermute | solution.py:75
  493.6 63.2 %collective-permute-start.86 = (bf16[2048,256]{1,0:T(8,128)(2,1)}, bf16[2048,256]{1,0:T(8,128)(2,1)}, u32[]{:S(2)}, u32[]{:S(2)}) collective-permute-start(bf16[2048,256]{1,0:T(8,128)(2,1)} %add_convert_fusion.4), channel_id=1, source_target_pairs={{0,4},{4,8},{8,12},{12,28},{28,24},{24,20},{20,16},{16,0},{1,5},{5... | collective-permute-start | bytes 3145736 | tf_op jit(solution)/shard_map/ppermute | solution.py:75
  502.4 98.8 %collective-permute-start.90 = (bf16[2048,256]{1,0:T(8,128)(2,1)}, bf16[2048,256]{1,0:T(8,128)(2,1)}, u32[]{:S(2)}, u32[]{:S(2)}) collective-permute-start(bf16[2048,256]{1,0:T(8,128)(2,1)} %add_convert_fusion.1), channel_id=1, source_target_pairs={{4,0},{8,4},{12,8},{28,12},{24,28},{20,24},{16,20},{0,16},{5,1},{9... | collective-permute-start | bytes 3145736 | tf_op jit(solution)/shard_map/ppermute | solution.py:75
  504.4 46.3 %collective-permute-start.79 = (bf16[256,2048]{1,0:T(8,128)(2,1)}, bf16[256,2048]{1,0:T(8,128)(2,1)}, u32[]{:S(2)}, u32[]{:S(2)}) collective-permute-start(bf16[256,2048]{1,0:T(8,128)(2,1)} %add_convert_fusion.7), channel_id=1, source_target_pairs={{4,0},{8,4},{12,8},{28,12},{24,28},{20,24},{16,20},{0,16},{5,1},{9... | collective-permute-start | bytes 3145736 | tf_op jit(solution)/shard_map/ppermute | solution.py:75
  584.9 51.4 %collective-permute-start.76 = (bf16[256,2048]{1,0:T(8,128)(2,1)S(1)}, bf16[256,2048]{1,0:T(8,128)(2,1)S(1)}, u32[]{:S(2)}, u32[]{:S(2)}) collective-permute-start(bf16[256,2048]{1,0:T(8,128)(2,1)S(1)} %copy-done.28), channel_id=1, source_target_pairs={{0,4},{4,8},{8,12},{12,28},{28,24},{24,20},{20,16},{16,0},{1,5},{5... | collective-permute-start | bytes 3145736 | tf_op jit(solution)/shard_map/ppermute | solution.py:75
  586.7 46.8 %collective-permute-start.87 = (bf16[2048,256]{1,0:T(8,128)(2,1)S(1)}, bf16[2048,256]{1,0:T(8,128)(2,1)S(1)}, u32[]{:S(2)}, u32[]{:S(2)}) collective-permute-start(bf16[2048,256]{1,0:T(8,128)(2,1)S(1)} %add_convert_fusion.3), channel_id=1, source_target_pairs={{0,4},{4,8},{8,12},{12,28},{28,24},{24,20},{20,16},{16,0},{1,5},{5... | collective-permute-start | bytes 3145736 | tf_op jit(solution)/shard_map/ppermute | solution.py:75
  597.3 62.8 %collective-permute-start.68 = (bf16[512,256]{1,0:T(8,128)(2,1)}, bf16[512,256]{1,0:T(8,128)(2,1)}, u32[]{:S(2)}, u32[]{:S(2)}) collective-permute-start(bf16[512,256]{1,0:T(8,128)(2,1)} %add_convert_fusion.20), channel_id=1, source_target_pairs={{4,0},{8,4},{12,8},{28,12},{24,28},{20,24},{16,20},{0,16},{5,1},{9... | collective-permute-start | bytes 786440 | tf_op jit(solution)/shard_map/ppermute | solution.py:75
  601.2 58.9 %collective-permute-start.65 = (bf16[512,256]{1,0:T(8,128)(2,1)}, bf16[512,256]{1,0:T(8,128)(2,1)}, u32[]{:S(2)}, u32[]{:S(2)}) collective-permute-start(bf16[512,256]{1,0:T(8,128)(2,1)} %add_convert_fusion.22), channel_id=1, source_target_pairs={{0,4},{4,8},{8,12},{12,28},{28,24},{24,20},{20,16},{16,0},{1,5},{5... | collective-permute-start | bytes 786440 | tf_op jit(solution)/shard_map/ppermute | solution.py:75
  (178 other events, 2353.2 us)

commit v2 on v1

--- a/solution.py
+++ b/solution.py
@@ -4,6 +4,8 @@
 import jax.numpy as jnp
 import numpy as np
 from jax import lax
+from jax.experimental import pallas as pl
+from jax.experimental.pallas import tpu as pltpu
 from jax.sharding import PartitionSpec as P
 
 eps = 1e-05
@@ -26,6 +28,12 @@
         if cols % 2 == 0 or rows == 2:
             return [r * cols + c for r, c in walk]
     return list(range(rows * cols))
+
+
+def after(value, gate):
+    if gate is None:
+        return value
+    return lax.optimization_barrier((value, gate))[0]
 
 
 class Ring:
@@ -49,14 +57,14 @@
         near = self.size - 1 - far
         return (near, far) if flip else (far, near)
 
-    def gather(self, shard, flip):
+    def gather(self, shard, flip, gate_right=None, gate_left=None):
         hops_right, hops_left = self.hops(flip)
         slots = [shard] * self.size
-        moving = shard
+        moving = after(shard, gate_right)
         for k in range(1, hops_right + 1):
             moving = lax.ppermute(moving, ring_axes, self.right)
             slots[k] = moving
-        moving = shard
+        moving = after(shard, gate_left)
         for k in range(1, hops_left + 1):
             moving = lax.ppermute(moving, ring_axes, self.left)
             slots[self.size - k] = moving
@@ -111,22 +119,21 @@
         bit *= 2
 
 
-def share_sum(rows):
+def share_sum(keep, send, groups=1):
+    width = keep.shape[-1]
     for bit in bits_of("tp"):
-        count = lax.axis_size("tp") // bit
-        pairs = rows.reshape((count // 2, 2) + (-1,) + rows.shape[1:])
-        other = swap(pairs[:, 1].astype(bf16), "tp", bit)
-        rows = pairs[:, 0].astype(f32) + other.astype(f32)
-        rows = rows.reshape((-1,) + rows.shape[2:])
-    return rows
+        total = keep.astype(f32) + swap(send, "tp", bit).astype(f32)
+        if 2 * bit == lax.axis_size("tp"):
+            return total
+        halves = total.reshape(groups, 2, -1, width)
+        keep = halves[:, 0].reshape(-1, width)
+        send = halves[:, 1].reshape(-1, width).astype(bf16)
 
 
 def share_spread(rows):
     for bit in reversed(list(bits_of("tp"))):
-        rows = rows.reshape((-1, 1) + (lax.axis_size("tp") and rows.shape[-2:]))
-        rows = jnp.concatenate([rows, swap(rows, "tp", bit)], axis=1)
-        rows = rows.reshape((-1,) + rows.shape[2:])
-    return rows.reshape((-1,) + rows.shape[-1:])
+        rows = jnp.concatenate([rows, swap(rows, "tp", bit)], axis=0)
+    return rows
 
 
 def everyone_sum(values, axes):
@@ -157,6 +164,312 @@
     pulled = grad * gain
     term = pulled - jnp.mean(pulled, axis=-1, keepdims=True)
     return inv * (term - norm * jnp.mean(pulled * norm, axis=-1, keepdims=True))
+
+
+def params(megabytes):
+    return pltpu.CompilerParams(vmem_limit_bytes=megabytes << 20)
+
+
+def cost(flops, moved, heavy=0):
+    return pl.CostEstimate(flops=flops, bytes_accessed=moved, transcendentals=heavy)
+
+
+def arrange(values, gain, shift, ring, row_blocks):
+    rows, width = values.shape
+    blocks = row_blocks.shape[0]
+    pieces = ring.size
+    share = rows // blocks
+    piece = width // pieces
+    norm = gain is not None
+    moved = piece % 128 == 0
+    if not moved:
+        values = ring.into(values)
+        if norm:
+            gain, shift = ring.into(gain), ring.into(shift)
+
+    def source(slot_ref, k):
+        if not moved:
+            return slice(k * piece, (k + 1) * piece)
+        return pl.ds(pl.multiple_of(slot_ref[k] * piece, piece), piece)
+
+    def kernel(slot_ref, block_ref, *refs):
+        del block_ref
+        if norm:
+            in_ref, gain_ref, shift_ref, share_ref, act_ref, natural = refs
+        else:
+            in_ref, share_ref = refs
+        for k in range(pieces):
+            from_cols = source(slot_ref, k)
+            cols = slice(k * piece, (k + 1) * piece)
+            if norm:
+                @pl.when(pl.program_id(0) == 0)
+                def _(cols=cols, from_cols=from_cols):
+                    share_ref[:, cols] = in_ref[:, from_cols]
+            else:
+                share_ref[:, cols] = in_ref[:, from_cols]
+        if norm:
+            unit, _ = normed(in_ref[...].astype(f32))
+            natural[...] = (unit * gain_ref[...] + shift_ref[...]).astype(bf16)
+            for k in range(pieces):
+                from_cols = source(slot_ref, k)
+                act_ref[:, k * piece : (k + 1) * piece] = natural[:, from_cols]
+
+    row_in = pl.BlockSpec((share, width), lambda i, s, b: (b[i], 0))
+    row_out = pl.BlockSpec((share, width), lambda i, s, b: (i, 0))
+    first = pl.BlockSpec((share, width), lambda i, s, b: (0, 0))
+    line = pl.BlockSpec((1, width), lambda i, s, b: (0, 0))
+    full = jax.ShapeDtypeStruct((rows, width), bf16)
+    return pl.pallas_call(
+        kernel,
+        out_shape=(jax.ShapeDtypeStruct((share, width), bf16), full) if norm else full,
+        grid_spec=pltpu.PrefetchScalarGridSpec(
+            num_scalar_prefetch=2,
+            grid=(blocks,),
+            in_specs=[row_in, line, line] if norm else [row_in],
+            out_specs=(first, row_out) if norm else row_out,
+            scratch_shapes=[pltpu.VMEM((share, width), bf16)] if norm else [],
+        ),
+        compiler_params=params(24),
+        cost_estimate=cost(10 * rows * width, 4 * rows * width),
+    )(ring.slots, row_blocks, values, *((gain, shift) if norm else ()))
+
+
+def slot_list(chunks, axis):
+    if chunks[0].shape[axis] % 128 != 0:
+        return [jnp.concatenate(chunks, axis=axis)]
+    return chunks
+
+
+def chunk_sum(left, chunks, turned, tile, extras, finish, outs, megabytes=40):
+    chunks = slot_list(chunks, 1 if turned else 0)
+    rows, depth = left.shape
+    count = len(chunks)
+    piece = depth // count
+    columns = chunks[0].shape[0 if turned else 1]
+    tile = min(tile, columns)
+
+    def kernel(*refs):
+        left_ref = refs[0]
+        chunk_refs = refs[1 : 1 + count]
+        extra_refs = refs[1 + count : 1 + count + len(extras)]
+        out_refs = refs[1 + count + len(extras) :]
+        total = None
+        for k in range(count):
+            part = dot(left_ref[:, k * piece : (k + 1) * piece], chunk_refs[k][...], NT if turned else NN)
+            total = part if total is None else total + part
+        finish(total, extra_refs, out_refs)
+
+    if turned:
+        chunk_spec = pl.BlockSpec((tile, piece), lambda i: (i, 0))
+    else:
+        chunk_spec = pl.BlockSpec((piece, tile), lambda i: (0, i))
+    return pl.pallas_call(
+        kernel,
+        out_shape=tuple(jax.ShapeDtypeStruct((r, columns), d) for d, r in outs),
+        grid=(columns // tile,),
+        in_specs=[pl.BlockSpec((rows, depth), lambda i: (0, 0))]
+        + [chunk_spec] * count
+        + [pl.BlockSpec((r, tile), lambda i: (0, i)) for _, r in extras],
+        out_specs=tuple(pl.BlockSpec((r, tile), lambda i: (0, i)) for _, r in outs),
+        compiler_params=params(megabytes),
+        cost_estimate=cost(
+            2 * rows * depth * columns, 2 * (rows * depth + depth * columns) + 8 * rows * columns
+        ),
+    )(left, *chunks, *(a for a, _ in extras))
+
+
+def chunk_side(left, chunks, turned, megabytes=40):
+    chunks = slot_list(chunks, 0 if turned else 1)
+    rows, depth = left.shape
+    count = len(chunks)
+    piece = chunks[0].shape[0 if turned else 1]
+    block = (piece, depth) if turned else (depth, piece)
+    half = rows // 2
+
+    def kernel(*refs):
+        left_ref = refs[0]
+        chunk_refs = refs[1 : 1 + count]
+        keep_ref, send_ref, held, sems = refs[1 + count :]
+        def copy(k):
+            source = chunk_refs[k]
+            if chunk_refs[k].shape != block:
+                source = source.at[:, :depth] if turned else source.at[:depth, :]
+            return pltpu.make_async_copy(source, held.at[k], sems.at[k])
+        for k in range(count):
+            copy(k).start()
+        for k in range(count):
+            copy(k).wait()
+            part = dot(left_ref[...], held[k], NT if turned else NN).astype(bf16)
+            keep_ref[:, k * piece : (k + 1) * piece] = part[:half]
+            send_ref[:, k * piece : (k + 1) * piece] = part[half:]
+
+    shape = jax.ShapeDtypeStruct((half, piece * count), bf16)
+    return pl.pallas_call(
+        kernel,
+        out_shape=(shape, shape),
+        in_specs=[pl.BlockSpec(memory_space=pltpu.VMEM)]
+        + [pl.BlockSpec(memory_space=pl.ANY)] * count,
+        out_specs=(pl.BlockSpec(memory_space=pltpu.VMEM),) * 2,
+        scratch_shapes=[pltpu.VMEM((count,) + block, bf16), pltpu.SemaphoreType.DMA((count,))],
+        compiler_params=params(megabytes),
+        cost_estimate=cost(
+            2 * rows * depth * piece * count,
+            2 * (rows * depth + depth * piece * count + rows * piece * count),
+        ),
+    )(left, *chunks)
+
+
+def mask_of(info_ref, key_ref, keys):
+    own, one, two, place = (info_ref[i : i + 1, :] for i in range(4))
+    seg = key_ref[keys, 0:1]
+    spot = key_ref[keys, 1:2]
+    return ((seg == own) | (seg == one) | (seg == two)) & (spot <= place)
+
+
+def attend(qkv, kv_blocks, key_info, query_info, heads, head, scale, rows_at_once=256):
+    rows = qkv.shape[0]
+    count = len(kv_blocks)
+    span = kv_blocks[0].shape[0]
+    keys = span * count
+
+    def kernel(q_ref, *refs):
+        kv_refs = refs[:count]
+        key_ref, info_ref, out_ref, log_ref, turned, score, exps = refs[count:]
+
+        @pl.when(pl.program_id(0) == 0)
+        def _():
+            for d in range(count):
+                turned[:, d * span : (d + 1) * span] = kv_refs[d][:, head:].T
+
+        masks = [
+            mask_of(info_ref, key_ref, slice(d * span, (d + 1) * span)) for d in range(count)
+        ]
+        for h in range(heads):
+            query = q_ref[:, h * head : (h + 1) * head]
+            top = None
+            for d in range(count):
+                raw = dot(kv_refs[d][:, :head], query, NT) * scale
+                raw = jnp.where(masks[d], raw, masked_score)
+                score[d * span : (d + 1) * span, :] = raw
+                peak = jnp.max(raw, axis=0, keepdims=True)
+                top = peak if top is None else jnp.maximum(top, peak)
+            total = None
+            for d in range(count):
+                e = jnp.exp(score[d * span : (d + 1) * span, :] - top)
+                exps[d * span : (d + 1) * span, :] = e
+                summed = jnp.sum(e, axis=0, keepdims=True)
+                total = summed if total is None else total + summed
+            mixed = None
+            inverse = 1.0 / total
+            for d in range(count):
+                low = (exps[d * span : (d + 1) * span, :] * inverse).astype(bf16)
+                part = dot(turned[:, d * span : (d + 1) * span], low, NN)
+                mixed = part if mixed is None else mixed + part
+            out_ref[:, h * head : (h + 1) * head] = mixed.T.astype(bf16)
+            log_ref[h : h + 1, :] = top + jnp.log(total)
+
+    block = rows_at_once
+    return pl.pallas_call(
+        kernel,
+        out_shape=(
+            jax.ShapeDtypeStruct((rows, heads * head), bf16),
+            jax.ShapeDtypeStruct((8, rows), f32),
+        ),
+        grid=(rows // block,),
+        in_specs=[pl.BlockSpec((block, heads * head), lambda i: (i, 0))]
+        + [pl.BlockSpec((span, 2 * head), lambda i: (0, 0))] * count
+        + [
+            pl.BlockSpec((keys, 2), lambda i: (0, 0)),
+            pl.BlockSpec((8, block), lambda i: (0, i)),
+        ],
+        out_specs=(
+            pl.BlockSpec((block, heads * head), lambda i: (i, 0)),
+            pl.BlockSpec((8, block), lambda i: (0, i)),
+        ),
+        scratch_shapes=[
+            pltpu.VMEM((head, keys), bf16),
+            pltpu.VMEM((keys, block), f32),
+            pltpu.VMEM((keys, block), f32),
+        ],
+        compiler_params=params(40),
+        cost_estimate=cost(4 * rows * keys * heads * head, 4 * rows * heads * head, rows * keys * heads),
+    )(qkv, *kv_blocks, key_info, query_info)
+
+
+def attend_back(qkv, kv_blocks, key_info, query_info, logs, grad, heads, head, scale, rows_at_once=256):
+    rows = qkv.shape[0]
+    count = len(kv_blocks)
+    span = kv_blocks[0].shape[0]
+    keys = span * count
+
+    def kernel(q_ref, *refs):
+        kv_refs = refs[:count]
+        key_ref, info_ref, log_ref, grad_ref, dq_ref, dkv_ref, turned, probs, pulls = refs[count:]
+
+        @pl.when(pl.program_id(0) == 0)
+        def _():
+            for d in range(count):
+                turned[:, d * span : (d + 1) * span] = kv_refs[d][:, :head].T
+            dkv_ref[...] = jnp.zeros_like(dkv_ref)
+
+        masks = [
+            mask_of(info_ref, key_ref, slice(d * span, (d + 1) * span)) for d in range(count)
+        ]
+        for h in range(heads):
+            cols = slice(h * head, (h + 1) * head)
+            query = q_ref[:, cols]
+            pulled = grad_ref[:, cols]
+            log = log_ref[h : h + 1, :]
+            delta = None
+            for d in range(count):
+                at = slice(d * span, (d + 1) * span)
+                raw = dot(kv_refs[d][:, :head], query, NT) * scale
+                p = jnp.exp(jnp.where(masks[d], raw, masked_score) - log)
+                g = dot(kv_refs[d][:, head:], pulled, NT)
+                probs[at, :] = p
+                pulls[at, :] = g
+                part = jnp.sum(p * g, axis=0, keepdims=True)
+                delta = part if delta is None else delta + part
+                dkv_ref[at, head:] += dot(p.astype(bf16), pulled, NN)
+            mixed = None
+            for d in range(count):
+                at = slice(d * span, (d + 1) * span)
+                ds = (probs[at, :] * (pulls[at, :] - delta)).astype(bf16)
+                dkv_ref[at, :head] += dot(ds, query, NN) * scale
+                part = dot(turned[:, at], ds, NN)
+                mixed = part if mixed is None else mixed + part
+            dq_ref[:, cols] = (mixed * scale).T.astype(bf16)
+
+    block = rows_at_once
+    return pl.pallas_call(
+        kernel,
+        out_shape=(
+            jax.ShapeDtypeStruct((rows, heads * head), bf16),
+            jax.ShapeDtypeStruct((keys, 2 * head), f32),
+        ),
+        grid=(rows // block,),
+        in_specs=[pl.BlockSpec((block, heads * head), lambda i: (i, 0))]
+        + [pl.BlockSpec((span, 2 * head), lambda i: (0, 0))] * count
+        + [
+            pl.BlockSpec((keys, 2), lambda i: (0, 0)),
+            pl.BlockSpec((8, block), lambda i: (0, i)),
+            pl.BlockSpec((8, block), lambda i: (0, i)),
+            pl.BlockSpec((block, heads * head), lambda i: (i, 0)),
+        ],
+        out_specs=(
+            pl.BlockSpec((block, heads * head), lambda i: (i, 0)),
+            pl.BlockSpec((keys, 2 * head), lambda i: (0, 0)),
+        ),
+        scratch_shapes=[
+            pltpu.VMEM((head, keys), bf16),
+            pltpu.VMEM((keys, block), f32),
+            pltpu.VMEM((keys, block), f32),
+        ],
+        compiler_params=params(44),
+        cost_estimate=cost(
+            10 * rows * keys * heads * head, 8 * keys * head + 6 * rows * heads * head, rows * keys * heads
+        ),
+    )(qkv, *kv_blocks, key_info, query_info, logs, grad)
 
 
 def parent_lookup(seg_ids, parents):
@@ -213,10 +526,14 @@
 
     qkv_slots = ring.gather(jnp.concatenate([q_weight, kv_weight], axis=1), False)
     o_slots = ring.gather(o_weight, True)
-    up_slots = ring.gather(up_weight, False)
-    down_slots = ring.gather(down_weight, True)
-
-    row_blocks = [tp_index ^ j for j in range(tp_count)]
+    half = n // 2
+    up_slots = ring.gather(up_weight, False, o_slots[half - 1], o_slots[half])
+    down_slots = ring.gather(down_weight, True, up_slots[2 % n], up_slots[(n - 2) % n])
+
+    masks = [0]
+    for bit in reversed(list(bits_of("tp"))):
+        masks = masks + [m ^ bit for m in masks]
+    row_blocks = [tp_index ^ m for m in masks]
 
     def rows_in(values):
         return jnp.concatenate(
@@ -227,12 +544,15 @@
             axis=0,
         )
 
-    x_low = ring.into(rows_in(tokens))
-    g_low = ring.into(rows_in(out_grad))
+    row_ids = jnp.stack(row_blocks)
+    x_low_share, act_one = arrange(
+        tokens, ln1_gain.astype(f32)[None], ln1_bias.astype(f32)[None], ring, row_ids
+    )
+    g_low = arrange(out_grad, None, None, ring, row_ids)
     vectors = ring.into(
-        jnp.stack([ln1_gain, ln1_bias, o_bias, ln2_gain, ln2_bias, down_bias])
-    ).astype(f32)
-    gain_one, shift_one, o_shift, gain_two, shift_two, down_shift = (
+        jnp.stack([ln1_gain, ln1_bias, o_bias, ln2_gain, ln2_bias, down_bias]).astype(f32)
+    )
+    gain_one, _, o_shift, gain_two, shift_two, down_shift = (
         vectors[i : i + 1] for i in range(6)
     )
     own_place = rows_in(jnp.arange(row_count, dtype=jnp.int32))
@@ -256,72 +576,75 @@
     )
     seg_one = parent_lookup(own_seg, parents)
     seg_two = parent_lookup(seg_one, parents)
-    allowed = (
-        (key_segment[None, :] == own_seg[:, None])
-        | (key_segment[None, :] == seg_one[:, None])
-        | (key_segment[None, :] == seg_two[:, None])
-    ) & (key_place[None, :] <= query_place[:, None])
-
-    norm_one, inv_one = normed(x_low.astype(f32))
-    act_one = (norm_one * gain_one + shift_one).astype(bf16)
-    qkv_full = jnp.concatenate(qkv_slots, axis=0)
+    key_info = jnp.stack([key_segment, key_place], axis=1)
+    blank = jnp.zeros_like(own_seg)
+    query_info = jnp.stack([own_seg, seg_one, seg_two, query_place, blank, blank, blank, blank])
+
     qkv_shift = jnp.concatenate(
         [q_bias.astype(f32), jnp.zeros((head_size,), f32), value_bias.astype(f32)]
     )
-    qkv = (dot(act_one, qkv_full, NN) + qkv_shift).astype(bf16)
-    queries = qkv[:, :local_width]
+
+    def add_shift(total, extra, out):
+        out[0][...] = (total + extra[0][...]).astype(bf16)
+
+    (qkv,) = chunk_sum(
+        act_one, qkv_slots, False, 256, [(qkv_shift[None], 1)], add_shift, [(bf16, row_count)]
+    )
     kv_own = qkv[:, local_width:]
-    kv_rows = jnp.concatenate(
-        [kv_own]
-        + [
-            lax.ppermute(kv_own, "ctx", [(c, c + d) for c in range(ctx_count - d)])
-            for d in range(1, ctx_count)
-        ],
-        axis=0,
-    )
-    keys_all = kv_rows[:, :head_size]
-    values_all = kv_rows[:, head_size:]
-
-    def scores_of(h):
-        raw = dot(queries[:, h * head_size : (h + 1) * head_size], keys_all, NT) * score_scale
-        return jnp.where(allowed, raw, masked_score)
-
-    mixed, logs = [], []
-    for h in range(local_heads):
-        scores = scores_of(h)
-        row_max = jnp.max(scores, axis=1, keepdims=True)
-        exp_scores = jnp.exp(scores - row_max)
-        row_total = jnp.sum(exp_scores, axis=1, keepdims=True)
-        probs_low = (exp_scores / row_total).astype(bf16)
-        mixed.append(dot(probs_low, values_all, NN).astype(bf16))
-        logs.append(row_max + jnp.log(row_total))
-    attended = jnp.concatenate(mixed, axis=1)
-
-    o_full = jnp.concatenate(o_slots, axis=1)
-    attn_share = share_sum(dot(attended, o_full, NN).astype(bf16))
-    x_share = x_low[:share_rows].astype(f32)
+    kv_blocks = [kv_own] + [
+        lax.ppermute(kv_own, "ctx", [(c, c + d) for c in range(ctx_count - d)])
+        for d in range(1, ctx_count)
+    ]
+    attended, logs = attend(
+        qkv, kv_blocks, key_info, query_info, local_heads, head_size, score_scale
+    )
+    attn_share = share_sum(*chunk_side(attended, o_slots, False))
+    x_share = x_low_share.astype(f32)
     residual = x_share + (attn_share + o_shift)
     norm_two, inv_two = normed(residual)
     act_two = share_spread((norm_two * gain_two + shift_two).astype(bf16))
 
-    up_full = jnp.concatenate(up_slots, axis=0)
-    pre_act = dot(act_two, up_full, NN) + up_bias.astype(f32)
-    gelu_out, gelu_slope = gelu_parts(pre_act)
-    hidden = gelu_out.astype(bf16)
+
+    def activate(total, extra, out):
+        gelu_out, gelu_slope = gelu_parts(total + extra[0][...])
+        out[0][...] = gelu_out.astype(bf16)
+        out[1][...] = gelu_slope
+
+    hidden, gelu_slope = chunk_sum(
+        act_two,
+        up_slots,
+        False,
+        256,
+        [(up_bias.astype(f32)[None], 1)],
+        activate,
+        [(bf16, row_count), (f32, row_count)],
+    )
     down_w_grad = ring.scatter(
         lambda k: dot(hidden, g_low[:, k * piece : (k + 1) * piece], TN), False
     )
-    down_full = jnp.concatenate(down_slots, axis=1)
-    grad_hidden = dot(g_low, down_full, NT)
-    grad_pre = (grad_hidden * gelu_slope).astype(bf16)
+
+    def deactivate(total, extra, out):
+        low = (total * extra[0][...]).astype(bf16)
+        out[0][...] = low
+        out[1][...] = jnp.sum(low.astype(f32), axis=0, keepdims=True)
+
+    grad_pre, up_bias_grad = chunk_sum(
+        g_low,
+        down_slots,
+        True,
+        256,
+        [(gelu_slope, row_count)],
+        deactivate,
+        [(bf16, row_count), (f32, 1)],
+    )
+    up_bias_grad = up_bias_grad[0]
     up_w_grad = ring.scatter(
         lambda k: dot(act_two[:, k * piece : (k + 1) * piece], grad_pre, TN), True
     )
-    grad_two = share_sum(dot(grad_pre, up_full, NT).astype(bf16))
-    ffn_share = share_sum(dot(hidden, down_full, NN).astype(bf16))
+    grad_two = share_sum(*chunk_side(grad_pre, up_slots, True))
+    ffn_share = share_sum(*chunk_side(hidden, down_slots, False))
     layer_out = ring.back((residual + (ffn_share + down_shift)).astype(bf16))
 
-    up_bias_grad = jnp.sum(grad_pre.astype(f32), axis=0)
     g_share = g_low[:share_rows].astype(f32)
     grad_res = g_share + normed_back(grad_two, gain_two, norm_two, inv_two)
     grad_attn_share = grad_res.astype(bf16)
@@ -329,7 +652,13 @@
     out_w_grad = ring.scatter(
         lambda k: dot(attended, grad_attn[:, k * piece : (k + 1) * piece], TN), False
     )
-    grad_attended = dot(grad_attn, o_full, NT).astype(bf16)
+
+    def only_round(total, extra, out):
+        out[0][...] = total.astype(bf16)
+
+    (grad_attended,) = chunk_sum(
+        grad_attn, o_slots, True, 256, [], only_round, [(bf16, row_count)]
+    )
     early = jnp.stack(
         [
             jnp.sum(g_share, axis=0),
@@ -338,30 +667,20 @@
             jnp.sum(grad_two, axis=0),
         ]
     )
-    early = everyone_sum(ring.back(early), ("tp", "ctx", "fsdp"))
-    up_bias_out = everyone_sum(up_bias_grad, ("ctx", "fsdp"))
-
-    key_grad = jnp.zeros((tree_length, head_size), f32)
-    value_grad = jnp.zeros((tree_length, head_size), f32)
-    query_grads = []
-    for h in range(local_heads):
-        cols = slice(h * head_size, (h + 1) * head_size)
-        attn_probs = jnp.exp(scores_of(h) - logs[h])
-        probs_low = attn_probs.astype(bf16)
-        grad_head = grad_attended[:, cols]
-        grad_probs = dot(grad_head, values_all, NT)
-        row_delta = jnp.sum(attn_probs * grad_probs, axis=1, keepdims=True)
-        grad_scores = (attn_probs * (grad_probs - row_delta)).astype(bf16)
-        query_grads.append((dot(grad_scores, keys_all, NN) * score_scale).astype(bf16))
-        key_grad = key_grad + dot(grad_scores, queries[:, cols], TN) * score_scale
-        value_grad = value_grad + dot(probs_low, grad_head, TN)
-    grad_query = jnp.concatenate(query_grads, axis=1)
+    early = everyone_sum(ring.back(early).reshape(-1), ("tp",))
+
+    grad_query, kv_grad = attend_back(
+        qkv, kv_blocks, key_info, query_info, logs, grad_attended,
+        local_heads, head_size, score_scale,
+    )
     q_bias_grad = jnp.sum(grad_query.astype(f32), axis=0)
 
-    kv_part = jnp.concatenate([key_grad, value_grad], axis=1).astype(bf16)
-    kv_part = kv_part.reshape(ctx_count, tp_count, share_rows, 2 * head_size)
-    kv_part = jnp.swapaxes(kv_part, 0, 1).reshape(tp_count * ctx_count * share_rows, -1)
-    kv_part = share_sum(kv_part).reshape(ctx_count, share_rows, 2 * head_size)
+    kv_part = kv_grad.astype(bf16).reshape(ctx_count, 2, row_count // 2, 2 * head_size)
+    kv_part = share_sum(
+        kv_part[:, 0].reshape(-1, 2 * head_size),
+        kv_part[:, 1].reshape(-1, 2 * head_size),
+        ctx_count,
+    ).reshape(ctx_count, share_rows, 2 * head_size)
     kv_sum = kv_part[0]
     for d in range(1, ctx_count):
         kv_sum = kv_sum + lax.ppermute(
@@ -371,27 +690,25 @@
     kv_low = share_spread(kv_low_share)
 
     sub = piece // tp_count
-    kv_cols = act_one.reshape(row_count, n, tp_count, sub)
-    kv_cols = lax.dynamic_slice_in_dim(kv_cols, tp_index, 1, 2).reshape(row_count, n * sub)
 
     def q_kv_part(k):
-        q_piece = dot(act_one[:, k * piece : (k + 1) * piece], grad_query, TN)
-        kv_piece = dot(kv_cols[:, k * sub : (k + 1) * sub], kv_low, TN)
-        return jnp.concatenate([q_piece.reshape(-1), kv_piece.reshape(-1)]).reshape(
-            -1, local_width
-        )
+        act_piece = act_one[:, k * piece : (k + 1) * piece]
+        q_piece = dot(act_piece, grad_query, TN)
+        kv_piece = lax.dynamic_slice_in_dim(dot(act_piece, kv_low, TN), tp_index * sub, sub, 0)
+        kv_piece = jnp.concatenate([kv_piece[: sub // 2], kv_piece[sub // 2 :]], axis=1)
+        return jnp.concatenate([q_piece, kv_piece], axis=0)
 
     q_kv = ring.scatter(q_kv_part, True)
     q_w_grad = q_kv[:piece]
-    kv_w_grad = q_kv[piece:].reshape(sub, 2 * head_size)
-
-    q_full = qkv_full[:, :local_width]
-    kv_full = qkv_full[:, local_width:]
-    grad_act = share_sum(dot(grad_query, q_full, NT).astype(bf16)) + dot(
+    kv_w_grad = jnp.concatenate(
+        [q_kv[piece:, : 2 * head_size], q_kv[piece:, 2 * head_size :]], axis=0
+    )
+
+    kv_full = jnp.concatenate([c[:, local_width:] for c in qkv_slots], axis=0)
+    grad_act = share_sum(*chunk_side(grad_query, qkv_slots, True)) + dot(
         kv_low_share, kv_full, NT
     )
-    norm_share = norm_one[:share_rows]
-    inv_share = inv_one[:share_rows]
+    norm_share, inv_share = normed(x_share)
     input_grad = ring.back(
         (grad_res + normed_back(grad_act, gain_one, norm_share, inv_share)).astype(bf16)
     )
@@ -399,16 +716,23 @@
     late = ring.back(late).reshape(-1)
     value_bias_grad = jnp.sum(kv_low_share[:, head_size:].astype(f32), axis=0)
     late = everyone_sum(jnp.concatenate([late, value_bias_grad]), ("tp",))
-    late = everyone_sum(jnp.concatenate([late, q_bias_grad]), ("ctx", "fsdp"))
+    sums = [late, early, q_bias_grad, up_bias_grad]
+    cuts = np.cumsum([v.shape[0] for v in sums])
+    sums = everyone_sum(jnp.concatenate(sums), ("ctx", "fsdp"))
+    late, early, q_bias_out, up_bias_out = (
+        sums[stop - v.shape[0] : stop]
+        for stop, v in zip(cuts, (late, early, q_bias_grad, up_bias_grad))
+    )
+    early = early.reshape(4, width)
     return (
         layer_out,
         input_grad,
         late[:width],
         late[width : 2 * width],
         q_w_grad,
-        late[2 * width + head_size :],
+        q_bias_out,
         kv_w_grad,
-        late[2 * width : 2 * width + head_size],
+        late[2 * width :],
         out_w_grad,
         early[1],
         early[2],

time: 714 us -> 564 us (0.79)
  Pallas kernels: 0 us -> 88.4 us
  matrix products: 118 us -> 30.2 us
  local copies, waits for them, and re-layouts: 118 us -> 42 us
  other arithmetic: 56.7 us -> 19.2 us
  starting transfers between devices: 128 us -> 102 us
  between operations: 25.8 us -> 13.3 us
    ppermute x14, waiting for transfers between devices: 19.7 us -> 114 us  [gather(): moving = lax.ppermute(moving, ring_axes, self.right)]
    pallas_call x0 -> x12, Pallas kernels: none -> 88.4 us  [the longest x4 31.6 us: chunk_side(): pl.pallas_call(kernel, out_shape=(shape, shape), in_specs=[pl.BlockSpec(m...]
    dot_general x73 -> x41, matrix products: 118 us -> 30.2 us  [dot(): lax.dot_general(left, right, (dims, ((), ())), preferred_element_type=f32)]
    ppermute x14, waiting for transfers between devices: 91 us -> 14.4 us  [gather(): moving = lax.ppermute(moving, ring_axes, self.left)]
    ppermute x29 -> x23, waiting for transfers between devices: 96.6 us -> 30.9 us  [swap(): return lax.ppermute(values, axis, [(i, i ^ bit) for i in range(count)])]
    ppermute x28, waiting for transfers between devices: 44.8 us -> 96.2 us  [scatter(): moving = lax.ppermute(piece.astype(bf16), ring_axes, pairs)]
    unnamed x314 -> x186, local copies, waits for them, and re-layouts: 65.9 us -> 28.1 us
    ppermute x14, starting transfers between devices: 51.8 us -> 28 us  [gather(): moving = lax.ppermute(moving, ring_axes, self.right)]
  transfers between devices with their start and end apart: 91 -> 85, of which waited for: 37 -> 41; matrix products, arithmetic and copies ran while one was open for 32% -> 12% of each run, Pallas kernels for 0% -> 15%
where the time goes in v2:
time: 564 us; the launch traced here: 559 us
  waiting for transfers between devices  264 us (47%)
  starting transfers between devices  102 us (18%)
  Pallas kernels  88.4 us (16%)
  local copies, waits for them, and re-layouts  42 us (7%)
  matrix products  30.2 us (5%)
  other arithmetic  19.2 us (3%)
  between operations  13.3 us (2%)
    ppermute x14, waiting for transfers between devices, gather(): moving = lax.ppermute(moving, ring_axes, self.right)  114 us
    ppermute x28, waiting for transfers between devices, scatter(): moving = lax.ppermute(piece.astype(bf16), ring_axes, pairs)  96.2 us
    ppermute x28, starting transfers between devices, scatter(): moving = lax.ppermute(piece.astype(bf16), ring_axes, pairs)  35.3 us
    pallas_call x4, Pallas kernels, chunk_side(): pl.pallas_call(kernel, out_shape=(shape, shape), in_specs=[pl.BlockSpec(m...  31.6 us
    ppermute x23, waiting for transfers between devices, swap(): return lax.ppermute(values, axis, [(i, i ^ bit) for i in range(count)])  30.9 us
    dot_general x41, matrix products, dot(): lax.dot_general(left, right, (dims, ((), ())), preferred_element_type=f32)  30.2 us
    unnamed x186, local copies, waits for them, and re-layouts  28.1 us
    ppermute x14, starting transfers between devices, gather(): moving = lax.ppermute(moving, ring_axes, self.right)  28 us
  transfers between devices with their start and end apart: 85, of which 41 were waited for; matrix products, arithmetic and copies ran while one was open for 12% of the time, Pallas kernels for 15%

profile of v2, /device:TPU:0, one launch (start us, length us, event | category | flops | bytes accessed | tf_op | source)
XLA Modules:
  0.0 558.6 jit_solution(5994114791083491439)
XLA Ops:
  21.1 8.2 %collective-permute-done.1.refs_3_ = bf16[256,768]{1,0:T(8,128)(2,1)S(1)} collective-permute-done((bf16[256,768]{1,0:T(8,128)(2,1)S(1)}, bf16[256,768]{1,0:T(8,128)(2,1)S(1)}, u32[]{:S(2)}, u32[]{:S(2)}) %collective-permute-start.1) | collective-permute-done | bytes 393248 | tf_op jit(solution)/shard_map/ppermute | solution.py:65
  33.9 5.7 %collective-permute-done.2.refs_4_ = bf16[256,768]{1,0:T(8,128)(2,1)S(1)} collective-permute-done((bf16[256,768]{1,0:T(8,128)(2,1)S(1)}, bf16[256,768]{1,0:T(8,128)(2,1)S(1)}, u32[]{:S(2)}, u32[]{:S(2)}) %collective-permute-start.2) | collective-permute-done | bytes 393248 | tf_op jit(solution)/shard_map/ppermute | solution.py:65
  75.9 12.7 %shard_map.326 = (bf16[512,512]{1,0:T(8,128)(2,1)S(1)}, f32[8,512]{1,0:T(8,128)S(1)}) custom-call(bf16[512,768]{1,0:T(8,128)(2,1)S(1)} %shard_map.325.q_ref, bf16[512,256]{1,0:T(8,128)(2,1)} %slice.483.refs_0_, bf16[512,256]{1,0:T(8,128)(2,1)} %collective-permute-done.7.refs_1_, bf16[512,256]{1,0:T(8,128)(2,1)} %collective-permute-done.8.refs_2_, ...), custom_call_target="tpu_custom_call" | custom-call | flops 2147483648 | bytes 1048576 | tf_op jit(solution)/shard_map/pallas_call | solution.py:372
  103.7 7.0 %collective-permute-start.21 = (bf16[256,2048]{1,0:T(8,128)(2,1)}, bf16[256,2048]{1,0:T(8,128)(2,1)S(1)}, u32[]{:S(2)}, u32[]{:S(2)}) collective-permute-start(bf16[256,2048]{1,0:T(8,128)(2,1)} %refs_1_.10), channel_id=1, source_target_pairs={{0,4},{4,8},{8,12},{12,28},{28,24},{24,20},{20,16},{16,0},{1,5},{5... | collective-permute-start | bytes 3145736 | tf_op jit(solution)/shard_map/ppermute | solution.py:65
  114.3 19.8 %collective-permute-done.21.refs_2_ = bf16[256,2048]{1,0:T(8,128)(2,1)S(1)} collective-permute-done((bf16[256,2048]{1,0:T(8,128)(2,1)}, bf16[256,2048]{1,0:T(8,128)(2,1)S(1)}, u32[]{:S(2)}, u32[]{:S(2)}) %collective-permute-start.21) | collective-permute-done | bytes 1048608 | tf_op jit(solution)/shard_map/ppermute | solution.py:65
  139.3 20.2 %collective-permute-done.22.refs_3_ = bf16[256,2048]{1,0:T(8,128)(2,1)S(1)} collective-permute-done((bf16[256,2048]{1,0:T(8,128)(2,1)S(1)}, bf16[256,2048]{1,0:T(8,128)(2,1)S(1)}, u32[]{:S(2)}, u32[]{:S(2)}) %collective-permute-start.22) | collective-permute-done | bytes 1048608 | tf_op jit(solution)/shard_map/ppermute | solution.py:65
  165.7 18.5 %collective-permute-done.23.refs_4_ = bf16[256,2048]{1,0:T(8,128)(2,1)} collective-permute-done((bf16[256,2048]{1,0:T(8,128)(2,1)S(1)}, bf16[256,2048]{1,0:T(8,128)(2,1)}, u32[]{:S(2)}, u32[]{:S(2)}) %collective-permute-start.23) | collective-permute-done | bytes 1048608 | tf_op jit(solution)/shard_map/ppermute | solution.py:65
  198.2 13.1 %collective-permute-done.27.refs_6_ = bf16[256,2048]{1,0:T(8,128)(2,1)} collective-permute-done((bf16[256,2048]{1,0:T(8,128)(2,1)}, bf16[256,2048]{1,0:T(8,128)(2,1)}, u32[]{:S(2)}, u32[]{:S(2)}) %collective-permute-start.27) | collective-permute-done | bytes 1048608 | tf_op jit(solution)/shard_map/ppermute | solution.py:69
  211.3 10.9 %shard_map.328 = (bf16[512,2048]{1,0:T(8,128)(2,1)S(1)}, f32[512,2048]{1,0:T(8,128)}) custom-call(bf16[512,2048]{1,0:T(8,128)(2,1)S(1)} %pad_maximum_fusion.refs_0_, bf16[256,2048]{1,0:T(8,128)(2,1)S(1)} %copy-done.31, bf16[256,2048]{1,0:T(8,128)(2,1)S(1)} %copy-done.33, bf16[256,2048]{1,0:T(8,128)(2,1)S(1)} %copy-done.38, ...), custom_call_target="tpu_custom_call" | custom-call | flops 4294967296 | bytes 18874368 | tf_op jit(solution)/shard_map/pallas_call | solution.py:266
  227.8 5.4 collective-permute-done.28.refs_2_
  235.3 20.8 %collective-permute-done.82 = bf16[2048,256]{1,0:T(8,128)(2,1)S(1)} collective-permute-done((bf16[2048,256]{1,0:T(8,128)(2,1)S(1)}, bf16[2048,256]{1,0:T(8,128)(2,1)S(1)}, u32[]{:S(2)}, u32[]{:S(2)}) %collective-permute-start.82) | collective-permute-done | bytes 1048608 | tf_op jit(solution)/shard_map/ppermute | solution.py:83
  260.7 17.4 %collective-permute-done.29.refs_3_ = bf16[2048,256]{1,0:T(8,128)(2,1)S(1)} collective-permute-done((bf16[2048,256]{1,0:T(8,128)(2,1)S(1)}, bf16[2048,256]{1,0:T(8,128)(2,1)S(1)}, u32[]{:S(2)}, u32[]{:S(2)}) %collective-permute-start.29) | collective-permute-done | bytes 1048608 | tf_op jit(solution)/shard_map/ppermute | solution.py:65
  280.2 20.8 %collective-permute-done.83 = bf16[2048,256]{1,0:T(8,128)(2,1)S(1)} collective-permute-done((bf16[2048,256]{1,0:T(8,128)(2,1)S(1)}, bf16[2048,256]{1,0:T(8,128)(2,1)S(1)}, u32[]{:S(2)}, u32[]{:S(2)}) %collective-permute-start.83) | collective-permute-done | bytes 1048608 | tf_op jit(solution)/shard_map/ppermute | solution.py:83
  306.9 16.1 %collective-permute-done.30.refs_4_ = bf16[2048,256]{1,0:T(8,128)(2,1)S(1)} collective-permute-done((bf16[2048,256]{1,0:T(8,128)(2,1)S(1)}, bf16[2048,256]{1,0:T(8,128)(2,1)S(1)}, u32[]{:S(2)}, u32[]{:S(2)}) %collective-permute-start.30) | collective-permute-done | bytes 1048608 | tf_op jit(solution)/shard_map/ppermute | solution.py:65
  323.5 9.0 %shard_map.331 = (bf16[512,2048]{1,0:T(8,128)(2,1)S(1)}, f32[1,2048]{1,0:T(1,128)S(1)}) custom-call(bf16[512,2048]{1,0:T(8,128)(2,1)S(1)} %shard_map.330.refs_0_, bf16[2048,256]{1,0:T(8,128)(2,1)} %refs_1_.9, bf16[2048,256]{1,0:T(8,128)(2,1)S(1)} %collective-permute-done.28.refs_2_, bf16[2048,256]{1,0:T(8,128)(2,1)S(1)} %collective-permute-done.29.refs_3_, ...), custom_call_target="tpu_custom_call" | custom-call | flops 4294967296 | bytes 18874368 | tf_op jit(solution)/shard_map/pallas_call | solution.py:266
  335.0 11.5 %shard_map.332 = (bf16[256,2048]{1,0:T(8,128)(2,1)S(1)}, bf16[256,2048]{1,0:T(8,128)(2,1)}) custom-call(bf16[512,2048]{1,0:T(8,128)(2,1)S(1)} %get-tuple-element.51.refs_0_, bf16[256,2048]{1,0:T(8,128)(2,1)S(1)} %copy-done.31, bf16[256,2048]{1,0:T(8,128)(2,1)S(1)} %copy-done.33, bf16[256,2048]{1,0:T(8,128)(2,1)S(1)} %copy-done.39, ...), custom_call_target="tpu_custom_call" | custom-call | flops 4294967296 | bytes 12582912 | tf_op jit(solution)/shard_map/pallas_call | solution.py:307
  352.7 11.1 %shard_map.329 = (bf16[256,2048]{1,0:T(8,128)(2,1)S(1)}, bf16[256,2048]{1,0:T(8,128)(2,1)S(1)}) custom-call(bf16[512,2048]{1,0:T(8,128)(2,1)S(1)} %get-tuple-element.45.refs_0_, bf16[2048,256]{1,0:T(8,128)(2,1)} %refs_1_.9, bf16[2048,256]{1,0:T(8,128)(2,1)S(1)} %copy-done.41, bf16[2048,256]{1,0:T(8,128)(2,1)S(1)} %copy-done.46, ...), custom_call_target="tpu_custom_call" | custom-call | flops 4294967296 | bytes 12582912 | tf_op jit(solution)/shard_map/pallas_call | solution.py:307
  375.8 14.7 %collective-permute-done.74 = bf16[256,2048]{1,0:T(8,128)(2,1)S(1)} collective-permute-done((bf16[256,2048]{1,0:T(8,128)(2,1)S(1)}, bf16[256,2048]{1,0:T(8,128)(2,1)S(1)}, u32[]{:S(2)}, u32[]{:S(2)}) %collective-permute-start.74) | collective-permute-done | bytes 1048608 | tf_op jit(solution)/shard_map/ppermute | solution.py:83
  397.3 6.4 %collective-permute-done.36 = bf16[128,2048]{1,0:T(8,128)(2,1)S(1)} collective-permute-done((bf16[128,2048]{1,0:T(8,128)(2,1)S(1)}, bf16[128,2048]{1,0:T(8,128)(2,1)S(1)}, u32[]{:S(2)}, u32[]{:S(2)}) %collective-permute-start.36) | collective-permute-done | bytes 524320 | tf_op jit(solution)/shard_map/ppermute | solution.py:111
  410.0 7.4 %collective-permute-done.75 = bf16[256,2048]{1,0:T(8,128)(2,1)S(1)} collective-permute-done((bf16[256,2048]{1,0:T(8,128)(2,1)S(1)}, bf16[256,2048]{1,0:T(8,128)(2,1)S(1)}, u32[]{:S(2)}, u32[]{:S(2)}) %collective-permute-start.75) | collective-permute-done | bytes 1048608 | tf_op jit(solution)/shard_map/ppermute | solution.py:83
  426.9 11.0 %collective-permute-done.72 = bf16[256,2048]{1,0:T(8,128)(2,1)S(1)} collective-permute-done((bf16[256,2048]{1,0:T(8,128)(2,1)S(1)}, bf16[256,2048]{1,0:T(8,128)(2,1)S(1)}, u32[]{:S(2)}, u32[]{:S(2)}) %collective-permute-start.72) | collective-permute-done | bytes 1048608 | tf_op jit(solution)/shard_map/ppermute | solution.py:83
  449.4 15.3 %shard_map.334 = (bf16[512,512]{1,0:T(8,128)(2,1)S(1)}, f32[2048,256]{1,0:T(8,128)S(1)}) custom-call(bf16[512,768]{1,0:T(8,128)(2,1)S(1)} %shard_map.325.q_ref, bf16[512,256]{1,0:T(8,128)(2,1)} %slice.483.refs_0_, bf16[512,256]{1,0:T(8,128)(2,1)} %collective-permute-done.7.refs_1_, bf16[512,256]{1,0:T(8,128)(2,1)} %collective-permute-done.8.refs_2_, ...), custom_call_target="tpu_custom_call" | custom-call | flops 5368709120 | bytes 3670016 | tf_op jit(solution)/shard_map/pallas_call | solution.py:444
  479.8 5.2 collective-permute-done.68
  544.3 5.5 collective-permute-done.53
  (523 shorter events, 251.8 us)
Async XLA Ops:
  6.2 40.5 %collective-permute-start.10 = (bf16[512,256]{1,0:T(8,128)(2,1)}, bf16[512,256]{1,0:T(8,128)(2,1)}, u32[]{:S(2)}, u32[]{:S(2)}) collective-permute-start(bf16[512,256]{1,0:T(8,128)(2,1)} %refs_1_.11), channel_id=1, source_target_pairs={{0,4},{4,8},{8,12},{12,28},{28,24},{24,20},{20,16},{16,0},{1,5},{5... | collective-permute-start | bytes 786440 | tf_op jit(solution)/shard_map/ppermute | solution.py:65
  8.2 33.5 %collective-permute-start.13 = (bf16[512,256]{1,0:T(8,128)(2,1)}, bf16[512,256]{1,0:T(8,128)(2,1)S(1)}, u32[]{:S(2)}, u32[]{:S(2)}) collective-permute-start(bf16[512,256]{1,0:T(8,128)(2,1)} %refs_1_.11), channel_id=1, source_target_pairs={{4,0},{8,4},{12,8},{28,12},{24,28},{20,24},{16,20},{0,16},{5,1},{9... | collective-permute-start | bytes 786440 | tf_op jit(solution)/shard_map/ppermute | solution.py:69
  103.7 30.4 %collective-permute-start.21 = (bf16[256,2048]{1,0:T(8,128)(2,1)}, bf16[256,2048]{1,0:T(8,128)(2,1)S(1)}, u32[]{:S(2)}, u32[]{:S(2)}) collective-permute-start(bf16[256,2048]{1,0:T(8,128)(2,1)} %refs_1_.10), channel_id=1, source_target_pairs={{0,4},{4,8},{8,12},{12,28},{28,24},{24,20},{20,16},{16,0},{1,5},{5... | collective-permute-start | bytes 3145736 | tf_op jit(solution)/shard_map/ppermute | solution.py:65
  162.4 33.8 %collective-permute-start.31 = (bf16[2048,256]{1,0:T(8,128)(2,1)}, bf16[2048,256]{1,0:T(8,128)(2,1)}, u32[]{:S(2)}, u32[]{:S(2)}) collective-permute-start(bf16[2048,256]{1,0:T(8,128)(2,1)} %refs_1_.9), channel_id=1, source_target_pairs={{4,0},{8,4},{12,8},{28,12},{24,28},{20,24},{16,20},{0,16},{5,1},{9... | collective-permute-start | bytes 3145736 | tf_op jit(solution)/shard_map/ppermute | solution.py:69
  163.8 33.0 %collective-permute-start.20 = (bf16[256,2048]{1,0:T(8,128)(2,1)}, bf16[256,2048]{1,0:T(8,128)(2,1)}, u32[]{:S(2)}, u32[]{:S(2)}) collective-permute-start(bf16[256,2048]{1,0:T(8,128)(2,1)} %pad_maximum_fusion.2), channel_id=1, source_target_pairs={{0,1},{1,0},{2,3},{3,2},{4,5},{5,4},{6,7},{7,6},{8,9},{9,8},{10,11... | collective-permute-start | bytes 3145736 | tf_op jit(solution)/shard_map/ppermute | solution.py:111
  163.8 47.4 %collective-permute-start.27 = (bf16[256,2048]{1,0:T(8,128)(2,1)}, bf16[256,2048]{1,0:T(8,128)(2,1)}, u32[]{:S(2)}, u32[]{:S(2)}) collective-permute-start(bf16[256,2048]{1,0:T(8,128)(2,1)} %collective-permute-done.26.refs_7_), channel_id=1, source_target_pairs={{4,0},{8,4},{12,8},{28,12},{24,28},{20,24},{16,20},{0,16},{5,1},{9... | collective-permute-start | bytes 3145736 | tf_op jit(solution)/shard_map/ppermute | solution.py:69
  184.2 27.0 %collective-permute-start.24 = (bf16[256,2048]{1,0:T(8,128)(2,1)}, bf16[256,2048]{1,0:T(8,128)(2,1)}, u32[]{:S(2)}, u32[]{:S(2)}) collective-permute-start(bf16[256,2048]{1,0:T(8,128)(2,1)} %collective-permute-done.23.refs_4_), channel_id=1, source_target_pairs={{0,4},{4,8},{8,12},{12,28},{28,24},{24,20},{20,16},{16,0},{1,5},{5... | collective-permute-start | bytes 3145736 | tf_op jit(solution)/shard_map/ppermute | solution.py:65
  194.5 38.6 %collective-permute-start.28 = (bf16[2048,256]{1,0:T(8,128)(2,1)}, bf16[2048,256]{1,0:T(8,128)(2,1)S(1)}, u32[]{:S(2)}, u32[]{:S(2)}) collective-permute-start(bf16[2048,256]{1,0:T(8,128)(2,1)} %refs_1_.9), channel_id=1, source_target_pairs={{0,4},{4,8},{8,12},{12,28},{28,24},{24,20},{20,16},{16,0},{1,5},{5... | collective-permute-start | bytes 3145736 | tf_op jit(solution)/shard_map/ppermute | solution.py:65
  196.1 38.0 %collective-permute-start.32 = (bf16[2048,256]{1,0:T(8,128)(2,1)}, bf16[2048,256]{1,0:T(8,128)(2,1)S(1)}, u32[]{:S(2)}, u32[]{:S(2)}) collective-permute-start(bf16[2048,256]{1,0:T(8,128)(2,1)} %collective-permute-done.31.refs_8_), channel_id=1, source_target_pairs={{4,0},{8,4},{12,8},{28,12},{24,28},{20,24},{16,20},{0,16},{5,1},{9... | collective-permute-start | bytes 3145736 | tf_op jit(solution)/shard_map/ppermute | solution.py:69
  223.0 33.1 %collective-permute-start.82 = (bf16[2048,256]{1,0:T(8,128)(2,1)S(1)}, bf16[2048,256]{1,0:T(8,128)(2,1)S(1)}, u32[]{:S(2)}, u32[]{:S(2)}) collective-permute-start(bf16[2048,256]{1,0:T(8,128)(2,1)S(1)} %convolution_convert_fusion), channel_id=1, source_target_pairs={{4,0},{8,4},{12,8},{28,12},{24,28},{20,24},{16,20},{0,16},{5,1},{9... | collective-permute-start | bytes 3145736 | tf_op jit(solution)/shard_map/ppermute | solution.py:83
  225.4 31.8 %collective-permute-start.78 = (bf16[2048,256]{1,0:T(8,128)(2,1)S(1)}, bf16[2048,256]{1,0:T(8,128)(2,1)S(1)}, u32[]{:S(2)}, u32[]{:S(2)}) collective-permute-start(bf16[2048,256]{1,0:T(8,128)(2,1)S(1)} %convolution_convert_fusion.1), channel_id=1, source_target_pairs={{0,4},{4,8},{8,12},{12,28},{28,24},{24,20},{20,16},{16,0},{1,5},{5... | collective-permute-start | bytes 3145736 | tf_op jit(solution)/shard_map/ppermute | solution.py:83
  233.2 44.9 %collective-permute-start.29 = (bf16[2048,256]{1,0:T(8,128)(2,1)S(1)}, bf16[2048,256]{1,0:T(8,128)(2,1)S(1)}, u32[]{:S(2)}, u32[]{:S(2)}) collective-permute-start(bf16[2048,256]{1,0:T(8,128)(2,1)S(1)} %collective-permute-done.28.refs_2_), channel_id=1, source_target_pairs={{0,4},{4,8},{8,12},{12,28},{28,24},{24,20},{20,16},{16,0},{1,5},{5... | collective-permute-start | bytes 3145736 | tf_op jit(solution)/shard_map/ppermute | solution.py:65
  234.2 44.9 %collective-permute-start.33 = (bf16[2048,256]{1,0:T(8,128)(2,1)S(1)}, bf16[2048,256]{1,0:T(8,128)(2,1)S(1)}, u32[]{:S(2)}, u32[]{:S(2)}) collective-permute-start(bf16[2048,256]{1,0:T(8,128)(2,1)S(1)} %collective-permute-done.32.refs_7_), channel_id=1, source_target_pairs={{4,0},{8,4},{12,8},{28,12},{24,28},{20,24},{16,20},{0,16},{5,1},{9... | collective-permute-start | bytes 3145736 | tf_op jit(solution)/shard_map/ppermute | solution.py:69
  256.9 44.1 %collective-permute-start.83 = (bf16[2048,256]{1,0:T(8,128)(2,1)S(1)}, bf16[2048,256]{1,0:T(8,128)(2,1)S(1)}, u32[]{:S(2)}, u32[]{:S(2)}) collective-permute-start(bf16[2048,256]{1,0:T(8,128)(2,1)S(1)} %fusion.11), channel_id=1, source_target_pairs={{4,0},{8,4},{12,8},{28,12},{24,28},{20,24},{16,20},{0,16},{5,1},{9... | collective-permute-start | bytes 3145736 | tf_op jit(solution)/shard_map/ppermute | solution.py:83
  258.0 45.1 %collective-permute-start.79 = (bf16[2048,256]{1,0:T(8,128)(2,1)S(1)}, bf16[2048,256]{1,0:T(8,128)(2,1)S(1)}, u32[]{:S(2)}, u32[]{:S(2)}) collective-permute-start(bf16[2048,256]{1,0:T(8,128)(2,1)S(1)} %fusion.9), channel_id=1, source_target_pairs={{0,4},{4,8},{8,12},{12,28},{28,24},{24,20},{20,16},{16,0},{1,5},{5... | collective-permute-start | bytes 3145736 | tf_op jit(solution)/shard_map/ppermute | solution.py:83
  278.1 44.9 %collective-permute-start.30 = (bf16[2048,256]{1,0:T(8,128)(2,1)S(1)}, bf16[2048,256]{1,0:T(8,128)(2,1)S(1)}, u32[]{:S(2)}, u32[]{:S(2)}) collective-permute-start(bf16[2048,256]{1,0:T(8,128)(2,1)S(1)} %collective-permute-done.29.refs_3_), channel_id=1, source_target_pairs={{0,4},{4,8},{8,12},{12,28},{28,24},{24,20},{20,16},{16,0},{1,5},{5... | collective-permute-start | bytes 3145736 | tf_op jit(solution)/shard_map/ppermute | solution.py:65
  279.1 44.3 %collective-permute-start.34 = (bf16[2048,256]{1,0:T(8,128)(2,1)S(1)}, bf16[2048,256]{1,0:T(8,128)(2,1)S(1)}, u32[]{:S(2)}, u32[]{:S(2)}) collective-permute-start(bf16[2048,256]{1,0:T(8,128)(2,1)S(1)} %collective-permute-done.33.refs_6_), channel_id=1, source_target_pairs={{4,0},{8,4},{12,8},{28,12},{24,28},{20,24},{16,20},{0,16},{5,1},{9... | collective-permute-start | bytes 3145736 | tf_op jit(solution)/shard_map/ppermute | solution.py:69
  302.8 120.8 %collective-permute-start.84 = (bf16[2048,256]{1,0:T(8,128)(2,1)}, bf16[2048,256]{1,0:T(8,128)(2,1)}, u32[]{:S(2)}, u32[]{:S(2)}) collective-permute-start(bf16[2048,256]{1,0:T(8,128)(2,1)} %fusion.10), channel_id=1, source_target_pairs={{4,0},{8,4},{12,8},{28,12},{24,28},{20,24},{16,20},{0,16},{5,1},{9... | collective-permute-start | bytes 3145736 | tf_op jit(solution)/shard_map/ppermute | solution.py:83
  304.8 63.1 %collective-permute-start.80 = (bf16[2048,256]{1,0:T(8,128)(2,1)}, bf16[2048,256]{1,0:T(8,128)(2,1)}, u32[]{:S(2)}, u32[]{:S(2)}) collective-permute-start(bf16[2048,256]{1,0:T(8,128)(2,1)} %fusion.8), channel_id=1, source_target_pairs={{0,4},{4,8},{8,12},{12,28},{28,24},{24,20},{20,16},{16,0},{1,5},{5... | collective-permute-start | bytes 3145736 | tf_op jit(solution)/shard_map/ppermute | solution.py:83
  370.2 53.3 %collective-permute-start.81 = (bf16[2048,256]{1,0:T(8,128)(2,1)S(1)}, bf16[2048,256]{1,0:T(8,128)(2,1)S(1)}, u32[]{:S(2)}, u32[]{:S(2)}) collective-permute-start(bf16[2048,256]{1,0:T(8,128)(2,1)S(1)} %fusion.7), channel_id=1, source_target_pairs={{0,4},{4,8},{8,12},{12,28},{28,24},{24,20},{20,16},{16,0},{1,5},{5... | collective-permute-start | bytes 3145736 | tf_op jit(solution)/shard_map/ppermute | solution.py:83
  407.8 30.1 %collective-permute-start.72 = (bf16[256,2048]{1,0:T(8,128)(2,1)S(1)}, bf16[256,2048]{1,0:T(8,128)(2,1)S(1)}, u32[]{:S(2)}, u32[]{:S(2)}) collective-permute-start(bf16[256,2048]{1,0:T(8,128)(2,1)S(1)} %fusion.3), channel_id=1, source_target_pairs={{0,4},{4,8},{8,12},{12,28},{28,24},{24,20},{20,16},{16,0},{1,5},{5... | collective-permute-start | bytes 3145736 | tf_op jit(solution)/shard_map/ppermute | solution.py:83
  439.6 73.7 %collective-permute-start.73 = (bf16[256,2048]{1,0:T(8,128)(2,1)}, bf16[256,2048]{1,0:T(8,128)(2,1)S(1)}, u32[]{:S(2)}, u32[]{:S(2)}) collective-permute-start(bf16[256,2048]{1,0:T(8,128)(2,1)} %fusion.2), channel_id=1, source_target_pairs={{0,4},{4,8},{8,12},{12,28},{28,24},{24,20},{20,16},{16,0},{1,5},{5... | collective-permute-start | bytes 3145736 | tf_op jit(solution)/shard_map/ppermute | solution.py:83
  445.5 68.0 %collective-permute-start.77 = (bf16[256,2048]{1,0:T(8,128)(2,1)}, bf16[256,2048]{1,0:T(8,128)(2,1)S(1)}, u32[]{:S(2)}, u32[]{:S(2)}) collective-permute-start(bf16[256,2048]{1,0:T(8,128)(2,1)} %fusion.4), channel_id=1, source_target_pairs={{4,0},{8,4},{12,8},{28,12},{24,28},{20,24},{16,20},{0,16},{5,1},{9... | collective-permute-start | bytes 3145736 | tf_op jit(solution)/shard_map/ppermute | solution.py:83
  474.1 41.4 %collective-permute-start.41 = (bf16[256,2048]{1,0:T(8,128)(2,1)S(1)}, bf16[256,2048]{1,0:T(8,128)(2,1)S(1)}, u32[]{:S(2)}, u32[]{:S(2)}) collective-permute-start(bf16[256,2048]{1,0:T(8,128)(2,1)S(1)} %get-tuple-element.57), channel_id=1, source_target_pairs={{0,1},{1,0},{2,3},{3,2},{4,5},{5,4},{6,7},{7,6},{8,9},{9,8},{10,11... | collective-permute-start | bytes 3145736 | tf_op jit(solution)/shard_map/ppermute | solution.py:111
  (135 other events, 1710.8 us)

commit v3 on v2

--- a/solution.py
+++ b/solution.py
@@ -10,6 +10,7 @@
 
 eps = 1e-05
 masked_score = -1000000000.0
+log2_e = math.log2(math.e)
 f32 = jnp.float32
 bf16 = jnp.bfloat16
 ring_axes = ("fsdp", "ctx")
@@ -73,7 +74,7 @@
     def scatter(self, part, flip):
         hops_right, hops_left = self.hops(flip)
         n = self.size
-        total = part(0)
+        last = []
         for hops, sign, pairs in ((hops_right, -1, self.right), (hops_left, 1, self.left)):
             moving = None
             for k in range(hops, 0, -1):
@@ -82,8 +83,15 @@
                     piece = piece + moving.astype(f32)
                 moving = lax.ppermute(piece.astype(bf16), ring_axes, pairs)
             if moving is not None:
-                total = total + moving.astype(f32)
-        return total
+                last.append(moving)
+
+        def finish(gate=None):
+            total = part(0)
+            for moving in last:
+                total = total + after(moving, gate).astype(f32)
+            return total
+
+        return finish
 
     def into(self, values):
         width = values.shape[-1] // self.size
@@ -253,11 +261,18 @@
         chunk_refs = refs[1 : 1 + count]
         extra_refs = refs[1 + count : 1 + count + len(extras)]
         out_refs = refs[1 + count + len(extras) :]
-        total = None
-        for k in range(count):
-            part = dot(left_ref[:, k * piece : (k + 1) * piece], chunk_refs[k][...], NT if turned else NN)
-            total = part if total is None else total + part
-        finish(total, extra_refs, out_refs)
+        step = min(rows, 256)
+        for start in range(0, rows, step):
+            at = slice(start, start + step)
+            total = None
+            for k in range(count):
+                part = dot(
+                    left_ref[at, k * piece : (k + 1) * piece],
+                    chunk_refs[k][...],
+                    NT if turned else NN,
+                )
+                total = part if total is None else total + part
+            finish(total, extra_refs, out_refs, at)
 
     if turned:
         chunk_spec = pl.BlockSpec((tile, piece), lambda i: (i, 0))
@@ -299,9 +314,9 @@
             copy(k).start()
         for k in range(count):
             copy(k).wait()
-            part = dot(left_ref[...], held[k], NT if turned else NN).astype(bf16)
-            keep_ref[:, k * piece : (k + 1) * piece] = part[:half]
-            send_ref[:, k * piece : (k + 1) * piece] = part[half:]
+            for out_ref, start in ((keep_ref, 0), (send_ref, half)):
+                part = dot(left_ref[start : start + half, :], held[k], NT if turned else NN)
+                out_ref[:, k * piece : (k + 1) * piece] = part.astype(bf16)
 
     shape = jax.ShapeDtypeStruct((half, piece * count), bf16)
     return pl.pallas_call(
@@ -326,7 +341,7 @@
     return ((seg == own) | (seg == one) | (seg == two)) & (spot <= place)
 
 
-def attend(qkv, kv_blocks, key_info, query_info, heads, head, scale, rows_at_once=256):
+def attend(qkv, kv_blocks, key_info, query_info, heads, head, scale, rows_at_once=512):
     rows = qkv.shape[0]
     count = len(kv_blocks)
     span = kv_blocks[0].shape[0]
@@ -334,7 +349,7 @@
 
     def kernel(q_ref, *refs):
         kv_refs = refs[:count]
-        key_ref, info_ref, out_ref, log_ref, turned, score, exps = refs[count:]
+        key_ref, info_ref, out_ref, log_ref, turned, score = refs[count:]
 
         @pl.when(pl.program_id(0) == 0)
         def _():
@@ -348,27 +363,22 @@
             query = q_ref[:, h * head : (h + 1) * head]
             top = None
             for d in range(count):
-                raw = dot(kv_refs[d][:, :head], query, NT) * scale
-                raw = jnp.where(masks[d], raw, masked_score)
+                raw = dot(kv_refs[d][:, :head], query, NT)
+                raw = jnp.where(masks[d], raw, masked_score / scale)
                 score[d * span : (d + 1) * span, :] = raw
                 peak = jnp.max(raw, axis=0, keepdims=True)
                 top = peak if top is None else jnp.maximum(top, peak)
-            total = None
+            total = mixed = None
             for d in range(count):
-                e = jnp.exp(score[d * span : (d + 1) * span, :] - top)
-                exps[d * span : (d + 1) * span, :] = e
+                e = jnp.exp2((score[d * span : (d + 1) * span, :] - top) * (scale * log2_e))
                 summed = jnp.sum(e, axis=0, keepdims=True)
                 total = summed if total is None else total + summed
-            mixed = None
-            inverse = 1.0 / total
-            for d in range(count):
-                low = (exps[d * span : (d + 1) * span, :] * inverse).astype(bf16)
-                part = dot(turned[:, d * span : (d + 1) * span], low, NN)
+                part = dot(turned[:, d * span : (d + 1) * span], e.astype(bf16), NN)
                 mixed = part if mixed is None else mixed + part
-            out_ref[:, h * head : (h + 1) * head] = mixed.T.astype(bf16)
-            log_ref[h : h + 1, :] = top + jnp.log(total)
-
-    block = rows_at_once
+            out_ref[:, h * head : (h + 1) * head] = (mixed * (1.0 / total)).T.astype(bf16)
+            log_ref[h : h + 1, :] = (top * scale + jnp.log(total)) * log2_e
+
+    block = min(rows_at_once, rows)
     return pl.pallas_call(
         kernel,
         out_shape=(
@@ -389,14 +399,13 @@
         scratch_shapes=[
             pltpu.VMEM((head, keys), bf16),
             pltpu.VMEM((keys, block), f32),
-            pltpu.VMEM((keys, block), f32),
         ],
         compiler_params=params(40),
         cost_estimate=cost(4 * rows * keys * heads * head, 4 * rows * heads * head, rows * keys * heads),
     )(qkv, *kv_blocks, key_info, query_info)
 
 
-def attend_back(qkv, kv_blocks, key_info, query_info, logs, grad, heads, head, scale, rows_at_once=256):
+def attend_back(qkv, kv_blocks, key_info, query_info, logs, grad, out, heads, head, scale, rows_at_once=256):
     rows = qkv.shape[0]
     count = len(kv_blocks)
     span = kv_blocks[0].shape[0]
@@ -404,7 +413,7 @@
 
     def kernel(q_ref, *refs):
         kv_refs = refs[:count]
-        key_ref, info_ref, log_ref, grad_ref, dq_ref, dkv_ref, turned, probs, pulls = refs[count:]
+        key_ref, info_ref, log_ref, grad_ref, out_ref, dq_ref, dkv_ref, turned = refs[count:]
 
         @pl.when(pl.program_id(0) == 0)
         def _():
@@ -420,27 +429,23 @@
             query = q_ref[:, cols]
             pulled = grad_ref[:, cols]
             log = log_ref[h : h + 1, :]
-            delta = None
-            for d in range(count):
-                at = slice(d * span, (d + 1) * span)
-                raw = dot(kv_refs[d][:, :head], query, NT) * scale
-                p = jnp.exp(jnp.where(masks[d], raw, masked_score) - log)
-                g = dot(kv_refs[d][:, head:], pulled, NT)
-                probs[at, :] = p
-                pulls[at, :] = g
-                part = jnp.sum(p * g, axis=0, keepdims=True)
-                delta = part if delta is None else delta + part
-                dkv_ref[at, head:] += dot(p.astype(bf16), pulled, NN)
+            delta = jnp.sum(
+                (pulled.astype(f32) * out_ref[:, cols].astype(f32)).T, axis=0, keepdims=True
+            )
             mixed = None
             for d in range(count):
                 at = slice(d * span, (d + 1) * span)
-                ds = (probs[at, :] * (pulls[at, :] - delta)).astype(bf16)
+                raw = dot(kv_refs[d][:, :head], query, NT) * (scale * log2_e)
+                p = jnp.exp2(jnp.where(masks[d], raw, masked_score) - log)
+                g = dot(kv_refs[d][:, head:], pulled, NT)
+                ds = (p * (g - delta)).astype(bf16)
+                dkv_ref[at, head:] += dot(p.astype(bf16), pulled, NN)
                 dkv_ref[at, :head] += dot(ds, query, NN) * scale
                 part = dot(turned[:, at], ds, NN)
                 mixed = part if mixed is None else mixed + part
             dq_ref[:, cols] = (mixed * scale).T.astype(bf16)
 
-    block = rows_at_once
+    block = min(rows_at_once, rows)
     return pl.pallas_call(
         kernel,
         out_shape=(
@@ -455,6 +460,7 @@
             pl.BlockSpec((8, block), lambda i: (0, i)),
             pl.BlockSpec((8, block), lambda i: (0, i)),
             pl.BlockSpec((block, heads * head), lambda i: (i, 0)),
+            pl.BlockSpec((block, heads * head), lambda i: (i, 0)),
         ],
         out_specs=(
             pl.BlockSpec((block, heads * head), lambda i: (i, 0)),
@@ -462,14 +468,12 @@
         ),
         scratch_shapes=[
             pltpu.VMEM((head, keys), bf16),
-            pltpu.VMEM((keys, block), f32),
-            pltpu.VMEM((keys, block), f32),
         ],
         compiler_params=params(44),
         cost_estimate=cost(
             10 * rows * keys * heads * head, 8 * keys * head + 6 * rows * heads * head, rows * keys * heads
         ),
-    )(qkv, *kv_blocks, key_info, query_info, logs, grad)
+    )(qkv, *kv_blocks, key_info, query_info, logs, grad, out)
 
 
 def parent_lookup(seg_ids, parents):
@@ -524,11 +528,11 @@
     n = ring.size
     piece = width // n
 
-    qkv_slots = ring.gather(jnp.concatenate([q_weight, kv_weight], axis=1), False)
-    o_slots = ring.gather(o_weight, True)
+    qkv_slots = ring.gather(jnp.concatenate([q_weight, kv_weight], axis=1), True)
+    o_slots = ring.gather(o_weight, False)
     half = n // 2
-    up_slots = ring.gather(up_weight, False, o_slots[half - 1], o_slots[half])
-    down_slots = ring.gather(down_weight, True, up_slots[2 % n], up_slots[(n - 2) % n])
+    up_slots = ring.gather(up_weight, False, o_slots[1], o_slots[n - 1])
+    down_slots = ring.gather(down_weight, True, up_slots[1], up_slots[n - 1])
 
     masks = [0]
     for bit in reversed(list(bits_of("tp"))):
@@ -584,8 +588,8 @@
         [q_bias.astype(f32), jnp.zeros((head_size,), f32), value_bias.astype(f32)]
     )
 
-    def add_shift(total, extra, out):
-        out[0][...] = (total + extra[0][...]).astype(bf16)
+    def add_shift(total, extra, out, at):
+        out[0][at, :] = (total + extra[0][...]).astype(bf16)
 
     (qkv,) = chunk_sum(
         act_one, qkv_slots, False, 256, [(qkv_shift[None], 1)], add_shift, [(bf16, row_count)]
@@ -605,16 +609,16 @@
     act_two = share_spread((norm_two * gain_two + shift_two).astype(bf16))
 
 
-    def activate(total, extra, out):
+    def activate(total, extra, out, at):
         gelu_out, gelu_slope = gelu_parts(total + extra[0][...])
-        out[0][...] = gelu_out.astype(bf16)
-        out[1][...] = gelu_slope
+        out[0][at, :] = gelu_out.astype(bf16)
+        out[1][at, :] = gelu_slope
 
     hidden, gelu_slope = chunk_sum(
         act_two,
         up_slots,
         False,
-        256,
+        512,
         [(up_bias.astype(f32)[None], 1)],
         activate,
         [(bf16, row_count), (f32, row_count)],
@@ -623,16 +627,17 @@
         lambda k: dot(hidden, g_low[:, k * piece : (k + 1) * piece], TN), False
     )
 
-    def deactivate(total, extra, out):
-        low = (total * extra[0][...]).astype(bf16)
-        out[0][...] = low
-        out[1][...] = jnp.sum(low.astype(f32), axis=0, keepdims=True)
+    def deactivate(total, extra, out, at):
+        low = (total * extra[0][at, :]).astype(bf16)
+        out[0][at, :] = low
+        summed = jnp.sum(low.astype(f32), axis=0, keepdims=True)
+        out[1][...] = summed if at.start == 0 else out[1][...] + summed
 
     grad_pre, up_bias_grad = chunk_sum(
         g_low,
         down_slots,
         True,
-        256,
+        512,
         [(gelu_slope, row_count)],
         deactivate,
         [(bf16, row_count), (f32, 1)],
@@ -653,8 +658,8 @@
         lambda k: dot(attended, grad_attn[:, k * piece : (k + 1) * piece], TN), False
     )
 
-    def only_round(total, extra, out):
-        out[0][...] = total.astype(bf16)
+    def only_round(total, extra, out, at):
+        out[0][at, :] = total.astype(bf16)
 
     (grad_attended,) = chunk_sum(
         grad_attn, o_slots, True, 256, [], only_round, [(bf16, row_count)]
@@ -670,7 +675,7 @@
     early = everyone_sum(ring.back(early).reshape(-1), ("tp",))
 
     grad_query, kv_grad = attend_back(
-        qkv, kv_blocks, key_info, query_info, logs, grad_attended,
+        qkv, kv_blocks, key_info, query_info, logs, grad_attended, attended,
         local_heads, head_size, score_scale,
     )
     q_bias_grad = jnp.sum(grad_query.astype(f32), axis=0)
@@ -698,7 +703,7 @@
         kv_piece = jnp.concatenate([kv_piece[: sub // 2], kv_piece[sub // 2 :]], axis=1)
         return jnp.concatenate([q_piece, kv_piece], axis=0)
 
-    q_kv = ring.scatter(q_kv_part, True)
+    q_kv = ring.scatter(q_kv_part, True)()
     q_w_grad = q_kv[:piece]
     kv_w_grad = jnp.concatenate(
         [q_kv[piece:, : 2 * head_size], q_kv[piece:, 2 * head_size :]], axis=0
@@ -724,6 +729,9 @@
         for stop, v in zip(cuts, (late, early, q_bias_grad, up_bias_grad))
     )
     early = early.reshape(4, width)
+    down_w_grad = down_w_grad(grad_query)
+    up_w_grad = up_w_grad(grad_query)
+    out_w_grad = out_w_grad(None)
     return (
         layer_out,
         input_grad,

time: 564 us -> 517 us (0.917)
  waiting for transfers between devices: 264 us -> 223 us
  Pallas kernels: 88.4 us -> 69.7 us
  matrix products: 30.2 us -> 37.3 us
    ppermute x14, waiting for transfers between devices: 114 us -> 37.1 us  [gather(): moving = lax.ppermute(moving, ring_axes, self.right)]
    ppermute x14, waiting for transfers between devices: 14.4 us -> 78.7 us  [gather(): moving = lax.ppermute(moving, ring_axes, self.left)]
    ppermute x28, waiting for transfers between devices: 96.2 us -> 78.3 us  [scatter(): moving = lax.ppermute(piece.astype(bf16), ring_axes, pairs)]
    pallas_call x4, Pallas kernels: 31.6 us -> 22 us  [chunk_side(): pl.pallas_call(kernel, out_shape=(shape, shape), in_specs=[pl.BlockSpec(m...]
    ppermute x14, starting transfers between devices: 8.54 us -> 17.3 us  [gather(): moving = lax.ppermute(moving, ring_axes, self.left)]
    dot_general x41, matrix products: 30.2 us -> 37.3 us  [dot(): lax.dot_general(left, right, (dims, ((), ())), preferred_element_type=f32)]
    ppermute x23, waiting for transfers between devices: 30.9 us -> 25.1 us  [swap(): return lax.ppermute(values, axis, [(i, i ^ bit) for i in range(count)])]
    ppermute x23, starting transfers between devices: 15.9 us -> 21.7 us  [swap(): return lax.ppermute(values, axis, [(i, i ^ bit) for i in range(count)])]
  transfers between devices with their start and end apart: 85 -> 85, of which waited for: 41 -> 33; matrix products, arithmetic and copies ran while one was open for 12% -> 14% of each run, Pallas kernels for 15% -> 14%
where the time goes in v3:
time: 517 us; the launch traced here: 512 us
  waiting for transfers between devices  223 us (43%)
  starting transfers between devices  107 us (21%)
  Pallas kernels  69.7 us (13%)
  local copies, waits for them, and re-layouts  45.9 us (9%)
  matrix products  37.3 us (7%)
  other arithmetic  15.3 us (3%)
  between operations  13.4 us (3%)
    ppermute x14, waiting for transfers between devices, gather(): moving = lax.ppermute(moving, ring_axes, self.left)  78.7 us
    ppermute x28, waiting for transfers between devices, scatter(): moving = lax.ppermute(piece.astype(bf16), ring_axes, pairs)  78.3 us
    dot_general x41, matrix products, dot(): lax.dot_general(left, right, (dims, ((), ())), preferred_element_type=f32)  37.3 us
    ppermute x14, waiting for transfers between devices, gather(): moving = lax.ppermute(moving, ring_axes, self.right)  37.1 us
    unnamed x216, local copies, waits for them, and re-layouts  31.1 us
    ppermute x28, starting transfers between devices, scatter(): moving = lax.ppermute(piece.astype(bf16), ring_axes, pairs)  29.7 us
    ppermute x14, starting transfers between devices, gather(): moving = lax.ppermute(moving, ring_axes, self.right)  25.5 us
    ppermute x23, waiting for transfers between devices, swap(): return lax.ppermute(values, axis, [(i, i ^ bit) for i in range(count)])  25.1 us
  transfers between devices with their start and end apart: 85, of which 33 were waited for; matrix products, arithmetic and copies ran while one was open for 14% of the time, Pallas kernels for 14%

profile of v3, /device:TPU:0, one launch (start us, length us, event | category | flops | bytes accessed | tf_op | source)
XLA Modules:
  0.0 511.9 jit_solution(1285169471744365138)
XLA Ops:
  20.5 10.4 %collective-permute-done.4.refs_7_ = bf16[256,768]{1,0:T(8,128)(2,1)S(1)} collective-permute-done((bf16[256,768]{1,0:T(8,128)(2,1)S(1)}, bf16[256,768]{1,0:T(8,128)(2,1)S(1)}, u32[]{:S(2)}, u32[]{:S(2)}) %collective-permute-start.4) | collective-permute-done | bytes 393248 | tf_op jit(solution)/shard_map/ppermute | solution.py:70
  35.3 5.2 %collective-permute-done.5.refs_6_ = bf16[256,768]{1,0:T(8,128)(2,1)S(1)} collective-permute-done((bf16[256,768]{1,0:T(8,128)(2,1)S(1)}, bf16[256,768]{1,0:T(8,128)(2,1)S(1)}, u32[]{:S(2)}, u32[]{:S(2)}) %collective-permute-start.5) | collective-permute-done | bytes 393248 | tf_op jit(solution)/shard_map/ppermute | solution.py:70
  64.7 4.4 collective-permute-start.8
  73.9 9.8 %collective-permute-start.21 = (bf16[256,2048]{1,0:T(8,128)(2,1)}, bf16[256,2048]{1,0:T(8,128)(2,1)}, u32[]{:S(2)}, u32[]{:S(2)}) collective-permute-start(bf16[256,2048]{1,0:T(8,128)(2,1)} %refs_1_.10), channel_id=1, source_target_pairs={{0,4},{4,8},{8,12},{12,28},{28,24},{24,20},{20,16},{16,0},{1,5},{5... | collective-permute-start | bytes 3145736 | tf_op jit(solution)/shard_map/ppermute | solution.py:66
  83.9 9.4 %shard_map.326 = (bf16[512,512]{1,0:T(8,128)(2,1)S(1)}, f32[8,512]{1,0:T(8,128)S(1)}) custom-call(bf16[512,768]{1,0:T(8,128)(2,1)S(1)} %shard_map.325.q_ref, bf16[512,256]{1,0:T(8,128)(2,1)S(1)} %slice.483.refs_0_, bf16[512,256]{1,0:T(8,128)(2,1)S(1)} %collective-permute-done.7.refs_1_, bf16[512,256]{1,0:T(8,128)(2,1)S(1)} %collective-permute-done.8.refs_2_, ...), custom_call_target="tpu_custom_call" | custom-call | flops 2147483648 | bytes 1048576 | tf_op jit(solution)/shard_map/pallas_call | solution.py:382
  93.4 4.4 shard_map.327
  112.1 6.4 %collective-permute-start.31 = (bf16[2048,256]{1,0:T(8,128)(2,1)S(1)}, bf16[2048,256]{1,0:T(8,128)(2,1)S(1)}, u32[]{:S(2)}, u32[]{:S(2)}) collective-permute-start(bf16[2048,256]{1,0:T(8,128)(2,1)S(1)} %copy-done.41), channel_id=1, source_target_pairs={{4,0},{8,4},{12,8},{28,12},{24,28},{20,24},{16,20},{0,16},{5,1},{9... | collective-permute-start | bytes 3145736 | tf_op jit(solution)/shard_map/ppermute | solution.py:70
  124.2 17.9 %collective-permute-done.31.refs_8_ = bf16[2048,256]{1,0:T(8,128)(2,1)S(1)} collective-permute-done((bf16[2048,256]{1,0:T(8,128)(2,1)S(1)}, bf16[2048,256]{1,0:T(8,128)(2,1)S(1)}, u32[]{:S(2)}, u32[]{:S(2)}) %collective-permute-start.31) | collective-permute-done | bytes 1048608 | tf_op jit(solution)/shard_map/ppermute | solution.py:70
  149.1 18.0 %collective-permute-done.28.refs_2_ = bf16[2048,256]{1,0:T(8,128)(2,1)S(1)} collective-permute-done((bf16[2048,256]{1,0:T(8,128)(2,1)S(1)}, bf16[2048,256]{1,0:T(8,128)(2,1)S(1)}, u32[]{:S(2)}, u32[]{:S(2)}) %collective-permute-start.28) | collective-permute-done | bytes 1048608 | tf_op jit(solution)/shard_map/ppermute | solution.py:66
  167.1 19.8 %collective-permute-done.32.refs_7_ = bf16[2048,256]{1,0:T(8,128)(2,1)S(1)} collective-permute-done((bf16[2048,256]{1,0:T(8,128)(2,1)S(1)}, bf16[2048,256]{1,0:T(8,128)(2,1)S(1)}, u32[]{:S(2)}, u32[]{:S(2)}) %collective-permute-start.32) | collective-permute-done | bytes 1048608 | tf_op jit(solution)/shard_map/ppermute | solution.py:70
  194.9 17.1 %collective-permute-done.29.refs_3_ = bf16[2048,256]{1,0:T(8,128)(2,1)S(1)} collective-permute-done((bf16[2048,256]{1,0:T(8,128)(2,1)S(1)}, bf16[2048,256]{1,0:T(8,128)(2,1)S(1)}, u32[]{:S(2)}, u32[]{:S(2)}) %collective-permute-start.29) | collective-permute-done | bytes 1048608 | tf_op jit(solution)/shard_map/ppermute | solution.py:66
  215.2 20.2 %collective-permute-done.27.refs_6_ = bf16[256,2048]{1,0:T(8,128)(2,1)S(1)} collective-permute-done((bf16[256,2048]{1,0:T(8,128)(2,1)S(1)}, bf16[256,2048]{1,0:T(8,128)(2,1)S(1)}, u32[]{:S(2)}, u32[]{:S(2)}) %collective-permute-start.27) | collective-permute-done | bytes 1048608 | tf_op jit(solution)/shard_map/ppermute | solution.py:70
  240.0 9.8 %shard_map.328 = (bf16[512,2048]{1,0:T(8,128)(2,1)S(1)}, f32[512,2048]{1,0:T(8,128)}) custom-call(bf16[512,2048]{1,0:T(8,128)(2,1)S(1)} %pad_maximum_fusion.refs_0_, bf16[256,2048]{1,0:T(8,128)(2,1)} %refs_1_.10, bf16[256,2048]{1,0:T(8,128)(2,1)} %collective-permute-done.21.refs_2_, bf16[256,2048]{1,0:T(8,128)(2,1)S(1)} %collective-permute-done.22.refs_3_, ...), custom_call_target="tpu_custom_call" | custom-call | flops 4294967296 | bytes 18874368 | tf_op jit(solution)/shard_map/pallas_call | solution.py:281
  258.0 7.0 %shard_map.331 = (bf16[512,2048]{1,0:T(8,128)(2,1)S(1)}, f32[1,2048]{1,0:T(1,128)S(1)}) custom-call(bf16[512,2048]{1,0:T(8,128)(2,1)S(1)} %shard_map.330.refs_0_, bf16[2048,256]{1,0:T(8,128)(2,1)S(1)} %copy-done.41, bf16[2048,256]{1,0:T(8,128)(2,1)S(1)} %collective-permute-done.28.refs_2_, bf16[2048,256]{1,0:T(8,128)(2,1)S(1)} %copy-done.55, ...), custom_call_target="tpu_custom_call" | custom-call | flops 4294967296 | bytes 18874368 | tf_op jit(solution)/shard_map/pallas_call | solution.py:281
  268.7 8.4 %shard_map.332 = (bf16[256,2048]{1,0:T(8,128)(2,1)S(1)}, bf16[256,2048]{1,0:T(8,128)(2,1)}) custom-call(bf16[512,2048]{1,0:T(8,128)(2,1)S(1)} %get-tuple-element.55.refs_0_, bf16[256,2048]{1,0:T(8,128)(2,1)} %refs_1_.10, bf16[256,2048]{1,0:T(8,128)(2,1)} %collective-permute-done.21.refs_2_, bf16[256,2048]{1,0:T(8,128)(2,1)S(1)} %collective-permute-done.22.refs_3_, ...), custom_call_target="tpu_custom_call" | custom-call | flops 4294967296 | bytes 12582912 | tf_op jit(solution)/shard_map/pallas_call | solution.py:322
  283.1 6.3 %shard_map.329 = (bf16[256,2048]{1,0:T(8,128)(2,1)S(1)}, bf16[256,2048]{1,0:T(8,128)(2,1)S(1)}) custom-call(bf16[512,2048]{1,0:T(8,128)(2,1)S(1)} %get-tuple-element.49.refs_0_, bf16[2048,256]{1,0:T(8,128)(2,1)S(1)} %copy-done.42, bf16[2048,256]{1,0:T(8,128)(2,1)S(1)} %copy-done.46, bf16[2048,256]{1,0:T(8,128)(2,1)S(1)} %copy-done.56, ...), custom_call_target="tpu_custom_call" | custom-call | flops 4294967296 | bytes 12582912 | tf_op jit(solution)/shard_map/pallas_call | solution.py:322
  303.6 13.1 %collective-permute-done.74 = bf16[256,2048]{1,0:T(8,128)(2,1)S(1)} collective-permute-done((bf16[256,2048]{1,0:T(8,128)(2,1)S(1)}, bf16[256,2048]{1,0:T(8,128)(2,1)S(1)}, u32[]{:S(2)}, u32[]{:S(2)}) %collective-permute-start.74) | collective-permute-done | bytes 1048608 | tf_op jit(solution)/shard_map/ppermute | solution.py:84
  323.0 6.3 %collective-permute-done.36 = bf16[128,2048]{1,0:T(8,128)(2,1)S(1)} collective-permute-done((bf16[128,2048]{1,0:T(8,128)(2,1)S(1)}, bf16[128,2048]{1,0:T(8,128)(2,1)S(1)}, u32[]{:S(2)}, u32[]{:S(2)}) %collective-permute-start.36) | collective-permute-done | bytes 524320 | tf_op jit(solution)/shard_map/ppermute | solution.py:119
  333.1 9.0 %collective-permute-done.79 = bf16[2048,256]{1,0:T(8,128)(2,1)S(1)} collective-permute-done((bf16[2048,256]{1,0:T(8,128)(2,1)S(1)}, bf16[2048,256]{1,0:T(8,128)(2,1)S(1)}, u32[]{:S(2)}, u32[]{:S(2)}) %collective-permute-start.79) | collective-permute-done | bytes 1048608 | tf_op jit(solution)/shard_map/ppermute | solution.py:84
  344.8 16.2 %collective-permute-done.75 = bf16[256,2048]{1,0:T(8,128)(2,1)S(1)} collective-permute-done((bf16[256,2048]{1,0:T(8,128)(2,1)S(1)}, bf16[256,2048]{1,0:T(8,128)(2,1)S(1)}, u32[]{:S(2)}, u32[]{:S(2)}) %collective-permute-start.75) | collective-permute-done | bytes 1048608 | tf_op jit(solution)/shard_map/ppermute | solution.py:84
  371.4 15.6 %collective-permute-done.80 = bf16[2048,256]{1,0:T(8,128)(2,1)S(1)} collective-permute-done((bf16[2048,256]{1,0:T(8,128)(2,1)S(1)}, bf16[2048,256]{1,0:T(8,128)(2,1)S(1)}, u32[]{:S(2)}, u32[]{:S(2)}) %collective-permute-start.80) | collective-permute-done | bytes 1048608 | tf_op jit(solution)/shard_map/ppermute | solution.py:84
  394.9 11.5 %shard_map.334 = (bf16[512,512]{1,0:T(8,128)(2,1)S(1)}, f32[2048,256]{1,0:T(8,128)S(1)}) custom-call(bf16[512,768]{1,0:T(8,128)(2,1)S(1)} %shard_map.325.q_ref, bf16[512,256]{1,0:T(8,128)(2,1)S(1)} %copy-done.40, bf16[512,256]{1,0:T(8,128)(2,1)S(1)} %copy-done.67, bf16[512,256]{1,0:T(8,128)(2,1)S(1)} %copy-done.69, bf16[512,256]{1,0:T(8,128)(2,1)S(1)} %copy-done.71, ...), custom_call_target="tpu_custom_call" | custom-call | flops 5368709120 | bytes 3670016 | tf_op jit(solution)/shard_map/pallas_call | solution.py:449
  420.4 16.0 %collective-permute-done.64 = bf16[512,256]{1,0:T(8,128)(2,1)S(1)} collective-permute-done((bf16[512,256]{1,0:T(8,128)(2,1)S(1)}, bf16[512,256]{1,0:T(8,128)(2,1)S(1)}, u32[]{:S(2)}, u32[]{:S(2)}) %collective-permute-start.64) | collective-permute-done | bytes 262176 | tf_op jit(solution)/shard_map/ppermute | solution.py:84
  476.6 4.6 collective-permute-done.60
  (553 shorter events, 231.7 us)
Async XLA Ops:
  8.3 45.1 %collective-permute-start.14 = (bf16[512,256]{1,0:T(8,128)(2,1)}, bf16[512,256]{1,0:T(8,128)(2,1)}, u32[]{:S(2)}, u32[]{:S(2)}) collective-permute-start(bf16[512,256]{1,0:T(8,128)(2,1)} %refs_1_.11), channel_id=1, source_target_pairs={{4,0},{8,4},{12,8},{28,12},{24,28},{20,24},{16,20},{0,16},{5,1},{9... | collective-permute-start | bytes 786440 | tf_op jit(solution)/shard_map/ppermute | solution.py:70
  73.9 44.6 %collective-permute-start.21 = (bf16[256,2048]{1,0:T(8,128)(2,1)}, bf16[256,2048]{1,0:T(8,128)(2,1)}, u32[]{:S(2)}, u32[]{:S(2)}) collective-permute-start(bf16[256,2048]{1,0:T(8,128)(2,1)} %refs_1_.10), channel_id=1, source_target_pairs={{0,4},{4,8},{8,12},{12,28},{28,24},{24,20},{20,16},{16,0},{1,5},{5... | collective-permute-start | bytes 3145736 | tf_op jit(solution)/shard_map/ppermute | solution.py:66
  121.7 45.4 %collective-permute-start.28 = (bf16[2048,256]{1,0:T(8,128)(2,1)S(1)}, bf16[2048,256]{1,0:T(8,128)(2,1)S(1)}, u32[]{:S(2)}, u32[]{:S(2)}) collective-permute-start(bf16[2048,256]{1,0:T(8,128)(2,1)S(1)} %copy-done.41), channel_id=1, source_target_pairs={{0,4},{4,8},{8,12},{12,28},{28,24},{24,20},{20,16},{16,0},{1,5},{5... | collective-permute-start | bytes 3145736 | tf_op jit(solution)/shard_map/ppermute | solution.py:66
  123.5 66.6 %collective-permute-start.26 = (bf16[256,2048]{1,0:T(8,128)(2,1)}, bf16[256,2048]{1,0:T(8,128)(2,1)S(1)}, u32[]{:S(2)}, u32[]{:S(2)}) collective-permute-start(bf16[256,2048]{1,0:T(8,128)(2,1)} %collective-permute-done.25.refs_8_), channel_id=1, source_target_pairs={{4,0},{8,4},{12,8},{28,12},{24,28},{20,24},{16,20},{0,16},{5,1},{9... | collective-permute-start | bytes 3145736 | tf_op jit(solution)/shard_map/ppermute | solution.py:70
  142.2 44.7 %collective-permute-start.32 = (bf16[2048,256]{1,0:T(8,128)(2,1)S(1)}, bf16[2048,256]{1,0:T(8,128)(2,1)S(1)}, u32[]{:S(2)}, u32[]{:S(2)}) collective-permute-start(bf16[2048,256]{1,0:T(8,128)(2,1)S(1)} %collective-permute-done.31.refs_8_), channel_id=1, source_target_pairs={{4,0},{8,4},{12,8},{28,12},{24,28},{20,24},{16,20},{0,16},{5,1},{9... | collective-permute-start | bytes 3145736 | tf_op jit(solution)/shard_map/ppermute | solution.py:70
  144.7 47.0 %collective-permute-start.23 = (bf16[256,2048]{1,0:T(8,128)(2,1)S(1)}, bf16[256,2048]{1,0:T(8,128)(2,1)S(1)}, u32[]{:S(2)}, u32[]{:S(2)}) collective-permute-start(bf16[256,2048]{1,0:T(8,128)(2,1)S(1)} %collective-permute-done.22.refs_3_), channel_id=1, source_target_pairs={{0,4},{4,8},{8,12},{12,28},{28,24},{24,20},{20,16},{16,0},{1,5},{5... | collective-permute-start | bytes 3145736 | tf_op jit(solution)/shard_map/ppermute | solution.py:66
  145.7 43.3 %collective-permute-start.19 = (bf16[128,2048]{1,0:T(8,128)(2,1)S(1)}, bf16[128,2048]{1,0:T(8,128)(2,1)S(1)}, u32[]{:S(2)}, u32[]{:S(2)}) collective-permute-start(bf16[128,2048]{1,0:T(8,128)(2,1)S(1)} %add_convert_fusion), channel_id=1, source_target_pairs={{0,2},{1,3},{2,0},{3,1},{4,6},{5,7},{6,4},{7,5},{8,10},{9,11},{10,... | collective-permute-start | bytes 1572872 | tf_op jit(solution)/shard_map/ppermute | solution.py:119
  167.1 44.9 %collective-permute-start.29 = (bf16[2048,256]{1,0:T(8,128)(2,1)S(1)}, bf16[2048,256]{1,0:T(8,128)(2,1)S(1)}, u32[]{:S(2)}, u32[]{:S(2)}) collective-permute-start(bf16[2048,256]{1,0:T(8,128)(2,1)S(1)} %collective-permute-done.28.refs_2_), channel_id=1, source_target_pairs={{0,4},{4,8},{8,12},{12,28},{28,24},{24,20},{20,16},{16,0},{1,5},{5... | collective-permute-start | bytes 3145736 | tf_op jit(solution)/shard_map/ppermute | solution.py:66
  190.1 45.3 %collective-permute-start.27 = (bf16[256,2048]{1,0:T(8,128)(2,1)S(1)}, bf16[256,2048]{1,0:T(8,128)(2,1)S(1)}, u32[]{:S(2)}, u32[]{:S(2)}) collective-permute-start(bf16[256,2048]{1,0:T(8,128)(2,1)S(1)} %collective-permute-done.26.refs_7_), channel_id=1, source_target_pairs={{4,0},{8,4},{12,8},{28,12},{24,28},{20,24},{16,20},{0,16},{5,1},{9... | collective-permute-start | bytes 3145736 | tf_op jit(solution)/shard_map/ppermute | solution.py:70
  191.6 44.9 %collective-permute-start.24 = (bf16[256,2048]{1,0:T(8,128)(2,1)S(1)}, bf16[256,2048]{1,0:T(8,128)(2,1)S(1)}, u32[]{:S(2)}, u32[]{:S(2)}) collective-permute-start(bf16[256,2048]{1,0:T(8,128)(2,1)S(1)} %collective-permute-done.23.refs_4_), channel_id=1, source_target_pairs={{0,4},{4,8},{8,12},{12,28},{28,24},{24,20},{20,16},{16,0},{1,5},{5... | collective-permute-start | bytes 3145736 | tf_op jit(solution)/shard_map/ppermute | solution.py:66
  212.1 45.0 %collective-permute-start.30 = (bf16[2048,256]{1,0:T(8,128)(2,1)S(1)}, bf16[2048,256]{1,0:T(8,128)(2,1)}, u32[]{:S(2)}, u32[]{:S(2)}) collective-permute-start(bf16[2048,256]{1,0:T(8,128)(2,1)S(1)} %collective-permute-done.29.refs_3_), channel_id=1, source_target_pairs={{0,4},{4,8},{8,12},{12,28},{28,24},{24,20},{20,16},{16,0},{1,5},{5... | collective-permute-start | bytes 3145736 | tf_op jit(solution)/shard_map/ppermute | solution.py:66
  212.9 45.0 %collective-permute-start.34 = (bf16[2048,256]{1,0:T(8,128)(2,1)S(1)}, bf16[2048,256]{1,0:T(8,128)(2,1)}, u32[]{:S(2)}, u32[]{:S(2)}) collective-permute-start(bf16[2048,256]{1,0:T(8,128)(2,1)S(1)} %collective-permute-done.33.refs_6_), channel_id=1, source_target_pairs={{4,0},{8,4},{12,8},{28,12},{24,28},{20,24},{16,20},{0,16},{5,1},{9... | collective-permute-start | bytes 3145736 | tf_op jit(solution)/shard_map/ppermute | solution.py:70
  251.5 42.0 %collective-permute-start.82 = (bf16[2048,256]{1,0:T(8,128)(2,1)}, bf16[2048,256]{1,0:T(8,128)(2,1)}, u32[]{:S(2)}, u32[]{:S(2)}) collective-permute-start(bf16[2048,256]{1,0:T(8,128)(2,1)} %convolution_convert_fusion), channel_id=1, source_target_pairs={{4,0},{8,4},{12,8},{28,12},{24,28},{20,24},{16,20},{0,16},{5,1},{9... | collective-permute-start | bytes 3145736 | tf_op jit(solution)/shard_map/ppermute | solution.py:84
  255.4 40.2 %collective-permute-start.78 = (bf16[2048,256]{1,0:T(8,128)(2,1)}, bf16[2048,256]{1,0:T(8,128)(2,1)}, u32[]{:S(2)}, u32[]{:S(2)}) collective-permute-start(bf16[2048,256]{1,0:T(8,128)(2,1)} %convolution_convert_fusion.1), channel_id=1, source_target_pairs={{0,4},{4,8},{8,12},{12,28},{28,24},{24,20},{20,16},{16,0},{1,5},{5... | collective-permute-start | bytes 3145736 | tf_op jit(solution)/shard_map/ppermute | solution.py:84
  295.6 47.3 %collective-permute-start.83 = (bf16[2048,256]{1,0:T(8,128)(2,1)S(1)}, bf16[2048,256]{1,0:T(8,128)(2,1)S(1)}, u32[]{:S(2)}, u32[]{:S(2)}) collective-permute-start(bf16[2048,256]{1,0:T(8,128)(2,1)S(1)} %fusion.11), channel_id=1, source_target_pairs={{4,0},{8,4},{12,8},{28,12},{24,28},{20,24},{16,20},{0,16},{5,1},{9... | collective-permute-start | bytes 3145736 | tf_op jit(solution)/shard_map/ppermute | solution.py:84
  299.9 42.2 %collective-permute-start.79 = (bf16[2048,256]{1,0:T(8,128)(2,1)S(1)}, bf16[2048,256]{1,0:T(8,128)(2,1)S(1)}, u32[]{:S(2)}, u32[]{:S(2)}) collective-permute-start(bf16[2048,256]{1,0:T(8,128)(2,1)S(1)} %fusion.9), channel_id=1, source_target_pairs={{0,4},{4,8},{8,12},{12,28},{28,24},{24,20},{20,16},{16,0},{1,5},{5... | collective-permute-start | bytes 3145736 | tf_op jit(solution)/shard_map/ppermute | solution.py:84
  319.6 41.4 %collective-permute-start.75 = (bf16[256,2048]{1,0:T(8,128)(2,1)S(1)}, bf16[256,2048]{1,0:T(8,128)(2,1)S(1)}, u32[]{:S(2)}, u32[]{:S(2)}) collective-permute-start(bf16[256,2048]{1,0:T(8,128)(2,1)S(1)} %fusion.6), channel_id=1, source_target_pairs={{4,0},{8,4},{12,8},{28,12},{24,28},{20,24},{16,20},{0,16},{5,1},{9... | collective-permute-start | bytes 3145736 | tf_op jit(solution)/shard_map/ppermute | solution.py:84
  322.3 46.9 %collective-permute-start.72 = (bf16[256,2048]{1,0:T(8,128)(2,1)S(1)}, bf16[256,2048]{1,0:T(8,128)(2,1)S(1)}, u32[]{:S(2)}, u32[]{:S(2)}) collective-permute-start(bf16[256,2048]{1,0:T(8,128)(2,1)S(1)} %fusion.3), channel_id=1, source_target_pairs={{0,4},{4,8},{8,12},{12,28},{28,24},{24,20},{20,16},{16,0},{1,5},{5... | collective-permute-start | bytes 3145736 | tf_op jit(solution)/shard_map/ppermute | solution.py:84
  342.9 44.1 %collective-permute-start.80 = (bf16[2048,256]{1,0:T(8,128)(2,1)S(1)}, bf16[2048,256]{1,0:T(8,128)(2,1)S(1)}, u32[]{:S(2)}, u32[]{:S(2)}) collective-permute-start(bf16[2048,256]{1,0:T(8,128)(2,1)S(1)} %fusion.8), channel_id=1, source_target_pairs={{0,4},{4,8},{8,12},{12,28},{28,24},{24,20},{20,16},{16,0},{1,5},{5... | collective-permute-start | bytes 3145736 | tf_op jit(solution)/shard_map/ppermute | solution.py:84
  367.7 51.8 %collective-permute-start.84 = (bf16[2048,256]{1,0:T(8,128)(2,1)}, bf16[2048,256]{1,0:T(8,128)(2,1)}, u32[]{:S(2)}, u32[]{:S(2)}) collective-permute-start(bf16[2048,256]{1,0:T(8,128)(2,1)} %fusion.10), channel_id=1, source_target_pairs={{4,0},{8,4},{12,8},{28,12},{24,28},{20,24},{16,20},{0,16},{5,1},{9... | collective-permute-start | bytes 3145736 | tf_op jit(solution)/shard_map/ppermute | solution.py:84
  371.0 46.5 %collective-permute-start.73 = (bf16[256,2048]{1,0:T(8,128)(2,1)}, bf16[256,2048]{1,0:T(8,128)(2,1)}, u32[]{:S(2)}, u32[]{:S(2)}) collective-permute-start(bf16[256,2048]{1,0:T(8,128)(2,1)} %fusion.2), channel_id=1, source_target_pairs={{0,4},{4,8},{8,12},{12,28},{28,24},{24,20},{20,16},{16,0},{1,5},{5... | collective-permute-start | bytes 3145736 | tf_op jit(solution)/shard_map/ppermute | solution.py:84
  388.8 50.4 %collective-permute-start.81 = (bf16[2048,256]{1,0:T(8,128)(2,1)}, bf16[2048,256]{1,0:T(8,128)(2,1)}, u32[]{:S(2)}, u32[]{:S(2)}) collective-permute-start(bf16[2048,256]{1,0:T(8,128)(2,1)} %fusion.7), channel_id=1, source_target_pairs={{0,4},{4,8},{8,12},{12,28},{28,24},{24,20},{20,16},{16,0},{1,5},{5... | collective-permute-start | bytes 3145736 | tf_op jit(solution)/shard_map/ppermute | solution.py:84
  417.4 48.0 %collective-permute-start.77 = (bf16[256,2048]{1,0:T(8,128)(2,1)S(1)}, bf16[256,2048]{1,0:T(8,128)(2,1)S(1)}, u32[]{:S(2)}, u32[]{:S(2)}) collective-permute-start(bf16[256,2048]{1,0:T(8,128)(2,1)S(1)} %copy-done.77), channel_id=1, source_target_pairs={{4,0},{8,4},{12,8},{28,12},{24,28},{20,24},{16,20},{0,16},{5,1},{9... | collective-permute-start | bytes 3145736 | tf_op jit(solution)/shard_map/ppermute | solution.py:84
  419.5 49.3 %collective-permute-start.41 = (bf16[256,2048]{1,0:T(8,128)(2,1)S(1)}, bf16[256,2048]{1,0:T(8,128)(2,1)S(1)}, u32[]{:S(2)}, u32[]{:S(2)}) collective-permute-start(bf16[256,2048]{1,0:T(8,128)(2,1)S(1)} %get-tuple-element.61), channel_id=1, source_target_pairs={{0,1},{1,0},{2,3},{3,2},{4,5},{5,4},{6,7},{7,6},{8,9},{9,8},{10,11... | collective-permute-start | bytes 3145736 | tf_op jit(solution)/shard_map/ppermute | solution.py:119
  (150 other events, 2247.2 us)

commit v4 on v3

--- a/solution.py
+++ b/solution.py
@@ -71,27 +71,43 @@
             slots[self.size - k] = moving
         return slots
 
-    def scatter(self, part, flip):
+    def scatter(self, part, flip, early=None):
         hops_right, hops_left = self.hops(flip)
         n = self.size
         last = []
+        legs = []
         for hops, sign, pairs in ((hops_right, -1, self.right), (hops_left, 1, self.left)):
-            moving = None
-            for k in range(hops, 0, -1):
-                piece = part((sign * k) % n)
-                if moving is not None:
-                    piece = piece + moving.astype(f32)
-                moving = lax.ppermute(piece.astype(bf16), ring_axes, pairs)
-            if moving is not None:
-                last.append(moving)
+            if hops:
+                legs.append([hops, sign, pairs, None])
+
+        def run(stop, gate=None):
+            for leg in legs:
+                while leg[0] > stop(leg):
+                    hops, sign, pairs, moving = leg
+                    piece = part((sign * hops) % n)
+                    if moving is not None:
+                        if gate is not None:
+                            moving = after(moving, gate)
+                        piece = piece + moving.astype(f32)
+                    leg[3] = lax.ppermute(piece.astype(bf16), ring_axes, pairs)
+                    leg[0] = hops - 1
+
+        if early is None:
+            run(lambda leg: 0)
+        else:
+            begin = [leg[0] for leg in legs]
+            run(lambda leg: begin[legs.index(leg)] - early)
+
+        def resume(gate):
+            run(lambda leg: 0, gate)
 
         def finish(gate=None):
             total = part(0)
-            for moving in last:
-                total = total + after(moving, gate).astype(f32)
+            for leg in legs:
+                total = total + after(leg[3], gate).astype(f32)
             return total
 
-        return finish
+        return finish if early is None else (finish, resume)
 
     def into(self, values):
         width = values.shape[-1] // self.size
@@ -647,15 +663,13 @@
         lambda k: dot(act_two[:, k * piece : (k + 1) * piece], grad_pre, TN), True
     )
     grad_two = share_sum(*chunk_side(grad_pre, up_slots, True))
-    ffn_share = share_sum(*chunk_side(hidden, down_slots, False))
-    layer_out = ring.back((residual + (ffn_share + down_shift)).astype(bf16))
 
     g_share = g_low[:share_rows].astype(f32)
     grad_res = g_share + normed_back(grad_two, gain_two, norm_two, inv_two)
     grad_attn_share = grad_res.astype(bf16)
     grad_attn = share_spread(grad_attn_share)
-    out_w_grad = ring.scatter(
-        lambda k: dot(attended, grad_attn[:, k * piece : (k + 1) * piece], TN), False
+    out_w_grad, out_resume = ring.scatter(
+        lambda k: dot(attended, grad_attn[:, k * piece : (k + 1) * piece], TN), False, 1
     )
 
     def only_round(total, extra, out, at):
@@ -664,6 +678,8 @@
     (grad_attended,) = chunk_sum(
         grad_attn, o_slots, True, 256, [], only_round, [(bf16, row_count)]
     )
+    ffn_share = share_sum(*chunk_side(after(hidden, grad_attended), down_slots, False))
+    layer_out = ring.back((residual + (ffn_share + down_shift)).astype(bf16))
     early = jnp.stack(
         [
             jnp.sum(g_share, axis=0),
@@ -672,7 +688,7 @@
             jnp.sum(grad_two, axis=0),
         ]
     )
-    early = everyone_sum(ring.back(early).reshape(-1), ("tp",))
+    early = ring.back(early).reshape(-1)
 
     grad_query, kv_grad = attend_back(
         qkv, kv_blocks, key_info, query_info, logs, grad_attended, attended,
@@ -693,6 +709,7 @@
         ).astype(f32)
     kv_low_share = kv_sum.astype(bf16)
     kv_low = share_spread(kv_low_share)
+    out_resume(kv_low)
 
     sub = piece // tp_count
 
@@ -720,7 +737,9 @@
     late = jnp.stack([jnp.sum(grad_act * norm_share, axis=0), jnp.sum(grad_act, axis=0)])
     late = ring.back(late).reshape(-1)
     value_bias_grad = jnp.sum(kv_low_share[:, head_size:].astype(f32), axis=0)
-    late = everyone_sum(jnp.concatenate([late, value_bias_grad]), ("tp",))
+    late = everyone_sum(jnp.concatenate([late, value_bias_grad, early]), ("tp",))
+    early = late[2 * width + head_size :]
+    late = late[: 2 * width + head_size]
     sums = [late, early, q_bias_grad, up_bias_grad]
     cuts = np.cumsum([v.shape[0] for v in sums])
     sums = everyone_sum(jnp.concatenate(sums), ("ctx", "fsdp"))

time: 517 us -> 509 us (0.985)
  waiting for transfers between devices: 223 us -> 213 us
    ppermute x14, waiting for transfers between devices: 78.7 us -> 60 us  [gather(): moving = lax.ppermute(moving, ring_axes, self.left)]
    ppermute x14, waiting for transfers between devices: 37.1 us -> 52.5 us  [gather(): moving = lax.ppermute(moving, ring_axes, self.right)]
    ppermute x23 -> x21, waiting for transfers between devices: 25.1 us -> 11.6 us  [swap(): return lax.ppermute(values, axis, [(i, i ^ bit) for i in range(count)])]
    ppermute x28, waiting for transfers between devices: 78.3 us -> 86.4 us  [run(): leg[3] = lax.ppermute(piece.astype(bf16), ring_axes, pairs)]
    unnamed x216 -> x230, local copies, waits for them, and re-layouts: 31.1 us -> 29.6 us
    ppermute x23 -> x21, starting transfers between devices: 21.7 us -> 20.7 us  [swap(): return lax.ppermute(values, axis, [(i, i ^ bit) for i in range(count)])]
  transfers between devices with their start and end apart: 85 -> 83, of which waited for: 33 -> 27; matrix products, arithmetic and copies ran while one was open for 14% -> 15% of each run, Pallas kernels for 14% -> 14%
where the time goes in v4:
time: 509 us; the launch traced here: 503 us
  waiting for transfers between devices  213 us (42%)
  starting transfers between devices  108 us (21%)
  Pallas kernels  69 us (14%)
  local copies, waits for them, and re-layouts  44.5 us (9%)
  matrix products  40.8 us (8%)
  other arithmetic  14.2 us (3%)
  between operations  13.4 us (3%)
    ppermute x28, waiting for transfers between devices, run(): leg[3] = lax.ppermute(piece.astype(bf16), ring_axes, pairs)  86.4 us
    ppermute x14, waiting for transfers between devices, gather(): moving = lax.ppermute(moving, ring_axes, self.left)  60 us
    ppermute x14, waiting for transfers between devices, gather(): moving = lax.ppermute(moving, ring_axes, self.right)  52.5 us
    dot_general x41, matrix products, dot(): lax.dot_general(left, right, (dims, ((), ())), preferred_element_type=f32)  40.8 us
    ppermute x28, starting transfers between devices, run(): leg[3] = lax.ppermute(piece.astype(bf16), ring_axes, pairs)  31.6 us
    unnamed x230, local copies, waits for them, and re-layouts  29.6 us
    ppermute x14, starting transfers between devices, gather(): moving = lax.ppermute(moving, ring_axes, self.right)  25.5 us
    pallas_call x4, Pallas kernels, chunk_sum(): pl.pallas_call(kernel, out_shape=tuple((jax.ShapeDtypeStruct((r, columns)...  23.3 us
  transfers between devices with their start and end apart: 83, of which 27 were waited for; matrix products, arithmetic and copies ran while one was open for 15% of the time, Pallas kernels for 14%

profile of v4, /device:TPU:0, one launch (start us, length us, event | category | flops | bytes accessed | tf_op | source)
XLA Modules:
  0.0 503.1 jit_solution(15987428285254812862)
XLA Ops:
  20.5 10.4 %collective-permute-done.4.refs_7_ = bf16[256,768]{1,0:T(8,128)(2,1)S(1)} collective-permute-done((bf16[256,768]{1,0:T(8,128)(2,1)S(1)}, bf16[256,768]{1,0:T(8,128)(2,1)S(1)}, u32[]{:S(2)}, u32[]{:S(2)}) %collective-permute-start.4) | collective-permute-done | bytes 393248 | tf_op jit(solution)/shard_map/ppermute | solution.py:70
  35.4 5.2 %collective-permute-done.5.refs_6_ = bf16[256,768]{1,0:T(8,128)(2,1)S(1)} collective-permute-done((bf16[256,768]{1,0:T(8,128)(2,1)S(1)}, bf16[256,768]{1,0:T(8,128)(2,1)S(1)}, u32[]{:S(2)}, u32[]{:S(2)}) %collective-permute-start.5) | collective-permute-done | bytes 393248 | tf_op jit(solution)/shard_map/ppermute | solution.py:70
  64.7 4.4 collective-permute-start.8
  73.9 9.7 %collective-permute-start.21 = (bf16[256,2048]{1,0:T(8,128)(2,1)}, bf16[256,2048]{1,0:T(8,128)(2,1)}, u32[]{:S(2)}, u32[]{:S(2)}) collective-permute-start(bf16[256,2048]{1,0:T(8,128)(2,1)} %refs_1_.9), channel_id=1, source_target_pairs={{0,4},{4,8},{8,12},{12,28},{28,24},{24,20},{20,16},{16,0},{1,5},{5... | collective-permute-start | bytes 3145736 | tf_op jit(solution)/shard_map/ppermute | solution.py:66
  84.0 9.4 %shard_map.326 = (bf16[512,512]{1,0:T(8,128)(2,1)S(1)}, f32[8,512]{1,0:T(8,128)S(1)}) custom-call(bf16[512,768]{1,0:T(8,128)(2,1)S(1)} %shard_map.325.q_ref, bf16[512,256]{1,0:T(8,128)(2,1)S(1)} %slice.486.refs_0_, bf16[512,256]{1,0:T(8,128)(2,1)S(1)} %collective-permute-done.7.refs_1_, bf16[512,256]{1,0:T(8,128)(2,1)S(1)} %collective-permute-done.8.refs_2_, ...), custom_call_target="tpu_custom_call" | custom-call | flops 2147483648 | bytes 1048576 | tf_op jit(solution)/shard_map/pallas_call | solution.py:398
  93.5 4.4 shard_map.327
  112.1 6.4 %collective-permute-start.31 = (bf16[2048,256]{1,0:T(8,128)(2,1)S(1)}, bf16[2048,256]{1,0:T(8,128)(2,1)S(1)}, u32[]{:S(2)}, u32[]{:S(2)}) collective-permute-start(bf16[2048,256]{1,0:T(8,128)(2,1)S(1)} %copy-done.40), channel_id=1, source_target_pairs={{4,0},{8,4},{12,8},{28,12},{24,28},{20,24},{16,20},{0,16},{5,1},{9... | collective-permute-start | bytes 3145736 | tf_op jit(solution)/shard_map/ppermute | solution.py:70
  124.4 20.3 %collective-permute-done.22.refs_3_ = bf16[256,2048]{1,0:T(8,128)(2,1)S(1)} collective-permute-done((bf16[256,2048]{1,0:T(8,128)(2,1)}, bf16[256,2048]{1,0:T(8,128)(2,1)S(1)}, u32[]{:S(2)}, u32[]{:S(2)}) %collective-permute-start.22) | collective-permute-done | bytes 1048608 | tf_op jit(solution)/shard_map/ppermute | solution.py:66
  152.1 15.1 %collective-permute-done.28.refs_2_ = bf16[2048,256]{1,0:T(8,128)(2,1)S(1)} collective-permute-done((bf16[2048,256]{1,0:T(8,128)(2,1)S(1)}, bf16[2048,256]{1,0:T(8,128)(2,1)S(1)}, u32[]{:S(2)}, u32[]{:S(2)}) %collective-permute-start.28) | collective-permute-done | bytes 1048608 | tf_op jit(solution)/shard_map/ppermute | solution.py:66
  167.1 19.8 %collective-permute-done.32.refs_7_ = bf16[2048,256]{1,0:T(8,128)(2,1)S(1)} collective-permute-done((bf16[2048,256]{1,0:T(8,128)(2,1)S(1)}, bf16[2048,256]{1,0:T(8,128)(2,1)S(1)}, u32[]{:S(2)}, u32[]{:S(2)}) %collective-permute-start.32) | collective-permute-done | bytes 1048608 | tf_op jit(solution)/shard_map/ppermute | solution.py:70
  194.9 17.1 %collective-permute-done.29.refs_3_ = bf16[2048,256]{1,0:T(8,128)(2,1)S(1)} collective-permute-done((bf16[2048,256]{1,0:T(8,128)(2,1)S(1)}, bf16[2048,256]{1,0:T(8,128)(2,1)S(1)}, u32[]{:S(2)}, u32[]{:S(2)}) %collective-permute-start.29) | collective-permute-done | bytes 1048608 | tf_op jit(solution)/shard_map/ppermute | solution.py:66
  215.2 20.1 %collective-permute-done.27.refs_6_ = bf16[256,2048]{1,0:T(8,128)(2,1)S(1)} collective-permute-done((bf16[256,2048]{1,0:T(8,128)(2,1)S(1)}, bf16[256,2048]{1,0:T(8,128)(2,1)S(1)}, u32[]{:S(2)}, u32[]{:S(2)}) %collective-permute-start.27) | collective-permute-done | bytes 1048608 | tf_op jit(solution)/shard_map/ppermute | solution.py:70
  242.3 9.8 %shard_map.328 = (bf16[512,2048]{1,0:T(8,128)(2,1)S(1)}, f32[512,2048]{1,0:T(8,128)}) custom-call(bf16[512,2048]{1,0:T(8,128)(2,1)S(1)} %pad_maximum_fusion.refs_0_, bf16[256,2048]{1,0:T(8,128)(2,1)} %refs_1_.9, bf16[256,2048]{1,0:T(8,128)(2,1)} %collective-permute-done.21.refs_2_, bf16[256,2048]{1,0:T(8,128)(2,1)S(1)} %copy-done.55, ...), custom_call_target="tpu_custom_call" | custom-call | flops 4294967296 | bytes 18874368 | tf_op jit(solution)/shard_map/pallas_call | solution.py:297
  258.0 7.1 %shard_map.330 = (bf16[512,2048]{1,0:T(8,128)(2,1)S(1)}, f32[1,2048]{1,0:T(1,128)S(1)}) custom-call(bf16[512,2048]{1,0:T(8,128)(2,1)S(1)} %shard_map.329.refs_0_, bf16[2048,256]{1,0:T(8,128)(2,1)S(1)} %copy-done.40, bf16[2048,256]{1,0:T(8,128)(2,1)S(1)} %collective-permute-done.28.refs_2_, bf16[2048,256]{1,0:T(8,128)(2,1)S(1)} %copy-done.49, ...), custom_call_target="tpu_custom_call" | custom-call | flops 4294967296 | bytes 18874368 | tf_op jit(solution)/shard_map/pallas_call | solution.py:297
  268.8 7.3 %shard_map.331 = (bf16[256,2048]{1,0:T(8,128)(2,1)S(1)}, bf16[256,2048]{1,0:T(8,128)(2,1)S(1)}) custom-call(bf16[512,2048]{1,0:T(8,128)(2,1)S(1)} %get-tuple-element.59.refs_0_, bf16[256,2048]{1,0:T(8,128)(2,1)} %refs_1_.9, bf16[256,2048]{1,0:T(8,128)(2,1)} %collective-permute-done.21.refs_2_, bf16[256,2048]{1,0:T(8,128)(2,1)S(1)} %copy-done.56, ...), custom_call_target="tpu_custom_call" | custom-call | flops 4294967296 | bytes 12582912 | tf_op jit(solution)/shard_map/pallas_call | solution.py:338
  288.2 14.9 %collective-permute-done.72 = bf16[256,2048]{1,0:T(8,128)(2,1)S(1)} collective-permute-done((bf16[256,2048]{1,0:T(8,128)(2,1)S(1)}, bf16[256,2048]{1,0:T(8,128)(2,1)S(1)}, u32[]{:S(2)}, u32[]{:S(2)}) %collective-permute-start.72) | collective-permute-done | bytes 1048608 | tf_op jit(solution)/shard_map/ppermute | solution.py:92
  310.7 17.8 %collective-permute-done.77 = bf16[2048,256]{1,0:T(8,128)(2,1)S(1)} collective-permute-done((bf16[2048,256]{1,0:T(8,128)(2,1)S(1)}, bf16[2048,256]{1,0:T(8,128)(2,1)S(1)}, u32[]{:S(2)}, u32[]{:S(2)}) %collective-permute-start.77) | collective-permute-done | bytes 1048608 | tf_op jit(solution)/shard_map/ppermute | solution.py:92
  331.2 16.7 %collective-permute-done.73 = bf16[256,2048]{1,0:T(8,128)(2,1)S(1)} collective-permute-done((bf16[256,2048]{1,0:T(8,128)(2,1)S(1)}, bf16[256,2048]{1,0:T(8,128)(2,1)S(1)}, u32[]{:S(2)}, u32[]{:S(2)}) %collective-permute-start.73) | collective-permute-done | bytes 1048608 | tf_op jit(solution)/shard_map/ppermute | solution.py:92
  354.6 18.9 %collective-permute-done.78 = bf16[2048,256]{1,0:T(8,128)(2,1)S(1)} collective-permute-done((bf16[2048,256]{1,0:T(8,128)(2,1)S(1)}, bf16[2048,256]{1,0:T(8,128)(2,1)S(1)}, u32[]{:S(2)}, u32[]{:S(2)}) %collective-permute-start.78) | collective-permute-done | bytes 1048608 | tf_op jit(solution)/shard_map/ppermute | solution.py:92
  382.3 11.5 %shard_map.334 = (bf16[512,512]{1,0:T(8,128)(2,1)S(1)}, f32[2048,256]{1,0:T(8,128)S(1)}) custom-call(bf16[512,768]{1,0:T(8,128)(2,1)S(1)} %shard_map.325.q_ref, bf16[512,256]{1,0:T(8,128)(2,1)S(1)} %copy-done.39, bf16[512,256]{1,0:T(8,128)(2,1)S(1)} %copy-done.70, bf16[512,256]{1,0:T(8,128)(2,1)S(1)} %copy-done.72, bf16[512,256]{1,0:T(8,128)(2,1)S(1)} %copy-done.74, ...), custom_call_target="tpu_custom_call" | custom-call | flops 5368709120 | bytes 3670016 | tf_op jit(solution)/shard_map/pallas_call | solution.py:465
  404.0 6.7 %shard_map.333 = (bf16[256,2048]{1,0:T(8,128)(2,1)S(1)}, bf16[256,2048]{1,0:T(8,128)(2,1)S(1)}) custom-call(bf16[512,2048]{1,0:T(8,128)(2,1)S(1)} %get-tuple-element.62.refs_0_, bf16[2048,256]{1,0:T(8,128)(2,1)S(1)} %copy-done.41, bf16[2048,256]{1,0:T(8,128)(2,1)S(1)} %copy-done.45, bf16[2048,256]{1,0:T(8,128)(2,1)S(1)} %copy-done.50, ...), custom_call_target="tpu_custom_call" | custom-call | flops 4294967296 | bytes 12582912 | tf_op jit(solution)/shard_map/pallas_call | solution.py:338
  422.5 3.7 fusion
  449.7 8.0 %collective-permute-done.67 = bf16[512,256]{1,0:T(8,128)(2,1)S(1)} collective-permute-done((bf16[512,256]{1,0:T(8,128)(2,1)S(1)}, bf16[512,256]{1,0:T(8,128)(2,1)S(1)}, u32[]{:S(2)}, u32[]{:S(2)}) %collective-permute-start.67) | collective-permute-done | bytes 262176 | tf_op jit(solution)/shard_map/ppermute | solution.py:92
  461.3 6.4 %collective-permute-done.55 = bf16[288,512]{1,0:T(8,128)(2,1)S(1)} collective-permute-done((bf16[288,512]{1,0:T(8,128)(2,1)S(1)}, bf16[288,512]{1,0:T(8,128)(2,1)S(1)}, u32[]{:S(2)}, u32[]{:S(2)}) %collective-permute-start.55) | collective-permute-done | bytes 294944 | tf_op jit(solution)/shard_map/ppermute | solution.py:92
  (562 shorter events, 218.6 us)
Async XLA Ops:
  6.3 34.9 %collective-permute-start.10 = (bf16[512,256]{1,0:T(8,128)(2,1)}, bf16[512,256]{1,0:T(8,128)(2,1)}, u32[]{:S(2)}, u32[]{:S(2)}) collective-permute-start(bf16[512,256]{1,0:T(8,128)(2,1)} %refs_1_.10), channel_id=1, source_target_pairs={{0,4},{4,8},{8,12},{12,28},{28,24},{24,20},{20,16},{16,0},{1,5},{5... | collective-permute-start | bytes 786440 | tf_op jit(solution)/shard_map/ppermute | solution.py:66
  8.3 45.1 %collective-permute-start.14 = (bf16[512,256]{1,0:T(8,128)(2,1)}, bf16[512,256]{1,0:T(8,128)(2,1)}, u32[]{:S(2)}, u32[]{:S(2)}) collective-permute-start(bf16[512,256]{1,0:T(8,128)(2,1)} %refs_1_.10), channel_id=1, source_target_pairs={{4,0},{8,4},{12,8},{28,12},{24,28},{20,24},{16,20},{0,16},{5,1},{9... | collective-permute-start | bytes 786440 | tf_op jit(solution)/shard_map/ppermute | solution.py:70
  73.9 44.5 %collective-permute-start.21 = (bf16[256,2048]{1,0:T(8,128)(2,1)}, bf16[256,2048]{1,0:T(8,128)(2,1)}, u32[]{:S(2)}, u32[]{:S(2)}) collective-permute-start(bf16[256,2048]{1,0:T(8,128)(2,1)} %refs_1_.9), channel_id=1, source_target_pairs={{0,4},{4,8},{8,12},{12,28},{28,24},{24,20},{20,16},{16,0},{1,5},{5... | collective-permute-start | bytes 3145736 | tf_op jit(solution)/shard_map/ppermute | solution.py:66
  121.7 45.4 %collective-permute-start.28 = (bf16[2048,256]{1,0:T(8,128)(2,1)S(1)}, bf16[2048,256]{1,0:T(8,128)(2,1)S(1)}, u32[]{:S(2)}, u32[]{:S(2)}) collective-permute-start(bf16[2048,256]{1,0:T(8,128)(2,1)S(1)} %copy-done.40), channel_id=1, source_target_pairs={{0,4},{4,8},{8,12},{12,28},{28,24},{24,20},{20,16},{16,0},{1,5},{5... | collective-permute-start | bytes 3145736 | tf_op jit(solution)/shard_map/ppermute | solution.py:66
  123.5 66.6 %collective-permute-start.26 = (bf16[256,2048]{1,0:T(8,128)(2,1)}, bf16[256,2048]{1,0:T(8,128)(2,1)S(1)}, u32[]{:S(2)}, u32[]{:S(2)}) collective-permute-start(bf16[256,2048]{1,0:T(8,128)(2,1)} %collective-permute-done.25.refs_8_), channel_id=1, source_target_pairs={{4,0},{8,4},{12,8},{28,12},{24,28},{20,24},{16,20},{0,16},{5,1},{9... | collective-permute-start | bytes 3145736 | tf_op jit(solution)/shard_map/ppermute | solution.py:70
  144.7 46.9 %collective-permute-start.23 = (bf16[256,2048]{1,0:T(8,128)(2,1)S(1)}, bf16[256,2048]{1,0:T(8,128)(2,1)S(1)}, u32[]{:S(2)}, u32[]{:S(2)}) collective-permute-start(bf16[256,2048]{1,0:T(8,128)(2,1)S(1)} %collective-permute-done.22.refs_3_), channel_id=1, source_target_pairs={{0,4},{4,8},{8,12},{12,28},{28,24},{24,20},{20,16},{16,0},{1,5},{5... | collective-permute-start | bytes 3145736 | tf_op jit(solution)/shard_map/ppermute | solution.py:66
  144.7 42.2 %collective-permute-start.32 = (bf16[2048,256]{1,0:T(8,128)(2,1)S(1)}, bf16[2048,256]{1,0:T(8,128)(2,1)S(1)}, u32[]{:S(2)}, u32[]{:S(2)}) collective-permute-start(bf16[2048,256]{1,0:T(8,128)(2,1)S(1)} %collective-permute-done.31.refs_8_), channel_id=1, source_target_pairs={{4,0},{8,4},{12,8},{28,12},{24,28},{20,24},{16,20},{0,16},{5,1},{9... | collective-permute-start | bytes 3145736 | tf_op jit(solution)/shard_map/ppermute | solution.py:70
  147.7 41.2 %collective-permute-start.19 = (bf16[128,2048]{1,0:T(8,128)(2,1)S(1)}, bf16[128,2048]{1,0:T(8,128)(2,1)S(1)}, u32[]{:S(2)}, u32[]{:S(2)}) collective-permute-start(bf16[128,2048]{1,0:T(8,128)(2,1)S(1)} %add_convert_fusion), channel_id=1, source_target_pairs={{0,2},{1,3},{2,0},{3,1},{4,6},{5,7},{6,4},{7,5},{8,10},{9,11},{10,... | collective-permute-start | bytes 1572872 | tf_op jit(solution)/shard_map/ppermute | solution.py:135
  167.1 44.9 %collective-permute-start.29 = (bf16[2048,256]{1,0:T(8,128)(2,1)S(1)}, bf16[2048,256]{1,0:T(8,128)(2,1)S(1)}, u32[]{:S(2)}, u32[]{:S(2)}) collective-permute-start(bf16[2048,256]{1,0:T(8,128)(2,1)S(1)} %collective-permute-done.28.refs_2_), channel_id=1, source_target_pairs={{0,4},{4,8},{8,12},{12,28},{28,24},{24,20},{20,16},{16,0},{1,5},{5... | collective-permute-start | bytes 3145736 | tf_op jit(solution)/shard_map/ppermute | solution.py:66
  190.1 45.3 %collective-permute-start.27 = (bf16[256,2048]{1,0:T(8,128)(2,1)S(1)}, bf16[256,2048]{1,0:T(8,128)(2,1)S(1)}, u32[]{:S(2)}, u32[]{:S(2)}) collective-permute-start(bf16[256,2048]{1,0:T(8,128)(2,1)S(1)} %collective-permute-done.26.refs_7_), channel_id=1, source_target_pairs={{4,0},{8,4},{12,8},{28,12},{24,28},{20,24},{16,20},{0,16},{5,1},{9... | collective-permute-start | bytes 3145736 | tf_op jit(solution)/shard_map/ppermute | solution.py:70
  191.6 44.8 %collective-permute-start.24 = (bf16[256,2048]{1,0:T(8,128)(2,1)S(1)}, bf16[256,2048]{1,0:T(8,128)(2,1)S(1)}, u32[]{:S(2)}, u32[]{:S(2)}) collective-permute-start(bf16[256,2048]{1,0:T(8,128)(2,1)S(1)} %collective-permute-done.23.refs_4_), channel_id=1, source_target_pairs={{0,4},{4,8},{8,12},{12,28},{28,24},{24,20},{20,16},{16,0},{1,5},{5... | collective-permute-start | bytes 3145736 | tf_op jit(solution)/shard_map/ppermute | solution.py:66
  212.1 45.7 %collective-permute-start.30 = (bf16[2048,256]{1,0:T(8,128)(2,1)S(1)}, bf16[2048,256]{1,0:T(8,128)(2,1)}, u32[]{:S(2)}, u32[]{:S(2)}) collective-permute-start(bf16[2048,256]{1,0:T(8,128)(2,1)S(1)} %collective-permute-done.29.refs_3_), channel_id=1, source_target_pairs={{0,4},{4,8},{8,12},{12,28},{28,24},{24,20},{20,16},{16,0},{1,5},{5... | collective-permute-start | bytes 3145736 | tf_op jit(solution)/shard_map/ppermute | solution.py:66
  212.9 45.0 %collective-permute-start.34 = (bf16[2048,256]{1,0:T(8,128)(2,1)S(1)}, bf16[2048,256]{1,0:T(8,128)(2,1)}, u32[]{:S(2)}, u32[]{:S(2)}) collective-permute-start(bf16[2048,256]{1,0:T(8,128)(2,1)S(1)} %collective-permute-done.33.refs_6_), channel_id=1, source_target_pairs={{4,0},{8,4},{12,8},{28,12},{24,28},{20,24},{16,20},{0,16},{5,1},{9... | collective-permute-start | bytes 3145736 | tf_op jit(solution)/shard_map/ppermute | solution.py:70
  282.1 47.4 %collective-permute-start.81 = (bf16[2048,256]{1,0:T(8,128)(2,1)S(1)}, bf16[2048,256]{1,0:T(8,128)(2,1)S(1)}, u32[]{:S(2)}, u32[]{:S(2)}) collective-permute-start(bf16[2048,256]{1,0:T(8,128)(2,1)S(1)} %fusion.11), channel_id=1, source_target_pairs={{4,0},{8,4},{12,8},{28,12},{24,28},{20,24},{16,20},{0,16},{5,1},{9... | collective-permute-start | bytes 3145736 | tf_op jit(solution)/shard_map/ppermute | solution.py:92
  286.1 42.4 %collective-permute-start.77 = (bf16[2048,256]{1,0:T(8,128)(2,1)S(1)}, bf16[2048,256]{1,0:T(8,128)(2,1)S(1)}, u32[]{:S(2)}, u32[]{:S(2)}) collective-permute-start(bf16[2048,256]{1,0:T(8,128)(2,1)S(1)} %fusion.9), channel_id=1, source_target_pairs={{0,4},{4,8},{8,12},{12,28},{28,24},{24,20},{20,16},{16,0},{1,5},{5... | collective-permute-start | bytes 3145736 | tf_op jit(solution)/shard_map/ppermute | solution.py:92
  303.9 44.0 %collective-permute-start.73 = (bf16[256,2048]{1,0:T(8,128)(2,1)S(1)}, bf16[256,2048]{1,0:T(8,128)(2,1)S(1)}, u32[]{:S(2)}, u32[]{:S(2)}) collective-permute-start(bf16[256,2048]{1,0:T(8,128)(2,1)S(1)} %fusion.6), channel_id=1, source_target_pairs={{4,0},{8,4},{12,8},{28,12},{24,28},{20,24},{16,20},{0,16},{5,1},{9... | collective-permute-start | bytes 3145736 | tf_op jit(solution)/shard_map/ppermute | solution.py:92
  306.8 45.9 %collective-permute-start.70 = (bf16[256,2048]{1,0:T(8,128)(2,1)S(1)}, bf16[256,2048]{1,0:T(8,128)(2,1)S(1)}, u32[]{:S(2)}, u32[]{:S(2)}) collective-permute-start(bf16[256,2048]{1,0:T(8,128)(2,1)S(1)} %fusion.3), channel_id=1, source_target_pairs={{0,4},{4,8},{8,12},{12,28},{28,24},{24,20},{20,16},{16,0},{1,5},{5... | collective-permute-start | bytes 3145736 | tf_op jit(solution)/shard_map/ppermute | solution.py:92
  309.1 41.4 %collective-permute-start.37 = (bf16[128,2048]{1,0:T(8,128)(2,1)S(1)}, bf16[128,2048]{1,0:T(8,128)(2,1)S(1)}, u32[]{:S(2)}, u32[]{:S(2)}) collective-permute-start(bf16[128,2048]{1,0:T(8,128)(2,1)S(1)} %get-tuple-element.89), channel_id=1, source_target_pairs={{0,2},{1,3},{2,0},{3,1},{4,6},{5,7},{6,4},{7,5},{8,10},{9,11},{10,... | collective-permute-start | bytes 1572872 | tf_op jit(solution)/shard_map/ppermute | solution.py:135
  329.3 44.2 %collective-permute-start.78 = (bf16[2048,256]{1,0:T(8,128)(2,1)S(1)}, bf16[2048,256]{1,0:T(8,128)(2,1)S(1)}, u32[]{:S(2)}, u32[]{:S(2)}) collective-permute-start(bf16[2048,256]{1,0:T(8,128)(2,1)S(1)} %fusion.8), channel_id=1, source_target_pairs={{0,4},{4,8},{8,12},{12,28},{28,24},{24,20},{20,16},{16,0},{1,5},{5... | collective-permute-start | bytes 3145736 | tf_op jit(solution)/shard_map/ppermute | solution.py:92
  350.8 64.8 %collective-permute-start.82 = (bf16[2048,256]{1,0:T(8,128)(2,1)}, bf16[2048,256]{1,0:T(8,128)(2,1)}, u32[]{:S(2)}, u32[]{:S(2)}) collective-permute-start(bf16[2048,256]{1,0:T(8,128)(2,1)} %fusion.10), channel_id=1, source_target_pairs={{4,0},{8,4},{12,8},{28,12},{24,28},{20,24},{16,20},{0,16},{5,1},{9... | collective-permute-start | bytes 3145736 | tf_op jit(solution)/shard_map/ppermute | solution.py:92
  354.3 61.1 %collective-permute-start.71 = (bf16[256,2048]{1,0:T(8,128)(2,1)}, bf16[256,2048]{1,0:T(8,128)(2,1)}, u32[]{:S(2)}, u32[]{:S(2)}) collective-permute-start(bf16[256,2048]{1,0:T(8,128)(2,1)} %fusion.2), channel_id=1, source_target_pairs={{0,4},{4,8},{8,12},{12,28},{28,24},{24,20},{20,16},{16,0},{1,5},{5... | collective-permute-start | bytes 3145736 | tf_op jit(solution)/shard_map/ppermute | solution.py:92
  375.2 42.6 %collective-permute-start.79 = (bf16[2048,256]{1,0:T(8,128)(2,1)}, bf16[2048,256]{1,0:T(8,128)(2,1)}, u32[]{:S(2)}, u32[]{:S(2)}) collective-permute-start(bf16[2048,256]{1,0:T(8,128)(2,1)} %fusion.7), channel_id=1, source_target_pairs={{0,4},{4,8},{8,12},{12,28},{28,24},{24,20},{20,16},{16,0},{1,5},{5... | collective-permute-start | bytes 3145736 | tf_op jit(solution)/shard_map/ppermute | solution.py:92
  376.9 58.5 %collective-permute-start.75 = (bf16[256,2048]{1,0:T(8,128)(2,1)}, bf16[256,2048]{1,0:T(8,128)(2,1)}, u32[]{:S(2)}, u32[]{:S(2)}) collective-permute-start(bf16[256,2048]{1,0:T(8,128)(2,1)} %fusion.4), channel_id=1, source_target_pairs={{4,0},{8,4},{12,8},{28,12},{24,28},{20,24},{16,20},{0,16},{5,1},{9... | collective-permute-start | bytes 3145736 | tf_op jit(solution)/shard_map/ppermute | solution.py:92
  458.5 36.1 %collective-permute-start.68 = (bf16[512,256]{1,0:T(8,128)(2,1)S(1)}, bf16[512,256]{1,0:T(8,128)(2,1)S(1)}, u32[]{:S(2)}, u32[]{:S(2)}) collective-permute-start(bf16[512,256]{1,0:T(8,128)(2,1)S(1)} %fusion.21), channel_id=1, source_target_pairs={{4,0},{8,4},{12,8},{28,12},{24,28},{20,24},{16,20},{0,16},{5,1},{9... | collective-permute-start | bytes 786440 | tf_op jit(solution)/shard_map/ppermute | solution.py:92
  (155 other events, 2287.4 us)

commit v5 on v4

--- a/solution.py
+++ b/solution.py
@@ -709,7 +709,7 @@
         ).astype(f32)
     kv_low_share = kv_sum.astype(bf16)
     kv_low = share_spread(kv_low_share)
-    out_resume(kv_low)
+    out_resume(kv_low_share)
 
     sub = piece // tp_count
 

time: 509 us -> 506 us (level)
  starting transfers between devices: 108 us -> 99.5 us
  waiting for transfers between devices: 213 us -> 220 us
    ppermute x21, starting transfers between devices: 20.7 us -> 14 us  [swap(): return lax.ppermute(values, axis, [(i, i ^ bit) for i in range(count)])]
    ppermute x21, waiting for transfers between devices: 11.6 us -> 18.2 us  [swap(): return lax.ppermute(values, axis, [(i, i ^ bit) for i in range(count)])]
where the time goes in v5:
time: 506 us; the launch traced here: 501 us
  waiting for transfers between devices  220 us (43%)
  starting transfers between devices  99.5 us (20%)
  Pallas kernels  69 us (14%)
  local copies, waits for them, and re-layouts  43.7 us (9%)
  matrix products  40.8 us (8%)
  other arithmetic  14.2 us (3%)
  between operations  13.4 us (3%)
    ppermute x28, waiting for transfers between devices, run(): leg[3] = lax.ppermute(piece.astype(bf16), ring_axes, pairs)  85 us
    ppermute x14, waiting for transfers between devices, gather(): moving = lax.ppermute(moving, ring_axes, self.left)  60 us
    ppermute x14, waiting for transfers between devices, gather(): moving = lax.ppermute(moving, ring_axes, self.right)  52.5 us
    dot_general x41, matrix products, dot(): lax.dot_general(left, right, (dims, ((), ())), preferred_element_type=f32)  40.8 us
    ppermute x28, starting transfers between devices, run(): leg[3] = lax.ppermute(piece.astype(bf16), ring_axes, pairs)  29.6 us
    unnamed x230, local copies, waits for them, and re-layouts  28.8 us
    ppermute x14, starting transfers between devices, gather(): moving = lax.ppermute(moving, ring_axes, self.right)  25.5 us
    pallas_call x4, Pallas kernels, chunk_sum(): pl.pallas_call(kernel, out_shape=tuple((jax.ShapeDtypeStruct((r, columns)...  23.3 us
  transfers between devices with their start and end apart: 83, of which 27 were waited for; matrix products, arithmetic and copies ran while one was open for 15% of the time, Pallas kernels for 14%

profile of v5, /device:TPU:0, one launch (start us, length us, event | category | flops | bytes accessed | tf_op | source)
XLA Modules:
  0.0 500.9 jit_solution(12974422109863310447)
XLA Ops:
  20.5 10.4 %collective-permute-done.4.refs_7_ = bf16[256,768]{1,0:T(8,128)(2,1)S(1)} collective-permute-done((bf16[256,768]{1,0:T(8,128)(2,1)S(1)}, bf16[256,768]{1,0:T(8,128)(2,1)S(1)}, u32[]{:S(2)}, u32[]{:S(2)}) %collective-permute-start.4) | collective-permute-done | bytes 393248 | tf_op jit(solution)/shard_map/ppermute | solution.py:70
  35.4 5.2 %collective-permute-done.5.refs_6_ = bf16[256,768]{1,0:T(8,128)(2,1)S(1)} collective-permute-done((bf16[256,768]{1,0:T(8,128)(2,1)S(1)}, bf16[256,768]{1,0:T(8,128)(2,1)S(1)}, u32[]{:S(2)}, u32[]{:S(2)}) %collective-permute-start.5) | collective-permute-done | bytes 393248 | tf_op jit(solution)/shard_map/ppermute | solution.py:70
  64.7 4.4 collective-permute-start.8
  73.9 9.7 %collective-permute-start.21 = (bf16[256,2048]{1,0:T(8,128)(2,1)}, bf16[256,2048]{1,0:T(8,128)(2,1)}, u32[]{:S(2)}, u32[]{:S(2)}) collective-permute-start(bf16[256,2048]{1,0:T(8,128)(2,1)} %refs_1_.9), channel_id=1, source_target_pairs={{0,4},{4,8},{8,12},{12,28},{28,24},{24,20},{20,16},{16,0},{1,5},{5... | collective-permute-start | bytes 3145736 | tf_op jit(solution)/shard_map/ppermute | solution.py:66
  84.0 9.4 %shard_map.326 = (bf16[512,512]{1,0:T(8,128)(2,1)S(1)}, f32[8,512]{1,0:T(8,128)S(1)}) custom-call(bf16[512,768]{1,0:T(8,128)(2,1)S(1)} %shard_map.325.q_ref, bf16[512,256]{1,0:T(8,128)(2,1)S(1)} %slice.486.refs_0_, bf16[512,256]{1,0:T(8,128)(2,1)S(1)} %collective-permute-done.7.refs_1_, bf16[512,256]{1,0:T(8,128)(2,1)S(1)} %collective-permute-done.8.refs_2_, ...), custom_call_target="tpu_custom_call" | custom-call | flops 2147483648 | bytes 1048576 | tf_op jit(solution)/shard_map/pallas_call | solution.py:398
  93.5 4.4 shard_map.327
  112.1 6.4 %collective-permute-start.31 = (bf16[2048,256]{1,0:T(8,128)(2,1)S(1)}, bf16[2048,256]{1,0:T(8,128)(2,1)S(1)}, u32[]{:S(2)}, u32[]{:S(2)}) collective-permute-start(bf16[2048,256]{1,0:T(8,128)(2,1)S(1)} %copy-done.40), channel_id=1, source_target_pairs={{4,0},{8,4},{12,8},{28,12},{24,28},{20,24},{16,20},{0,16},{5,1},{9... | collective-permute-start | bytes 3145736 | tf_op jit(solution)/shard_map/ppermute | solution.py:70
  124.4 20.3 %collective-permute-done.22.refs_3_ = bf16[256,2048]{1,0:T(8,128)(2,1)S(1)} collective-permute-done((bf16[256,2048]{1,0:T(8,128)(2,1)}, bf16[256,2048]{1,0:T(8,128)(2,1)S(1)}, u32[]{:S(2)}, u32[]{:S(2)}) %collective-permute-start.22) | collective-permute-done | bytes 1048608 | tf_op jit(solution)/shard_map/ppermute | solution.py:66
  152.1 15.1 %collective-permute-done.28.refs_2_ = bf16[2048,256]{1,0:T(8,128)(2,1)S(1)} collective-permute-done((bf16[2048,256]{1,0:T(8,128)(2,1)S(1)}, bf16[2048,256]{1,0:T(8,128)(2,1)S(1)}, u32[]{:S(2)}, u32[]{:S(2)}) %collective-permute-start.28) | collective-permute-done | bytes 1048608 | tf_op jit(solution)/shard_map/ppermute | solution.py:66
  167.1 19.8 %collective-permute-done.32.refs_7_ = bf16[2048,256]{1,0:T(8,128)(2,1)S(1)} collective-permute-done((bf16[2048,256]{1,0:T(8,128)(2,1)S(1)}, bf16[2048,256]{1,0:T(8,128)(2,1)S(1)}, u32[]{:S(2)}, u32[]{:S(2)}) %collective-permute-start.32) | collective-permute-done | bytes 1048608 | tf_op jit(solution)/shard_map/ppermute | solution.py:70
  194.9 17.1 %collective-permute-done.29.refs_3_ = bf16[2048,256]{1,0:T(8,128)(2,1)S(1)} collective-permute-done((bf16[2048,256]{1,0:T(8,128)(2,1)S(1)}, bf16[2048,256]{1,0:T(8,128)(2,1)S(1)}, u32[]{:S(2)}, u32[]{:S(2)}) %collective-permute-start.29) | collective-permute-done | bytes 1048608 | tf_op jit(solution)/shard_map/ppermute | solution.py:66
  215.2 20.1 %collective-permute-done.27.refs_6_ = bf16[256,2048]{1,0:T(8,128)(2,1)S(1)} collective-permute-done((bf16[256,2048]{1,0:T(8,128)(2,1)S(1)}, bf16[256,2048]{1,0:T(8,128)(2,1)S(1)}, u32[]{:S(2)}, u32[]{:S(2)}) %collective-permute-start.27) | collective-permute-done | bytes 1048608 | tf_op jit(solution)/shard_map/ppermute | solution.py:70
  242.3 9.8 %shard_map.328 = (bf16[512,2048]{1,0:T(8,128)(2,1)S(1)}, f32[512,2048]{1,0:T(8,128)}) custom-call(bf16[512,2048]{1,0:T(8,128)(2,1)S(1)} %pad_maximum_fusion.refs_0_, bf16[256,2048]{1,0:T(8,128)(2,1)} %refs_1_.9, bf16[256,2048]{1,0:T(8,128)(2,1)} %collective-permute-done.21.refs_2_, bf16[256,2048]{1,0:T(8,128)(2,1)S(1)} %copy-done.55, ...), custom_call_target="tpu_custom_call" | custom-call | flops 4294967296 | bytes 18874368 | tf_op jit(solution)/shard_map/pallas_call | solution.py:297
  258.0 7.1 %shard_map.330 = (bf16[512,2048]{1,0:T(8,128)(2,1)S(1)}, f32[1,2048]{1,0:T(1,128)S(1)}) custom-call(bf16[512,2048]{1,0:T(8,128)(2,1)S(1)} %shard_map.329.refs_0_, bf16[2048,256]{1,0:T(8,128)(2,1)S(1)} %copy-done.40, bf16[2048,256]{1,0:T(8,128)(2,1)S(1)} %collective-permute-done.28.refs_2_, bf16[2048,256]{1,0:T(8,128)(2,1)S(1)} %copy-done.49, ...), custom_call_target="tpu_custom_call" | custom-call | flops 4294967296 | bytes 18874368 | tf_op jit(solution)/shard_map/pallas_call | solution.py:297
  268.8 7.3 %shard_map.331 = (bf16[256,2048]{1,0:T(8,128)(2,1)S(1)}, bf16[256,2048]{1,0:T(8,128)(2,1)S(1)}) custom-call(bf16[512,2048]{1,0:T(8,128)(2,1)S(1)} %get-tuple-element.59.refs_0_, bf16[256,2048]{1,0:T(8,128)(2,1)} %refs_1_.9, bf16[256,2048]{1,0:T(8,128)(2,1)} %collective-permute-done.21.refs_2_, bf16[256,2048]{1,0:T(8,128)(2,1)S(1)} %copy-done.56, ...), custom_call_target="tpu_custom_call" | custom-call | flops 4294967296 | bytes 12582912 | tf_op jit(solution)/shard_map/pallas_call | solution.py:338
  288.2 14.9 %collective-permute-done.72 = bf16[256,2048]{1,0:T(8,128)(2,1)S(1)} collective-permute-done((bf16[256,2048]{1,0:T(8,128)(2,1)S(1)}, bf16[256,2048]{1,0:T(8,128)(2,1)S(1)}, u32[]{:S(2)}, u32[]{:S(2)}) %collective-permute-start.72) | collective-permute-done | bytes 1048608 | tf_op jit(solution)/shard_map/ppermute | solution.py:92
  310.7 17.8 %collective-permute-done.77 = bf16[2048,256]{1,0:T(8,128)(2,1)S(1)} collective-permute-done((bf16[2048,256]{1,0:T(8,128)(2,1)S(1)}, bf16[2048,256]{1,0:T(8,128)(2,1)S(1)}, u32[]{:S(2)}, u32[]{:S(2)}) %collective-permute-start.77) | collective-permute-done | bytes 1048608 | tf_op jit(solution)/shard_map/ppermute | solution.py:92
  331.2 16.7 %collective-permute-done.73 = bf16[256,2048]{1,0:T(8,128)(2,1)S(1)} collective-permute-done((bf16[256,2048]{1,0:T(8,128)(2,1)S(1)}, bf16[256,2048]{1,0:T(8,128)(2,1)S(1)}, u32[]{:S(2)}, u32[]{:S(2)}) %collective-permute-start.73) | collective-permute-done | bytes 1048608 | tf_op jit(solution)/shard_map/ppermute | solution.py:92
  354.6 18.9 %collective-permute-done.78 = bf16[2048,256]{1,0:T(8,128)(2,1)S(1)} collective-permute-done((bf16[2048,256]{1,0:T(8,128)(2,1)S(1)}, bf16[2048,256]{1,0:T(8,128)(2,1)S(1)}, u32[]{:S(2)}, u32[]{:S(2)}) %collective-permute-start.78) | collective-permute-done | bytes 1048608 | tf_op jit(solution)/shard_map/ppermute | solution.py:92
  382.3 11.5 %shard_map.334 = (bf16[512,512]{1,0:T(8,128)(2,1)S(1)}, f32[2048,256]{1,0:T(8,128)S(1)}) custom-call(bf16[512,768]{1,0:T(8,128)(2,1)S(1)} %shard_map.325.q_ref, bf16[512,256]{1,0:T(8,128)(2,1)S(1)} %copy-done.39, bf16[512,256]{1,0:T(8,128)(2,1)S(1)} %copy-done.70, bf16[512,256]{1,0:T(8,128)(2,1)S(1)} %copy-done.72, bf16[512,256]{1,0:T(8,128)(2,1)S(1)} %copy-done.74, ...), custom_call_target="tpu_custom_call" | custom-call | flops 5368709120 | bytes 3670016 | tf_op jit(solution)/shard_map/pallas_call | solution.py:465
  404.1 6.7 %shard_map.333 = (bf16[256,2048]{1,0:T(8,128)(2,1)S(1)}, bf16[256,2048]{1,0:T(8,128)(2,1)S(1)}) custom-call(bf16[512,2048]{1,0:T(8,128)(2,1)S(1)} %get-tuple-element.62.refs_0_, bf16[2048,256]{1,0:T(8,128)(2,1)S(1)} %copy-done.41, bf16[2048,256]{1,0:T(8,128)(2,1)S(1)} %copy-done.45, bf16[2048,256]{1,0:T(8,128)(2,1)S(1)} %copy-done.50, ...), custom_call_target="tpu_custom_call" | custom-call | flops 4294967296 | bytes 12582912 | tf_op jit(solution)/shard_map/pallas_call | solution.py:338
  434.0 5.6 %collective-permute-done.62 = bf16[512,256]{1,0:T(8,128)(2,1)S(1)} collective-permute-done((bf16[512,256]{1,0:T(8,128)(2,1)S(1)}, bf16[512,256]{1,0:T(8,128)(2,1)S(1)}, u32[]{:S(2)}, u32[]{:S(2)}) %collective-permute-start.62) | collective-permute-done | bytes 262176 | tf_op jit(solution)/shard_map/ppermute | solution.py:92
  454.6 5.7 %collective-permute-done.58 = bf16[288,512]{1,0:T(8,128)(2,1)S(1)} collective-permute-done((bf16[288,512]{1,0:T(8,128)(2,1)S(1)}, bf16[288,512]{1,0:T(8,128)(2,1)S(1)}, u32[]{:S(2)}, u32[]{:S(2)}) %collective-permute-start.58) | collective-permute-done | bytes 294944 | tf_op jit(solution)/shard_map/ppermute | solution.py:92
  486.2 5.8 %collective-permute-done.51 = f32[14976]{0:T(1024)S(1)} collective-permute-done((f32[14976]{0:T(1024)S(1)}, f32[14976]{0:T(1024)S(1)}, u32[]{:S(2)}, u32[]{:S(2)}) %collective-permute-start.51) | collective-permute-done | bytes 59936 | tf_op jit(solution)/shard_map/ppermute | solution.py:135
  (562 shorter events, 217.4 us)
Async XLA Ops:
  6.3 34.9 %collective-permute-start.10 = (bf16[512,256]{1,0:T(8,128)(2,1)}, bf16[512,256]{1,0:T(8,128)(2,1)}, u32[]{:S(2)}, u32[]{:S(2)}) collective-permute-start(bf16[512,256]{1,0:T(8,128)(2,1)} %refs_1_.10), channel_id=1, source_target_pairs={{0,4},{4,8},{8,12},{12,28},{28,24},{24,20},{20,16},{16,0},{1,5},{5... | collective-permute-start | bytes 786440 | tf_op jit(solution)/shard_map/ppermute | solution.py:66
  8.3 45.1 %collective-permute-start.14 = (bf16[512,256]{1,0:T(8,128)(2,1)}, bf16[512,256]{1,0:T(8,128)(2,1)}, u32[]{:S(2)}, u32[]{:S(2)}) collective-permute-start(bf16[512,256]{1,0:T(8,128)(2,1)} %refs_1_.10), channel_id=1, source_target_pairs={{4,0},{8,4},{12,8},{28,12},{24,28},{20,24},{16,20},{0,16},{5,1},{9... | collective-permute-start | bytes 786440 | tf_op jit(solution)/shard_map/ppermute | solution.py:70
  73.9 44.5 %collective-permute-start.21 = (bf16[256,2048]{1,0:T(8,128)(2,1)}, bf16[256,2048]{1,0:T(8,128)(2,1)}, u32[]{:S(2)}, u32[]{:S(2)}) collective-permute-start(bf16[256,2048]{1,0:T(8,128)(2,1)} %refs_1_.9), channel_id=1, source_target_pairs={{0,4},{4,8},{8,12},{12,28},{28,24},{24,20},{20,16},{16,0},{1,5},{5... | collective-permute-start | bytes 3145736 | tf_op jit(solution)/shard_map/ppermute | solution.py:66
  121.7 45.4 %collective-permute-start.28 = (bf16[2048,256]{1,0:T(8,128)(2,1)S(1)}, bf16[2048,256]{1,0:T(8,128)(2,1)S(1)}, u32[]{:S(2)}, u32[]{:S(2)}) collective-permute-start(bf16[2048,256]{1,0:T(8,128)(2,1)S(1)} %copy-done.40), channel_id=1, source_target_pairs={{0,4},{4,8},{8,12},{12,28},{28,24},{24,20},{20,16},{16,0},{1,5},{5... | collective-permute-start | bytes 3145736 | tf_op jit(solution)/shard_map/ppermute | solution.py:66
  123.5 66.6 %collective-permute-start.26 = (bf16[256,2048]{1,0:T(8,128)(2,1)}, bf16[256,2048]{1,0:T(8,128)(2,1)S(1)}, u32[]{:S(2)}, u32[]{:S(2)}) collective-permute-start(bf16[256,2048]{1,0:T(8,128)(2,1)} %collective-permute-done.25.refs_8_), channel_id=1, source_target_pairs={{4,0},{8,4},{12,8},{28,12},{24,28},{20,24},{16,20},{0,16},{5,1},{9... | collective-permute-start | bytes 3145736 | tf_op jit(solution)/shard_map/ppermute | solution.py:70
  144.7 46.9 %collective-permute-start.23 = (bf16[256,2048]{1,0:T(8,128)(2,1)S(1)}, bf16[256,2048]{1,0:T(8,128)(2,1)S(1)}, u32[]{:S(2)}, u32[]{:S(2)}) collective-permute-start(bf16[256,2048]{1,0:T(8,128)(2,1)S(1)} %collective-permute-done.22.refs_3_), channel_id=1, source_target_pairs={{0,4},{4,8},{8,12},{12,28},{28,24},{24,20},{20,16},{16,0},{1,5},{5... | collective-permute-start | bytes 3145736 | tf_op jit(solution)/shard_map/ppermute | solution.py:66
  144.7 42.2 %collective-permute-start.32 = (bf16[2048,256]{1,0:T(8,128)(2,1)S(1)}, bf16[2048,256]{1,0:T(8,128)(2,1)S(1)}, u32[]{:S(2)}, u32[]{:S(2)}) collective-permute-start(bf16[2048,256]{1,0:T(8,128)(2,1)S(1)} %collective-permute-done.31.refs_8_), channel_id=1, source_target_pairs={{4,0},{8,4},{12,8},{28,12},{24,28},{20,24},{16,20},{0,16},{5,1},{9... | collective-permute-start | bytes 3145736 | tf_op jit(solution)/shard_map/ppermute | solution.py:70
  147.7 41.2 %collective-permute-start.19 = (bf16[128,2048]{1,0:T(8,128)(2,1)S(1)}, bf16[128,2048]{1,0:T(8,128)(2,1)S(1)}, u32[]{:S(2)}, u32[]{:S(2)}) collective-permute-start(bf16[128,2048]{1,0:T(8,128)(2,1)S(1)} %add_convert_fusion), channel_id=1, source_target_pairs={{0,2},{1,3},{2,0},{3,1},{4,6},{5,7},{6,4},{7,5},{8,10},{9,11},{10,... | collective-permute-start | bytes 1572872 | tf_op jit(solution)/shard_map/ppermute | solution.py:135
  167.1 44.9 %collective-permute-start.29 = (bf16[2048,256]{1,0:T(8,128)(2,1)S(1)}, bf16[2048,256]{1,0:T(8,128)(2,1)S(1)}, u32[]{:S(2)}, u32[]{:S(2)}) collective-permute-start(bf16[2048,256]{1,0:T(8,128)(2,1)S(1)} %collective-permute-done.28.refs_2_), channel_id=1, source_target_pairs={{0,4},{4,8},{8,12},{12,28},{28,24},{24,20},{20,16},{16,0},{1,5},{5... | collective-permute-start | bytes 3145736 | tf_op jit(solution)/shard_map/ppermute | solution.py:66
  190.1 45.3 %collective-permute-start.27 = (bf16[256,2048]{1,0:T(8,128)(2,1)S(1)}, bf16[256,2048]{1,0:T(8,128)(2,1)S(1)}, u32[]{:S(2)}, u32[]{:S(2)}) collective-permute-start(bf16[256,2048]{1,0:T(8,128)(2,1)S(1)} %collective-permute-done.26.refs_7_), channel_id=1, source_target_pairs={{4,0},{8,4},{12,8},{28,12},{24,28},{20,24},{16,20},{0,16},{5,1},{9... | collective-permute-start | bytes 3145736 | tf_op jit(solution)/shard_map/ppermute | solution.py:70
  191.6 44.8 %collective-permute-start.24 = (bf16[256,2048]{1,0:T(8,128)(2,1)S(1)}, bf16[256,2048]{1,0:T(8,128)(2,1)S(1)}, u32[]{:S(2)}, u32[]{:S(2)}) collective-permute-start(bf16[256,2048]{1,0:T(8,128)(2,1)S(1)} %collective-permute-done.23.refs_4_), channel_id=1, source_target_pairs={{0,4},{4,8},{8,12},{12,28},{28,24},{24,20},{20,16},{16,0},{1,5},{5... | collective-permute-start | bytes 3145736 | tf_op jit(solution)/shard_map/ppermute | solution.py:66
  212.1 45.7 %collective-permute-start.30 = (bf16[2048,256]{1,0:T(8,128)(2,1)S(1)}, bf16[2048,256]{1,0:T(8,128)(2,1)}, u32[]{:S(2)}, u32[]{:S(2)}) collective-permute-start(bf16[2048,256]{1,0:T(8,128)(2,1)S(1)} %collective-permute-done.29.refs_3_), channel_id=1, source_target_pairs={{0,4},{4,8},{8,12},{12,28},{28,24},{24,20},{20,16},{16,0},{1,5},{5... | collective-permute-start | bytes 3145736 | tf_op jit(solution)/shard_map/ppermute | solution.py:66
  212.9 45.0 %collective-permute-start.34 = (bf16[2048,256]{1,0:T(8,128)(2,1)S(1)}, bf16[2048,256]{1,0:T(8,128)(2,1)}, u32[]{:S(2)}, u32[]{:S(2)}) collective-permute-start(bf16[2048,256]{1,0:T(8,128)(2,1)S(1)} %collective-permute-done.33.refs_6_), channel_id=1, source_target_pairs={{4,0},{8,4},{12,8},{28,12},{24,28},{20,24},{16,20},{0,16},{5,1},{9... | collective-permute-start | bytes 3145736 | tf_op jit(solution)/shard_map/ppermute | solution.py:70
  282.1 47.4 %collective-permute-start.81 = (bf16[2048,256]{1,0:T(8,128)(2,1)S(1)}, bf16[2048,256]{1,0:T(8,128)(2,1)S(1)}, u32[]{:S(2)}, u32[]{:S(2)}) collective-permute-start(bf16[2048,256]{1,0:T(8,128)(2,1)S(1)} %fusion.11), channel_id=1, source_target_pairs={{4,0},{8,4},{12,8},{28,12},{24,28},{20,24},{16,20},{0,16},{5,1},{9... | collective-permute-start | bytes 3145736 | tf_op jit(solution)/shard_map/ppermute | solution.py:92
  286.1 42.4 %collective-permute-start.77 = (bf16[2048,256]{1,0:T(8,128)(2,1)S(1)}, bf16[2048,256]{1,0:T(8,128)(2,1)S(1)}, u32[]{:S(2)}, u32[]{:S(2)}) collective-permute-start(bf16[2048,256]{1,0:T(8,128)(2,1)S(1)} %fusion.9), channel_id=1, source_target_pairs={{0,4},{4,8},{8,12},{12,28},{28,24},{24,20},{20,16},{16,0},{1,5},{5... | collective-permute-start | bytes 3145736 | tf_op jit(solution)/shard_map/ppermute | solution.py:92
  303.9 44.0 %collective-permute-start.73 = (bf16[256,2048]{1,0:T(8,128)(2,1)S(1)}, bf16[256,2048]{1,0:T(8,128)(2,1)S(1)}, u32[]{:S(2)}, u32[]{:S(2)}) collective-permute-start(bf16[256,2048]{1,0:T(8,128)(2,1)S(1)} %fusion.6), channel_id=1, source_target_pairs={{4,0},{8,4},{12,8},{28,12},{24,28},{20,24},{16,20},{0,16},{5,1},{9... | collective-permute-start | bytes 3145736 | tf_op jit(solution)/shard_map/ppermute | solution.py:92
  306.8 45.9 %collective-permute-start.70 = (bf16[256,2048]{1,0:T(8,128)(2,1)S(1)}, bf16[256,2048]{1,0:T(8,128)(2,1)S(1)}, u32[]{:S(2)}, u32[]{:S(2)}) collective-permute-start(bf16[256,2048]{1,0:T(8,128)(2,1)S(1)} %fusion.3), channel_id=1, source_target_pairs={{0,4},{4,8},{8,12},{12,28},{28,24},{24,20},{20,16},{16,0},{1,5},{5... | collective-permute-start | bytes 3145736 | tf_op jit(solution)/shard_map/ppermute | solution.py:92
  309.1 41.4 %collective-permute-start.37 = (bf16[128,2048]{1,0:T(8,128)(2,1)S(1)}, bf16[128,2048]{1,0:T(8,128)(2,1)S(1)}, u32[]{:S(2)}, u32[]{:S(2)}) collective-permute-start(bf16[128,2048]{1,0:T(8,128)(2,1)S(1)} %get-tuple-element.89), channel_id=1, source_target_pairs={{0,2},{1,3},{2,0},{3,1},{4,6},{5,7},{6,4},{7,5},{8,10},{9,11},{10,... | collective-permute-start | bytes 1572872 | tf_op jit(solution)/shard_map/ppermute | solution.py:135
  329.3 44.2 %collective-permute-start.78 = (bf16[2048,256]{1,0:T(8,128)(2,1)S(1)}, bf16[2048,256]{1,0:T(8,128)(2,1)S(1)}, u32[]{:S(2)}, u32[]{:S(2)}) collective-permute-start(bf16[2048,256]{1,0:T(8,128)(2,1)S(1)} %fusion.8), channel_id=1, source_target_pairs={{0,4},{4,8},{8,12},{12,28},{28,24},{24,20},{20,16},{16,0},{1,5},{5... | collective-permute-start | bytes 3145736 | tf_op jit(solution)/shard_map/ppermute | solution.py:92
  350.8 66.8 %collective-permute-start.82 = (bf16[2048,256]{1,0:T(8,128)(2,1)}, bf16[2048,256]{1,0:T(8,128)(2,1)}, u32[]{:S(2)}, u32[]{:S(2)}) collective-permute-start(bf16[2048,256]{1,0:T(8,128)(2,1)} %fusion.10), channel_id=1, source_target_pairs={{4,0},{8,4},{12,8},{28,12},{24,28},{20,24},{16,20},{0,16},{5,1},{9... | collective-permute-start | bytes 3145736 | tf_op jit(solution)/shard_map/ppermute | solution.py:92
  354.3 61.2 %collective-permute-start.71 = (bf16[256,2048]{1,0:T(8,128)(2,1)}, bf16[256,2048]{1,0:T(8,128)(2,1)}, u32[]{:S(2)}, u32[]{:S(2)}) collective-permute-start(bf16[256,2048]{1,0:T(8,128)(2,1)} %fusion.2), channel_id=1, source_target_pairs={{0,4},{4,8},{8,12},{12,28},{28,24},{24,20},{20,16},{16,0},{1,5},{5... | collective-permute-start | bytes 3145736 | tf_op jit(solution)/shard_map/ppermute | solution.py:92
  375.2 42.7 %collective-permute-start.79 = (bf16[2048,256]{1,0:T(8,128)(2,1)}, bf16[2048,256]{1,0:T(8,128)(2,1)}, u32[]{:S(2)}, u32[]{:S(2)}) collective-permute-start(bf16[2048,256]{1,0:T(8,128)(2,1)} %fusion.7), channel_id=1, source_target_pairs={{0,4},{4,8},{8,12},{12,28},{28,24},{24,20},{20,16},{16,0},{1,5},{5... | collective-permute-start | bytes 3145736 | tf_op jit(solution)/shard_map/ppermute | solution.py:92
  377.0 65.1 %collective-permute-start.75 = (bf16[256,2048]{1,0:T(8,128)(2,1)}, bf16[256,2048]{1,0:T(8,128)(2,1)}, u32[]{:S(2)}, u32[]{:S(2)}) collective-permute-start(bf16[256,2048]{1,0:T(8,128)(2,1)} %fusion.4), channel_id=1, source_target_pairs={{4,0},{8,4},{12,8},{28,12},{24,28},{20,24},{16,20},{0,16},{5,1},{9... | collective-permute-start | bytes 3145736 | tf_op jit(solution)/shard_map/ppermute | solution.py:92
  453.9 40.5 %collective-permute-start.68 = (bf16[512,256]{1,0:T(8,128)(2,1)S(1)}, bf16[512,256]{1,0:T(8,128)(2,1)S(1)}, u32[]{:S(2)}, u32[]{:S(2)}) collective-permute-start(bf16[512,256]{1,0:T(8,128)(2,1)S(1)} %fusion.21), channel_id=1, source_target_pairs={{4,0},{8,4},{12,8},{28,12},{24,28},{20,24},{16,20},{0,16},{5,1},{9... | collective-permute-start | bytes 786440 | tf_op jit(solution)/shard_map/ppermute | solution.py:92
  (155 other events, 2277.9 us)
